TPU v7x, 32 devices: a whole 2x2x4 slice. The times are simulated.
32 devices in a mesh: groups: 2 (over y), seq: 4 (over z), head: 2 (over x), rep: 2 (over core).
Axes of the slice: x: 2, y: 2, z: 4, core: 2. Of those that a mesh axis runs over, the one named last changes fastest.
Arguments:
- queries: bfloat16 [8192, 5120], P(('groups', 'seq'), ('head', 'rep')), parts along dimension 0, may hold values from -4.5 to 4.5
- keys: bfloat16 [8192, 5120], P(('groups', 'seq'), ('head', 'rep')), parts along dimension 0, may hold values from -4.5 to 4.5
- values: bfloat16 [8192, 5120], P(('groups', 'seq'), ('head', 'rep')), parts along dimension 0, may hold values from -5 to 5
- rates: float32 [40, 8192], P(('head', 'rep'), ('groups', 'seq')), parts along dimension 1, may hold values from 0.0005 to 0.005
- fast_weights: bfloat16 [128, 40, 3, 128], P(None, ('head', 'rep')), may hold values from -0.5 to 0.5
- momentum: float32 [128, 40, 3, 128], P('seq', ('head', 'rep')), may hold values from -0.3 to 0.3
Outputs:
- mixed: bfloat16 [8192, 5120], P(('groups', 'seq'), ('head', 'rep')), parts along dimension 0
- new_weights: bfloat16 [256, 40, 3, 128], P(('groups', 'seq'), ('head', 'rep')), parts along dimension 0
- new_momentum: float32 [256, 40, 3, 128], P(('groups', 'seq'), ('head', 'rep')), parts along dimension 0
There are 2 independent parts, one for each index of `groups`. A program takes and returns all parts, laid end to end along the dimension named above; an argument that names none is the same for every part. Nothing has to cross between parts.
All inputs are finite; a program needn't handle non-finite values.
Results may differ from a plain program's by a relative error of at most 0.013.
Values may be sent and summed in bfloat16 or wider, within the bound.
No kernel may reach another device: no remote copies, remote signals or barrier semaphores. Data moves between devices by JAX's collectives and lax.ppermute only.
A program may use at most 128 MiB of HBM per device.

v0:
```python
import jax
import jax.numpy as jnp
from jax import lax
from jax.sharding import PartitionSpec as P

WIN = 512


momentum_keep = 0.9
epsilon = 1e-06


def passed_along(value, axis, by):
    peers = lax.axis_size(axis)
    pairs = [(i, i + by) for i in range(peers) if 0 <= i + by < peers]
    return lax.ppermute(value, axis, pairs)


def window_block(query_block, key_block, value_block, first):
    width = query_block.shape[0]
    head_size = query_block.shape[2]
    scores = jnp.einsum(
        "qhd,khd->hqk", query_block, key_block, preferred_element_type=jnp.float32
    ) * head_size ** (-0.5)
    query_index = jnp.arange(width, dtype=jnp.int32)[:, None]
    key_index = jnp.arange(2 * width, dtype=jnp.int32)[None, :]
    allowed = (
        (key_index > query_index) & (key_index <= query_index + width) & (key_index + first >= 0)
    )
    scores = jnp.where(allowed[None], scores, -1e30)
    row_max = jnp.max(scores, axis=-1, keepdims=True)
    weights = jnp.exp(scores - row_max)
    total = jnp.sum(weights, axis=-1, keepdims=True)
    probabilities = (weights / total).astype(jnp.bfloat16)
    return jnp.einsum(
        "hqk,khd->qhd", probabilities, value_block, preferred_element_type=jnp.float32
    )


def swiglu_parts(inputs, weights):
    inner = jnp.einsum(
        "thr,rhcf->thcf", inputs, weights[:, :, 0:2], preferred_element_type=jnp.float32
    )
    return (inner[:, :, 0], inner[:, :, 1])


def refresh(old_weights, old_momentum, grads):
    new_momentum = momentum_keep * old_momentum + grads
    before = old_weights.astype(jnp.float32)
    moved = before + new_momentum
    ratio = jnp.sqrt(
        (jnp.mean(before * before, axis=-1, keepdims=True) + epsilon)
        / (jnp.mean(moved * moved, axis=-1, keepdims=True) + epsilon)
    )
    return ((moved * ratio).astype(jnp.bfloat16), new_momentum)


def shards(queries, keys, values, rates, fast_weights, momentum):
    tok_rows = queries.shape[0]
    heads_here = rates.shape[0]
    head_size = fast_weights.shape[0]
    own_rows = momentum.shape[0]
    query_heads = queries.reshape(tok_rows, heads_here, head_size)
    key_heads = keys.reshape(tok_rows, heads_here, head_size)
    value_heads = values.reshape(tok_rows, heads_here, head_size)
    tail = jnp.stack([keys[tok_rows - WIN :], values[tok_rows - WIN :]])
    previous = passed_along(tail, "seq", 1)
    gating, upward = swiglu_parts(key_heads, fast_weights)
    sigmoid_gate = jax.nn.sigmoid(gating)
    hidden = (gating * sigmoid_gate * upward).astype(jnp.bfloat16)
    scaled_values = (value_heads.astype(jnp.float32) * jnp.transpose(rates)[:, :, None]).astype(
        jnp.bfloat16
    )
    hidden_grad = jnp.einsum(
        "thr,rhf->thf", scaled_values, fast_weights[:, :, 2], preferred_element_type=jnp.float32
    )
    gate_grad = (
        hidden_grad * upward * sigmoid_gate * (1.0 + gating * (1.0 - sigmoid_gate))
    ).astype(jnp.bfloat16)
    upward_grad = (hidden_grad * gating * sigmoid_gate).astype(jnp.bfloat16)
    paired = jnp.stack([gate_grad, upward_grad], axis=2)
    row_offset = lax.axis_index("seq") * own_rows
    first_grads = jnp.einsum(
        "thr,thcf->rhcf", key_heads, paired, preferred_element_type=jnp.float32
    )
    second_grads = jnp.einsum(
        "thr,thf->rhf", scaled_values, hidden, preferred_element_type=jnp.float32
    )[:, :, None]
    grads = lax.psum(jnp.concatenate([first_grads, second_grads], axis=2), "seq")
    whole_momentum = lax.all_gather(
        momentum.astype(jnp.bfloat16), "seq", axis=0, tiled=True
    ).astype(momentum.dtype)
    new_weights, full_momentum = refresh(fast_weights, whole_momentum, grads)
    new_rows = lax.dynamic_slice_in_dim(new_weights, row_offset, own_rows, 0)
    new_momentum = lax.dynamic_slice_in_dim(full_momentum, row_offset, own_rows, 0)
    query_gating, query_upward = swiglu_parts(query_heads, new_weights)
    query_hidden = (jax.nn.silu(query_gating) * query_upward).astype(jnp.bfloat16)
    fast_out = jnp.einsum(
        "thf,rhf->thr", query_hidden, new_weights[:, :, 2], preferred_element_type=jnp.float32
    )
    extended_keys = jnp.concatenate([previous[0], keys], axis=0).reshape(
        WIN + tok_rows, heads_here, head_size
    )
    extended_values = jnp.concatenate([previous[1], values], axis=0).reshape(
        WIN + tok_rows, heads_here, head_size
    )
    first_key = lax.axis_index("seq") * tok_rows - WIN

    def one_block(block):
        query_block = lax.dynamic_slice_in_dim(query_heads, block * WIN, WIN, 0)
        key_block = lax.dynamic_slice_in_dim(extended_keys, block * WIN, 2 * WIN, 0)
        value_block = lax.dynamic_slice_in_dim(extended_values, block * WIN, 2 * WIN, 0)
        return window_block(query_block, key_block, value_block, first_key + block * WIN)

    attended = lax.map(one_block, jnp.arange(tok_rows // WIN, dtype=jnp.int32)).reshape(
        tok_rows, heads_here, head_size
    )
    mixed = (fast_out + attended).reshape(tok_rows, heads_here * head_size).astype(jnp.bfloat16)
    return (mixed, new_rows, new_momentum)


def solution(mesh):
    return jax.shard_map(
        shards,
        mesh=mesh,
        in_specs=(
            P(("groups", "seq"), ("head", "rep")),
            P(("groups", "seq"), ("head", "rep")),
            P(("groups", "seq"), ("head", "rep")),
            P(("head", "rep"), ("groups", "seq")),
            P(None, ("head", "rep"), None, None),
            P("seq", ("head", "rep"), None, None),
        ),
        out_specs=(
            P(("groups", "seq"), ("head", "rep")),
            P(("groups", "seq"), ("head", "rep"), None, None),
            P(("groups", "seq"), ("head", "rep"), None, None),
        ),
        check_vma=False,
    )
```

profile of v0, /device:TPU:0, one launch (start us, length us, event | category | flops | bytes accessed | tf_op | source)
XLA Modules:
  0.0 385.5 jit_solution(15369249530486513735)
XLA Ops:
  7.2 4.4 %copy.53 = bf16[1024,1280]{0,1:T(8,128)(2,1)} copy(bf16[1024,1280]{1,0:T(8,128)(2,1)} %param.10) | data formatting | bytes 5242880 | tf_op args[2]
  11.6 3.0 copy.57
  14.6 2.2 copy.51
  16.8 2.8 convolution_bitcast_fusion.1
  19.7 2.3 fusion.54
  22.0 4.3 %fusion.46 = (bf16[1024,10,1,128]{3,0,1,2:T(8,128)(2,1)S(1)}, bf16[1024,10,1,128]{3,0,1,2:T(8,128)(2,1)S(1)}) fusion(f32[1024,10,2,128]{3,0,1,2:T(8,128)S(1)} %convolution_bitcast_fusion.1, bf16[128,10,3,128]{3,0,2,1:T(8,128)(2,1)} %param.12, bf16[1024,10,128]{0,2,1:T(8,128)(2,1)S(1)} %bitcast.123, f32[1024,10]{0,1:T(8,128)S(1)} %bitcast.131), kind=kOutput, calls=%fused_computation.57 | convolution fusion | flops 356515840 | bytes 18718720 | tf_op jit(solution)/shard_map/thr,rhf->thf/dot_general | solution.py:74
  26.3 2.1 fusion.51
  31.5 1.7 pad_maximum_fusion.3
  33.2 6.4 %collective-permute-start = (bf16[2,512,1280]{1,2,0:T(8,128)(2,1)}, bf16[2,512,1280]{1,2,0:T(8,128)(2,1)}, u32[]{:S(2)}, u32[]{:S(2)}) collective-permute-start(bf16[2,512,1280]{1,2,0:T(8,128)(2,1)} %pad_maximum_fusion.3), channel_id=1, source_target_pairs={{0,4},{4,8},{8,12},{1,5},{5,9},{9,13},{2,6},{6,10},{10,14},{3,7},{... | collective-permute-start | bytes 7864328 | tf_op jit(solution)/shard_map/ppermute | solution.py:16
  39.7 4.5 %copy.64 = bf16[1024,1280]{0,1:T(8,128)(2,1)} copy(bf16[1024,1280]{1,0:T(8,128)(2,1)} %param.8) | data formatting | bytes 5242880 | tf_op args[0]
  44.2 134.8 %all_gather.3 = bf16[128,10,3,128]{3,0,2,1:T(8,128)(2,1)} all-gather(bf16[32,10,3,128]{3,0,2,1:T(8,128)(2,1)S(1)} %convert_element_type.40), channel_id=1, replica_groups=mesh['groups'=2,'seq'=4,'head'=2,'rep'=2] {'seq'}, dimensions={0}, use_global_device_ids=true | all-gather | bytes 1228800 | tf_op jit(solution)/shard_map/all_gather | solution.py:90
  179.1 2.2 copy.52
  181.3 2.9 fusion.48
  188.2 2.2 copy.74
  190.4 3.4 constant_dynamic-slice_fusion
  193.8 2.9 copy.75
  196.7 7.5 %convolution_bitcast_fusion = f32[1024,10,2,128]{3,0,1,2:T(8,128)} fusion(bf16[1024,10,128,1]{0,2,1,3:T(8,128)(2,1)} %bitcast.125, bf16[128,10,3,128]{0,3,2,1:T(8,128)(2,1)} %copy-done.4), kind=kOutput, calls=%fused_computation.51 | convolution fusion | flops 671088640 | bytes 13762560 | tf_op jit(solution)/shard_map/thr,rhcf->thcf/dot_general | solution.py:41
  204.2 2.0 fusion.71
  206.7 2.2 pad_maximum_fusion.1
  208.9 2.2 pad_maximum_fusion.2
  211.2 149.1 %while.10 = (s32[]{:T(128)}, f32[2,512,10,128]{1,0,3,2:T(2,128)}, s32[2]{0:T(128)S(1)}, bf16[1536,10,128]{0,2,1:T(8,128)(2,1)}, s32[]{:T(128)}, /*index=5*/bf16[...) while((s32[]{:T(128)}, f32[2,512,10,128]{1,0,3,2:T(2,128)}, ...), condition=%wide.region_6.7_spmd, body=%wide.region_3.6_spmd.sunk | while | flops 2717912576 | bytes 62699760 | solution.py:115
  212.9 13.1 %fusion.89 = (f32[10,512]{1,0:T(8,128)S(1)}, f32[10,512,1024]{2,1,0:T(8,128)}) fusion(pred[512,1024]{1,0:T(8,128)(4,1)S(1)} %fusion.88, bf16[1536,10,128]{0,2,1:T(8,128)(2,1)} %get-tuple-element.166, s32[]{:T(128)S(6)} %select_n.30, bf16[1024,10,128]{0,2,1:T(8,128)(2,1)} %get-tuple-element.165, s32[]{:T(128)S(6)} %select_n.31), kind=kOutput, calls=%fused_computation.81.clone.1 | convolution fusion | flops 1363149824 | bytes 25448456 | tf_op jit(solution)/shard_map/while/body/eval_jaxpr/sub | solution.py:32
  226.0 9.7 %fusion.90 = f32[1,512,10,128]{1,3,2,0:T(8,128)S(1)} fusion(f32[10,512,1024]{2,1,0:T(8,128)} %get-tuple-element.134, f32[10,512]{1,0:T(8,128)S(1)} %get-tuple-element.135, bf16[1536,10,128]{0,2,1:T(8,128)(2,1)} %get-tuple-element.163, s32[]{:T(128)S(6)} %select_n.30), kind=kOutput, calls=%fused_computation.18.clone.1 | convolution fusion | flops 1352663040 | bytes 26234884 | tf_op jit(solution)/shard_map/while/body/eval_jaxpr/hqk,khd->qhd/dot_general | solution.py:35
  235.8 2.7 copy.109
  238.5 47.2 %dynamic_update_slice.5 = f32[2,512,10,128]{1,0,3,2:T(2,128)} dynamic-update-slice(f32[2,512,10,128]{1,0,3,2:T(2,128)} %get-tuple-element.149, f32[1,512,10,128]{1,0,3,2:T(1,128)S(1)} %copy.109, s32[]{:T(128)S(6)} %copy.113, s32[]{:T(128)} %constant.18.clone.1..sunk, s32[]{:T(128)} %constant.18.clone.1..sunk, s32[]{:T(128)} %constant.18.clone.1..sunk) | dynamic-update-slice | bytes 5242884 | tf_op jit(solution)/shard_map/while/body/jit(dynamic_update_index_in_dim)/dynamic_update_slice | solution.py:115
  287.4 13.1 %fusion.89 = (f32[10,512]{1,0:T(8,128)S(1)}, f32[10,512,1024]{2,1,0:T(8,128)}) fusion(pred[512,1024]{1,0:T(8,128)(4,1)S(1)} %fusion.88, bf16[1536,10,128]{0,2,1:T(8,128)(2,1)} %get-tuple-element.166, s32[]{:T(128)S(6)} %select_n.30, bf16[1024,10,128]{0,2,1:T(8,128)(2,1)} %get-tuple-element.165, s32[]{:T(128)S(6)} %select_n.31), kind=kOutput, calls=%fused_computation.81.clone.1 | convolution fusion | flops 1363149824 | bytes 25448456 | tf_op jit(solution)/shard_map/while/body/eval_jaxpr/sub | solution.py:32
  300.5 9.7 %fusion.90 = f32[1,512,10,128]{1,3,2,0:T(8,128)S(1)} fusion(f32[10,512,1024]{2,1,0:T(8,128)} %get-tuple-element.134, f32[10,512]{1,0:T(8,128)S(1)} %get-tuple-element.135, bf16[1536,10,128]{0,2,1:T(8,128)(2,1)} %get-tuple-element.163, s32[]{:T(128)S(6)} %select_n.30), kind=kOutput, calls=%fused_computation.18.clone.1 | convolution fusion | flops 1352663040 | bytes 26234884 | tf_op jit(solution)/shard_map/while/body/eval_jaxpr/hqk,khd->qhd/dot_general | solution.py:35
  310.3 2.7 copy.109
  313.0 47.2 %dynamic_update_slice.5 = f32[2,512,10,128]{1,0,3,2:T(2,128)} dynamic-update-slice(f32[2,512,10,128]{1,0,3,2:T(2,128)} %get-tuple-element.149, f32[1,512,10,128]{1,0,3,2:T(1,128)S(1)} %copy.109, s32[]{:T(128)S(6)} %copy.113, s32[]{:T(128)} %constant.18.clone.1..sunk, s32[]{:T(128)} %constant.18.clone.1..sunk, s32[]{:T(128)} %constant.18.clone.1..sunk) | dynamic-update-slice | bytes 5242884 | tf_op jit(solution)/shard_map/while/body/jit(dynamic_update_index_in_dim)/dynamic_update_slice | solution.py:115
  360.2 8.1 %reshape.111 = f32[1024,10,128]{0,2,1:T(8,128)} reshape(f32[2,512,10,128]{1,0,3,2:T(2,128)} %get-tuple-element.40) | data formatting | bytes 10485760 | tf_op jit(solution)/shard_map/reshape | solution.py:115
  368.4 7.6 %fusion.34 = bf16[1024,10,128]{0,2,1:T(8,128)(2,1)S(1)} fusion(f32[1024,10,128]{0,2,1:T(8,128)} %reshape.111, f32[1024,10,2,128]{3,0,1,2:T(8,128)} %convolution_bitcast_fusion, bf16[128,10,3,128]{0,3,2,1:T(8,128)(2,1)} %copy-done.4), kind=kOutput, calls=%fused_computation.36 | convolution fusion | flops 346030080 | bytes 18677760 | tf_op jit(solution)/shard_map/thf,rhf->thr/dot_general | solution.py:98
  376.0 2.7 copy.73
  (34 shorter events, 9.6 us)
Async XLA Ops:
  7.2 174.2 %all-reduce.2.cloned.1.call-start = ((), (), s32[]{:S(2)}) async-start(), calls=%async_computation | async-start | bytes 3932160 | tf_op jit(solution)/shard_map/psum | solution.py:89
  16.8 2.8 copy-start.1
  16.8 2.8 copy-start.6
  33.2 170.9 %collective-permute-start = (bf16[2,512,1280]{1,2,0:T(8,128)(2,1)}, bf16[2,512,1280]{1,2,0:T(8,128)(2,1)}, u32[]{:S(2)}, u32[]{:S(2)}) collective-permute-start(bf16[2,512,1280]{1,2,0:T(8,128)(2,1)} %pad_maximum_fusion.3), channel_id=1, source_target_pairs={{0,4},{4,8},{8,12},{1,5},{5,9},{9,13},{2,6},{6,10},{10,14},{3,7},{... | collective-permute-start | bytes 7864328 | tf_op jit(solution)/shard_map/ppermute | solution.py:16
  39.7 4.5 %copy-start.5 = (f32[32,10,3,128]{3,0,2,1:T(8,128)S(1)}, f32[32,10,3,128]{3,0,2,1:T(8,128)}, u32[]{:S(2)}) copy-start(f32[32,10,3,128]{3,0,2,1:T(8,128)} %param.13) | copy-start | bytes 1474564
  181.3 4.2 %copy-start.3 = (bf16[128,10,3,128]{0,3,2,1:T(8,128)(2,1)S(1)}, bf16[128,10,3,128]{0,3,2,1:T(8,128)(2,1)}, u32[]{:S(2)}) copy-start(bf16[128,10,3,128]{0,3,2,1:T(8,128)(2,1)} %copy.51) | copy-start | bytes 2949124
  184.2 1.3 copy-start
  185.9 1.0 copy-start.4
  204.2 2.5 copy-start.2
Sparse Core Ops, SparseCore 0:
  30.1 138.0 all-reduce.1
where the time goes:
time: 393 us; the launch traced here: 386 us
  local copies, waits for them, and re-layouts  144 us (37%)
  blocking collectives  135 us (34%)
  matrix products  72.4 us (18%)
  between operations  14.2 us (4%)
  other arithmetic  11.8 us (3%)
  starting transfers between devices  6.47 us (2%)
    all_gather x1, blocking collectives, shards(): lax.all_gather(momentum.astype(jnp.bfloat16), 'seq', axis=0, tiled=True)  135 us
    dynamic_update_slice x4, local copies, waits for them, and re-layouts, shards(): lax.map(one_block, jnp.arange(tok_rows // WIN, dtype=jnp.int32))  99.9 us
    sub x2, matrix products, window_block(): weights = jnp.exp(scores - row_max)  26.3 us
    unnamed x21, local copies, waits for them, and re-layouts  24.7 us
    dot_general x2, matrix products, window_block(): jnp.einsum('hqk,khd->qhd', probabilities, value_block, preferred_element_...  19.5 us
    dot_general x2, matrix products, swiglu_parts(): jnp.einsum('thr,rhcf->thcf', inputs, weights[:, :, 0:2], preferred_elemen...  10.3 us
    reshape x1, local copies, waits for them, and re-layouts, shards(): lax.map(one_block, jnp.arange(tok_rows // WIN, dtype=jnp.int32))  8.14 us
  transfers between devices with their start and end apart: 2, of which 0 were waited for; matrix products, arithmetic and copies ran while one was open for 8% of the time, Pallas kernels for 0%

commit v1 on v0

v1 whole, which is shorter than its diff:
```python
import functools

import jax
import jax.numpy as jnp
from jax import lax
from jax.experimental import pallas as pl
from jax.experimental.pallas import tpu as pltpu
from jax.sharding import PartitionSpec as P

WIN = 512
TILE = 256

momentum_keep = 0.9
epsilon = 1e-06
MASKED = -1e30
NT = (((1,), (1,)), ((), ()))


def call(body, name, grid, in_specs, out_specs, out_shape, scratch=(), prefetch=0, flops=0, nbytes=0):
    return pl.pallas_call(
        body,
        name=name,
        out_shape=out_shape,
        grid_spec=pltpu.PrefetchScalarGridSpec(
            num_scalar_prefetch=prefetch,
            grid=grid,
            in_specs=in_specs,
            out_specs=out_specs,
            scratch_shapes=list(scratch),
        ),
        cost_estimate=pl.CostEstimate(flops=flops, bytes_accessed=nbytes, transcendentals=0),
    )


def sigmoid(x):
    return 0.5 * jnp.tanh(0.5 * x) + 0.5


def dot(a, b, dims=None):
    if dims is None:
        return jnp.dot(a, b, preferred_element_type=jnp.float32)
    return lax.dot_general(a, b, dims, preferred_element_type=jnp.float32)


def grad_body(peers, z_ref, k_ref, v_ref, r_ref, w_ref, *refs):
    outs, total = refs[:peers], refs[peers]
    size = k_ref.shape[1]
    keys, values = k_ref[...], v_ref[...]
    turned = jnp.transpose(w_ref[...])
    rate = r_ref[pl.ds(pl.program_id(0), 1), :]
    inner = dot(turned[: 2 * size], keys, NT)
    gate, up = inner[:size], inner[size:]
    hidden_grad = dot(turned[2 * size :], values, NT) * rate
    sig = sigmoid(gate)
    silu = gate * sig
    hidden = (silu * up * rate).astype(jnp.bfloat16)
    gate_grad = (hidden_grad * up * (sig + silu * (1.0 - sig))).astype(jnp.bfloat16)
    up_grad = (hidden_grad * silu).astype(jnp.bfloat16)
    total[:, :size] = jnp.transpose(dot(gate_grad, keys))
    total[:, size : 2 * size] = jnp.transpose(dot(up_grad, keys))
    total[:, 2 * size :] = jnp.transpose(dot(hidden, values))
    own = outs[0].shape[0]
    for m in range(peers):
        row = pl.multiple_of((z_ref[0] ^ m) * own, own)
        outs[m][...] = total[pl.ds(row, own), :].astype(outs[m].dtype)


def partial_grads(z, keys, values, rates, weights, peers, kinds):
    rows, heads = keys.shape[0], rates.shape[0]
    size = weights.shape[0]
    own = size // peers
    column = pl.BlockSpec((rows, size), lambda h, z: (0, h))
    return call(
        functools.partial(grad_body, peers),
        "grads",
        (heads,),
        [
            column,
            column,
            pl.BlockSpec((heads, rows), lambda h, z: (0, 0)),
            pl.BlockSpec((size, 3 * size), lambda h, z: (0, h)),
        ],
        [pl.BlockSpec((own, 3 * size), lambda h, z: (0, h))] * peers,
        [jax.ShapeDtypeStruct((own, heads * 3 * size), kind) for kind in kinds],
        [pltpu.VMEM((size, 3 * size), jnp.float32)],
        1,
        12 * rows * heads * size * size,
        4 * rows * heads * size,
    )(z, keys, values, rates, weights)


def update_body(heads, count, z_ref, w_ref, m_ref, *refs):
    terms, w_out, m_out = refs[:count], refs[count], refs[count + 1]
    size = w_ref.shape[1] // (3 * heads)
    for g in range(3 * heads):
        cols = slice(g * size, (g + 1) * size)
        new = momentum_keep * m_ref[:, cols]
        for term in terms:
            new = new + term[:, cols].astype(jnp.float32)
        before = w_ref[:, cols].astype(jnp.float32)
        moved = before + new
        ratio = jnp.sqrt(
            (jnp.mean(before * before, axis=-1, keepdims=True) + epsilon)
            / (jnp.mean(moved * moved, axis=-1, keepdims=True) + epsilon)
        )
        m_out[:, cols] = new
        w_out[:, cols] = (moved * ratio).astype(w_out.dtype)


def updated(z, weights, momentum, terms, heads):
    own, width = momentum.shape
    whole = pl.BlockSpec((own, width), lambda i, z: (0, 0))
    return call(
        functools.partial(update_body, heads, len(terms)),
        "update",
        (1,),
        [pl.BlockSpec((own, width), lambda i, z: (z[0], 0)), whole] + [whole] * len(terms),
        [whole, whole],
        [
            jax.ShapeDtypeStruct((own, width), jnp.bfloat16),
            jax.ShapeDtypeStruct((own, width), jnp.float32),
        ],
        (),
        1,
        20 * own * width,
        16 * own * width,
    )(z, weights, momentum, *terms)


def tile_attention(query, segments):
    factor = query.shape[1] ** (-0.5)
    scores = []
    for key, _, mask in segments:
        score = dot(query, key, NT)
        scores.append(score if mask is None else jnp.where(mask, score, MASKED))
    top = functools.reduce(jnp.maximum, [jnp.max(s, axis=-1, keepdims=True) for s in scores])
    total, out = 0.0, 0.0
    for score, (_, value, _) in zip(scores, segments):
        weight = jnp.exp((score - top) * factor)
        total = total + jnp.sum(weight, axis=-1, keepdims=True)
        out = out + dot(weight.astype(jnp.bfloat16), value)
    return out / total, top * factor + jnp.log(total)


def masks():
    row = lax.broadcasted_iota(jnp.int32, (TILE, TILE), 0)
    col = lax.broadcasted_iota(jnp.int32, (TILE, TILE), 1)
    return col <= row, col > row


def local_segments(k_ref, v_ref, t, first):
    causal, late = masks()
    depth = WIN // TILE
    found = []
    for j in range(max(first, t - depth), t + 1):
        mask = causal if j == t else late if j == t - depth else None
        rows = slice(j * TILE, (j + 1) * TILE)
        found.append((k_ref[rows, :], v_ref[rows, :], mask))
    return found


def later_body(q_ref, k_ref, v_ref, o_ref):
    for t in range(WIN // TILE, q_ref.shape[0] // TILE):
        rows = slice(t * TILE, (t + 1) * TILE)
        out, _ = tile_attention(q_ref[rows, :], local_segments(k_ref, v_ref, t, 0))
        o_ref[t * TILE - WIN : (t + 1) * TILE - WIN, :] = out.astype(o_ref.dtype)


def later_blocks(queries, keys, values, heads, size):
    rows = queries.shape[0]
    column = pl.BlockSpec((rows, size), lambda h: (0, h))
    return call(
        later_body,
        "later",
        (heads,),
        [column] * 3,
        pl.BlockSpec((rows - WIN, size), lambda h: (0, h)),
        jax.ShapeDtypeStruct((rows - WIN, heads * size), jnp.bfloat16),
        flops=6 * (rows - WIN) * WIN * size * heads,
        nbytes=8 * rows * size * heads,
    )(queries, keys, values)


def carried_body(z_ref, q_ref, k_ref, v_ref, pk_ref, pv_ref, o_ref):
    causal, late = masks()
    depth = WIN // TILE
    there = z_ref[0] > 0
    for t in range(depth):
        rows = slice(t * TILE, (t + 1) * TILE)
        found = local_segments(k_ref, v_ref, t, 0)
        for j in range(t, depth):
            mask = (late & there) if j == t else there
            span = slice(j * TILE, (j + 1) * TILE)
            found.append((pk_ref[span, :], pv_ref[span, :], jnp.broadcast_to(mask, causal.shape)))
        out, _ = tile_attention(q_ref[rows, :], found)
        o_ref[rows, :] = out.astype(o_ref.dtype)


def carried_block(z, queries, keys, values, carried, size):
    heads = carried.shape[2] // size
    column = pl.BlockSpec((WIN, size), lambda h, z: (0, h))
    return call(
        carried_body,
        "carried",
        (heads,),
        [column] * 3
        + [pl.BlockSpec((None, WIN, size), lambda h, z, c=c: (c, 0, h)) for c in range(2)],
        column,
        jax.ShapeDtypeStruct((WIN, heads * size), jnp.bfloat16),
        (),
        1,
        6 * WIN * WIN * size * heads,
        10 * WIN * size * heads,
    )(z, queries, keys, values, carried, carried)


EXTRA = 16


def put_partial(o_ref, t, out, level):
    rows = slice(t * TILE, (t + 1) * TILE)
    o_ref[rows, :] = out.astype(o_ref.dtype)
    size = out.shape[1]
    lines = []
    for c in range(TILE // size):
        wide = jnp.broadcast_to(level[c * size : (c + 1) * size], (size, size))
        lines.append(jnp.transpose(wide)[:1])
    return lines


def put_levels(o_ref, lines):
    line = jnp.concatenate(lines, axis=0)
    rest = line
    parts = []
    for _ in range(3):
        part = rest.astype(jnp.bfloat16).astype(jnp.float32)
        parts.append(part)
        rest = rest - part
    parts.append(jnp.zeros((EXTRA - 3 * line.shape[0], line.shape[1]), jnp.float32))
    o_ref[WIN:, :] = jnp.concatenate(parts, axis=0).astype(o_ref.dtype)


def get_levels(o_ref):
    size = o_ref.shape[1]
    count = WIN // size
    block = o_ref[WIN:, :].astype(jnp.float32)
    return block[:count] + (block[count : 2 * count] + block[2 * count : 3 * count])


def own_part_body(q_ref, k_ref, v_ref, o_ref):
    lines = []
    for t in range(WIN // TILE):
        rows = slice(t * TILE, (t + 1) * TILE)
        out, level = tile_attention(q_ref[rows, :], local_segments(k_ref, v_ref, t, 0))
        lines += put_partial(o_ref, t, out, level)
    put_levels(o_ref, lines)


def next_part_body(q_ref, k_ref, v_ref, o_ref):
    _, late = masks()
    depth = WIN // TILE
    lines = []
    for t in range(depth):
        rows = slice(t * TILE, (t + 1) * TILE)
        found = []
        for j in range(t, depth):
            span = slice(j * TILE, (j + 1) * TILE)
            found.append((k_ref[span, :], v_ref[span, :], late if j == t else None))
        out, level = tile_attention(q_ref[rows, :], found)
        lines += put_partial(o_ref, t, out, level)
    put_levels(o_ref, lines)


def part(body, name, queries, skip, keys, values, heads, first, size, block):
    column = pl.BlockSpec((WIN, size), lambda h: (block, h + first))
    return call(
        body,
        name,
        (heads,),
        [pl.BlockSpec((WIN, size), lambda h: (0, h + skip)), column, column],
        pl.BlockSpec((WIN + EXTRA, size), lambda h: (0, h)),
        jax.ShapeDtypeStruct((WIN + EXTRA, heads * size), jnp.bfloat16),
        flops=4 * WIN * WIN * size * heads,
        nbytes=8 * WIN * size * heads,
    )(queries, keys, values)


def final_body(peers, kept, z_ref, q_ref, later_ref, carried_ref, own_ref, next_ref, *refs):
    blocks, o_ref, whole = refs[:peers], refs[peers], refs[peers + 1]
    head = pl.program_id(0)
    size = q_ref.shape[1]
    rows = blocks[0].shape[0]
    for m in range(peers):
        row = pl.multiple_of((z_ref[0] ^ m) * rows, rows)
        whole[pl.ds(row, rows), :] = blocks[m][...].astype(whole.dtype)
    weights = whole[...].astype(jnp.bfloat16)

    def network(query):
        inner = dot(query, weights[:, : 2 * size])
        gate, up = inner[:, :size], inner[:, size:]
        hidden = (gate * sigmoid(gate) * up).astype(jnp.bfloat16)
        return dot(hidden, weights[:, 2 * size :], NT)

    o_ref[WIN:, :] = (network(q_ref[WIN:, :]) + later_ref[...].astype(jnp.float32)).astype(
        o_ref.dtype
    )
    fast = network(q_ref[:WIN, :])

    @pl.when(head < kept)
    def _():
        o_ref[:WIN, :] = (fast + carried_ref[...].astype(jnp.float32)).astype(o_ref.dtype)

    @pl.when(head >= kept)
    def _():
        share = jax.nn.sigmoid(get_levels(next_ref) - get_levels(own_ref))
        share = jnp.where(z_ref[0] > 0, share, 0.0)
        for c in range(WIN // size):
            rows = slice(c * size, (c + 1) * size)
            weight = jnp.transpose(jnp.broadcast_to(share[c : c + 1], (size, size)))
            own = own_ref[rows, :].astype(jnp.float32)
            other = next_ref[rows, :].astype(jnp.float32)
            o_ref[rows, :] = (fast[rows] + own + weight * (other - own)).astype(o_ref.dtype)


def final(z, queries, later, carried, own_part, next_part, blocks, kept, size):
    rows, width = queries.shape
    heads = width // size
    peers, own = len(blocks), blocks[0].shape[0]
    column = pl.BlockSpec((rows, size), lambda h, z: (0, h))
    partial = pl.BlockSpec((WIN + EXTRA, size), lambda h, z: (0, jnp.maximum(h - kept, 0)))
    return call(
        functools.partial(final_body, peers, kept),
        "final",
        (heads,),
        [
            column,
            pl.BlockSpec((rows - WIN, size), lambda h, z: (0, h)),
            pl.BlockSpec((WIN, size), lambda h, z: (0, jnp.minimum(h, kept - 1))),
            partial,
            partial,
        ]
        + [pl.BlockSpec((own, 3 * size), lambda h, z: (0, h))] * peers,
        column,
        jax.ShapeDtypeStruct((rows, width), jnp.bfloat16),
        [pltpu.VMEM((size, 3 * size), jnp.bfloat16 if own % 16 == 0 else jnp.float32)],
        1,
        6 * rows * width * size,
        6 * rows * width,
    )(z, queries, later, carried, own_part, next_part, *blocks)


def moved_by(value, by):
    peers = lax.axis_size("seq")
    pairs = [(i, i + by) for i in range(peers) if 0 <= i + by < peers]
    return lax.ppermute(value, "seq", pairs)


def swapped(value, mask):
    return lax.ppermute(value, "seq", [(i, i ^ mask) for i in range(lax.axis_size("seq"))])


def shards(queries, keys, values, rates, fast_weights, momentum):
    rows = queries.shape[0]
    heads = rates.shape[0]
    size = fast_weights.shape[0]
    own = momentum.shape[0]
    peers = lax.axis_size("seq")
    kept = heads * 2 // 5
    z = lax.axis_index("seq").astype(jnp.int32).reshape(1)
    cut = kept * size

    carried = moved_by(jnp.stack([keys[rows - WIN :, :cut], values[rows - WIN :, :cut]]), 1)
    asked = moved_by(queries[:WIN, cut:], -1)

    flat = fast_weights.reshape(size, heads * 3 * size)
    flat_momentum = momentum.reshape(own, heads * 3 * size)
    kinds = [jnp.bfloat16 if m % 2 else jnp.float32 for m in range(peers)]
    sums = [[block] for block in partial_grads(z, keys, values, rates, flat, peers, kinds)]

    step = 1
    while step < peers:
        for m in reversed(range(peers)):
            if m % (2 * step) == step:
                terms = sums[m]
                block = functools.reduce(jnp.add, [t.astype(jnp.float32) for t in terms])
                sums[m - step].append(swapped(block.astype(jnp.bfloat16), step))
        step *= 2

    later = later_blocks(queries, keys, values, heads, size)
    own_part = part(own_part_body, "own_part", queries, kept, keys, values, heads - kept, kept, size, 0)
    given = part(
        next_part_body, "next_part", asked, 0, keys, values, heads - kept, kept, size, rows // WIN - 1
    )
    next_part = moved_by(given, 1)
    carried_out = carried_block(z, queries, keys, values, carried, size)

    new_flat, momentum_flat = updated(z, flat, flat_momentum, sums[0], heads)
    blocks = {0: new_flat}
    step = peers // 2
    while step:
        for m in sorted(blocks):
            blocks[m + step] = swapped(blocks[m], step)
        step //= 2
    blocks = [blocks[m] for m in range(peers)]

    mixed = final(z, queries, later, carried_out, own_part, next_part, blocks, kept, size)
    shape = momentum.shape
    return (mixed, new_flat.reshape(shape), momentum_flat.reshape(shape))


def solution(mesh):
    return jax.shard_map(
        shards,
        mesh=mesh,
        in_specs=(
            P(("groups", "seq"), ("head", "rep")),
            P(("groups", "seq"), ("head", "rep")),
            P(("groups", "seq"), ("head", "rep")),
            P(("head", "rep"), ("groups", "seq")),
            P(None, ("head", "rep"), None, None),
            P("seq", ("head", "rep"), None, None),
        ),
        out_specs=(
            P(("groups", "seq"), ("head", "rep")),
            P(("groups", "seq"), ("head", "rep"), None, None),
            P(("groups", "seq"), ("head", "rep"), None, None),
        ),
        check_vma=False,
    )
```

time: 393 us -> 129 us (0.33); the launches traced: 386 us -> 128 us
  blocking collectives: 135 us -> 0 us
  local copies, waits for them, and re-layouts: 144 us -> 10.7 us
  matrix products: 72.4 us -> 0 us
  Pallas kernels: 0 us -> 60 us
  waiting for transfers between devices: 0.02 us -> 33.9 us
  starting transfers between devices: 6.47 us -> 20.4 us
  between operations: 14.2 us -> 0.72 us
  other arithmetic: 11.8 us -> 1.92 us
    all_gather x1 -> x0, blocking collectives: 135 us -> none  [shards(): lax.all_gather(momentum.astype(jnp.bfloat16), 'seq', axis=0, tiled=True)]
    dynamic_update_slice x4 -> x0, local copies, waits for them, and re-layouts: 99.9 us -> none  [shards(): lax.map(one_block, jnp.arange(tok_rows // WIN, dtype=jnp.int32))]
    pallas_call x0 -> x7, Pallas kernels: none -> 60 us  [the longest x2 15.1 us: part(): call(body, name, (heads,), [pl.BlockSpec((WIN, size), lambda h: (0, h + s...]
    dot_general x8 -> x0, matrix products: 46.1 us -> none  [the longest x2 19.5 us: window_block(): jnp.einsum('hqk,khd->qhd', probabilities, value_block, preferred_element_...]
    ppermute x1 -> x9, waiting for transfers between devices: 0.01 us -> 33.9 us  [the longest x6 33.9 us: swapped(): lax.ppermute(value, 'seq', [(i, i ^ mask) for i in range(lax.axis_size('s...]
    sub x2 -> x0, matrix products: 26.3 us -> none  [window_block(): weights = jnp.exp(scores - row_max)]
    unnamed x21 -> x10, local copies, waits for them, and re-layouts: 24.7 us -> 4.52 us
    ppermute x1 -> x9, starting transfers between devices: 6.43 us -> 20.4 us  [the longest x6 14.2 us: swapped(): lax.ppermute(value, 'seq', [(i, i ^ mask) for i in range(lax.axis_size('s...]
  transfers between devices with their start and end apart: 2 -> 9, of which waited for: 0 -> 2; matrix products, arithmetic and copies ran while one was open for 8% -> 8% of each run, Pallas kernels for 0% -> 38%
where the time goes in v1:
time: 129 us; the launch traced here: 128 us
  Pallas kernels  60 us (47%)
  waiting for transfers between devices  33.9 us (26%)
  starting transfers between devices  20.4 us (16%)
  local copies, waits for them, and re-layouts  10.7 us (8%)
  other arithmetic  1.92 us (1%)
    ppermute x6, waiting for transfers between devices, swapped(): lax.ppermute(value, 'seq', [(i, i ^ mask) for i in range(lax.axis_size('s...  33.9 us
    pallas_call x2, Pallas kernels, part(): call(body, name, (heads,), [pl.BlockSpec((WIN, size), lambda h: (0, h + s...  15.1 us
    ppermute x6, starting transfers between devices, swapped(): lax.ppermute(value, 'seq', [(i, i ^ mask) for i in range(lax.axis_size('s...  14.2 us
    pallas_call x1, Pallas kernels, later_blocks(): call(later_body, 'later', (heads,), [column] * 3, pl.BlockSpec((rows - WI...  12.8 us
    pallas_call x1, Pallas kernels, final(): call(functools.partial(final_body, peers, kept), 'final', (heads,), [colu...  11.7 us
    pallas_call x1, Pallas kernels, partial_grads(): call(functools.partial(grad_body, peers), 'grads', (heads,), [column, col...  11.6 us
    pallas_call x1, Pallas kernels, carried_block(): call(carried_body, 'carried', (heads,), [column] * 3 + [pl.BlockSpec((Non...  6.18 us
    ppermute x3, starting transfers between devices, moved_by(): return lax.ppermute(value, 'seq', pairs)  6.17 us
  transfers between devices with their start and end apart: 9, of which 2 were waited for; matrix products, arithmetic and copies ran while one was open for 8% of the time, Pallas kernels for 38%

profile of v1, /device:TPU:0, one launch (start us, length us, event | category | flops | bytes accessed | tf_op | source)
XLA Modules:
  0.0 127.6 jit_solution(13672959458059160259)
XLA Ops:
  0.6 1.2 slice.11
  1.8 1.3 %collective-permute-start.1 = (bf16[512,768]{1,0:T(8,128)(2,1)S(1)}, bf16[512,768]{1,0:T(8,128)(2,1)}, u32[]{:S(2)}, u32[]{:S(2)}) collective-permute-start(bf16[512,768]{1,0:T(8,128)(2,1)S(1)} %slice.11), channel_id=1, source_target_pairs={{4,0},{8,4},{12,8},{5,1},{9,5},{13,9},{6,2},{10,6},{14,10},{7,3},{... | collective-permute-start | bytes 2359304 | tf_op jit(solution)/shard_map/ppermute | solution.py:355
  3.1 1.6 %copy.13 = bf16[128,10,3,128]{0,3,2,1:T(8,128)(2,1)S(1)} copy(bf16[128,10,3,128]{3,0,2,1:T(8,128)(2,1)} %param.10) | data formatting | bytes 1966080 | tf_op args[4]
  4.7 1.3 %copy.16.w_ref = bf16[128,3840]{1,0:T(8,128)(2,1)} copy(bf16[128,3840]{0,1:T(8,128)(2,1)S(1)} %bitcast.6) | data formatting | bytes 1966080 | tf_op jit(solution)/shard_map/reshape | solution.py:375
  6.0 11.6 %grads.1 = (f32[32,3840]{1,0:T(8,128)}, bf16[32,3840]{1,0:T(8,128)(2,1)}, f32[32,3840]{1,0:T(8,128)}, bf16[32,3840]{1,0:T(8,128)(2,1)}) custom-call(s32[1]{0:T(128)} %bitcast.z_ref, bf16[1024,1280]{1,0:T(8,128)(2,1)} %k_ref.9, bf16[1024,1280]{1,0:T(8,128)(2,1)} %v_ref.9, f32[10,1024]{1,0:T(8,128)} %r_ref.1, bf16[128,3840]{1,0:T(8,128)(2,1)} %copy.16.w_ref), custom_call_target="tpu_custom_call" | custom-call | flops 2013265920 | bytes 5242880 | tf_op jit(solution)/shard_map/grads/pallas_call | solution.py:73
  17.6 3.7 %collective-permute-start.4 = (bf16[32,3840]{1,0:T(8,128)(2,1)}, bf16[32,3840]{1,0:T(8,128)(2,1)}, u32[]{:S(2)}, u32[]{:S(2)}) collective-permute-start(bf16[32,3840]{1,0:T(8,128)(2,1)} %get-tuple-element.12), channel_id=1, source_target_pairs={{0,4},{4,0},{8,12},{12,8},{1,5},{5,1},{9,13},{13,9},{2,6},{6,2},{1... | collective-permute-start | bytes 737288 | tf_op jit(solution)/shard_map/ppermute | solution.py:359
  21.3 1.3 slice_bitcast_fusion
  22.6 0.1 pad_maximum_fusion
  22.7 2.0 %collective-permute-start = (bf16[2,512,512]{2,1,0:T(8,128)(2,1)S(1)}, bf16[2,512,512]{2,1,0:T(8,128)(2,1)S(1)}, u32[]{:S(2)}, u32[]{:S(2)}) collective-permute-start(bf16[2,512,512]{2,1,0:T(8,128)(2,1)S(1)} %pad_maximum_fusion), channel_id=1, source_target_pairs={{0,4},{4,8},{8,12},{1,5},{5,9},{9,13},{2,6},{6,10},{10,14},{3,7},{... | collective-permute-start | bytes 3145736 | tf_op jit(solution)/shard_map/ppermute | solution.py:355
  24.7 0.0 copy-start.2
  24.7 4.5 %collective-permute-start.3 = (bf16[32,3840]{1,0:T(8,128)(2,1)}, bf16[32,3840]{1,0:T(8,128)(2,1)}, u32[]{:S(2)}, u32[]{:S(2)}) collective-permute-start(bf16[32,3840]{1,0:T(8,128)(2,1)} %get-tuple-element.10), channel_id=1, source_target_pairs={{0,4},{4,0},{8,12},{12,8},{1,5},{5,1},{9,13},{13,9},{2,6},{6,2},{1... | collective-permute-start | bytes 737288 | tf_op jit(solution)/shard_map/ppermute | solution.py:359
  29.2 7.6 %next_part.1 = bf16[528,768]{1,0:T(8,128)(2,1)} custom-call(bf16[512,768]{1,0:T(8,128)(2,1)} %collective-permute-done.1.q_ref, bf16[1024,1280]{1,0:T(8,128)(2,1)} %k_ref.9, bf16[1024,1280]{1,0:T(8,128)(2,1)} %v_ref.9), custom_call_target="tpu_custom_call" | custom-call | flops 805306368 | bytes 3145728 | tf_op jit(solution)/shard_map/next_part/pallas_call | solution.py:276
  36.8 2.9 %collective-permute-start.2 = (bf16[528,768]{1,0:T(8,128)(2,1)}, bf16[528,768]{1,0:T(8,128)(2,1)}, u32[]{:S(2)}, u32[]{:S(2)}) collective-permute-start(bf16[528,768]{1,0:T(8,128)(2,1)} %next_part.1), channel_id=1, source_target_pairs={{0,4},{4,8},{8,12},{1,5},{5,9},{9,13},{2,6},{6,10},{10,14},{3,7},{... | collective-permute-start | bytes 2433032 | tf_op jit(solution)/shard_map/ppermute | solution.py:355
  39.7 1.8 %add_convert_fusion = bf16[32,3840]{1,0:T(8,128)(2,1)} fusion(f32[32,3840]{1,0:T(8,128)} %get-tuple-element.11, bf16[32,3840]{1,0:T(8,128)(2,1)} %collective-permute-done.4), kind=kLoop, calls=%fused_computation.3 | loop fusion | flops 368640 | bytes 983040 | tf_op jit(solution)/shard_map/convert_element_type | solution.py:386
  41.5 0.5 collective-permute-start.5
  42.0 0.3 copy.14
  42.4 1.0 reshape.23.m_ref
  43.4 12.3 %collective-permute-done.3.refs_1_ = bf16[32,3840]{1,0:T(8,128)(2,1)} collective-permute-done((bf16[32,3840]{1,0:T(8,128)(2,1)}, bf16[32,3840]{1,0:T(8,128)(2,1)}, u32[]{:S(2)}, u32[]{:S(2)}) %collective-permute-start.3) | collective-permute-done | bytes 245792 | tf_op jit(solution)/shard_map/ppermute | solution.py:359
  55.7 21.6 %collective-permute-done.5.refs_2_ = bf16[32,3840]{1,0:T(8,128)(2,1)} collective-permute-done((bf16[32,3840]{1,0:T(8,128)(2,1)}, bf16[32,3840]{1,0:T(8,128)(2,1)}, u32[]{:S(2)}, u32[]{:S(2)}) %collective-permute-start.5) | collective-permute-done | bytes 245792 | tf_op jit(solution)/shard_map/ppermute | solution.py:359
  77.3 2.6 %update.1 = (bf16[32,3840]{1,0:T(8,128)(2,1)}, f32[32,3840]{1,0:T(8,128)}) custom-call(s32[1]{0:T(128)} %bitcast.z_ref, bf16[128,3840]{1,0:T(8,128)(2,1)} %copy.16.w_ref, f32[32,3840]{1,0:T(8,128)} %reshape.23.m_ref, f32[32,3840]{1,0:T(8,128)} %get-tuple-element.9.refs_0_, bf16[32,3840]{1,0:T(8,128)(2,1)} %collective-permute-done.3.refs_1_, ...), custom_call_target="tpu_custom_call" | custom-call | flops 2457600 | bytes 1966080 | tf_op jit(solution)/shard_map/update/pallas_call | solution.py:113
  79.9 3.4 %collective-permute-start.7 = (bf16[32,3840]{1,0:T(8,128)(2,1)}, bf16[32,3840]{1,0:T(8,128)(2,1)}, u32[]{:S(2)}, u32[]{:S(2)}) collective-permute-start(bf16[32,3840]{1,0:T(8,128)(2,1)} %get-tuple-element.13.refs_0_), channel_id=1, source_target_pairs={{0,8},{4,12},{8,0},{12,4},{1,9},{5,13},{9,1},{13,5},{2,10},{6,14},... | collective-permute-start | bytes 737288 | tf_op jit(solution)/shard_map/ppermute | solution.py:359
  83.3 7.5 %own_part.1.own_ref = bf16[528,768]{1,0:T(8,128)(2,1)} custom-call(bf16[1024,1280]{1,0:T(8,128)(2,1)} %q_ref.7, bf16[1024,1280]{1,0:T(8,128)(2,1)} %k_ref.9, bf16[1024,1280]{1,0:T(8,128)(2,1)} %v_ref.9), custom_call_target="tpu_custom_call" | custom-call | flops 805306368 | bytes 3145728 | tf_op jit(solution)/shard_map/own_part/pallas_call | solution.py:276
  90.9 2.0 %collective-permute-start.6 = (bf16[32,3840]{1,0:T(8,128)(2,1)S(1)}, bf16[32,3840]{1,0:T(8,128)(2,1)}, u32[]{:S(2)}, u32[]{:S(2)}) collective-permute-start(bf16[32,3840]{1,0:T(8,128)(2,1)S(1)} %copy-done.1), channel_id=1, source_target_pairs={{0,4},{4,0},{8,12},{12,8},{1,5},{5,1},{9,13},{13,9},{2,6},{6,2},{1... | collective-permute-start | bytes 737288 | tf_op jit(solution)/shard_map/ppermute | solution.py:359
  92.9 0.1 collective-permute-start.8
  92.9 12.8 %later.1.later_ref = bf16[512,1280]{1,0:T(8,128)(2,1)} custom-call(bf16[1024,1280]{1,0:T(8,128)(2,1)} %q_ref.7, bf16[1024,1280]{1,0:T(8,128)(2,1)} %k_ref.9, bf16[1024,1280]{1,0:T(8,128)(2,1)} %v_ref.9), custom_call_target="tpu_custom_call" | custom-call | flops 2013265920 | bytes 10485760 | tf_op jit(solution)/shard_map/later/pallas_call | solution.py:172
  105.7 0.1 reshape.24
  105.8 1.3 %reshape.25 = f32[32,10,3,128]{3,2,1,0:T(4,128)S(1)} reshape(f32[32,3840]{1,0:T(8,128)} %get-tuple-element.14) | data formatting | bytes 983040 | tf_op jit(solution)/shard_map/reshape | solution.py:408
  107.1 0.9 copy.18
  107.9 0.7 copy.17
  108.7 1.0 copy-done
  109.7 6.2 %carried.1.carried_ref = bf16[512,512]{1,0:T(8,128)(2,1)} custom-call(s32[1]{0:T(128)} %bitcast.z_ref, bf16[1024,1280]{1,0:T(8,128)(2,1)} %q_ref.7, bf16[1024,1280]{1,0:T(8,128)(2,1)} %k_ref.9, bf16[1024,1280]{1,0:T(8,128)(2,1)} %v_ref.9, bf16[2,512,512]{2,1,0:T(8,128)(2,1)} %copy-done, bf16[2,512,512]{2,1,0:T(8,128)(2,1)} %copy-done), custom_call_target="tpu_custom_call" | custom-call | flops 805306368 | bytes 2621440 | tf_op jit(solution)/shard_map/carried/pallas_call | solution.py:202
  115.9 11.7 %final.1 = bf16[1024,1280]{1,0:T(8,128)(2,1)} custom-call(s32[1]{0:T(128)} %bitcast.z_ref, bf16[1024,1280]{1,0:T(8,128)(2,1)} %q_ref.7, bf16[512,1280]{1,0:T(8,128)(2,1)} %later.1.later_ref, bf16[512,512]{1,0:T(8,128)(2,1)} %carried.1.carried_ref, bf16[528,768]{1,0:T(8,128)(2,1)} %own_part.1.own_ref, bf16[528,768]{1,0:T(8,128)(2,1)} %collective-permute-done.2.next_ref, ...), custom_call_target="tpu_custom_call" | custom-call | flops 1006632960 | bytes 7864320 | tf_op jit(solution)/shard_map/final/pallas_call | solution.py:331
  (11 shorter events, 0.0 us)
Async XLA Ops:
  1.8 27.4 %collective-permute-start.1 = (bf16[512,768]{1,0:T(8,128)(2,1)S(1)}, bf16[512,768]{1,0:T(8,128)(2,1)}, u32[]{:S(2)}, u32[]{:S(2)}) collective-permute-start(bf16[512,768]{1,0:T(8,128)(2,1)S(1)} %slice.11), channel_id=1, source_target_pairs={{4,0},{8,4},{12,8},{5,1},{9,5},{13,9},{6,2},{10,6},{14,10},{7,3},{... | collective-permute-start | bytes 2359304 | tf_op jit(solution)/shard_map/ppermute | solution.py:355
  17.6 22.1 %collective-permute-start.4 = (bf16[32,3840]{1,0:T(8,128)(2,1)}, bf16[32,3840]{1,0:T(8,128)(2,1)}, u32[]{:S(2)}, u32[]{:S(2)}) collective-permute-start(bf16[32,3840]{1,0:T(8,128)(2,1)} %get-tuple-element.12), channel_id=1, source_target_pairs={{0,4},{4,0},{8,12},{12,8},{1,5},{5,1},{9,13},{13,9},{2,6},{6,2},{1... | collective-permute-start | bytes 737288 | tf_op jit(solution)/shard_map/ppermute | solution.py:359
  22.7 86.0 %collective-permute-start = (bf16[2,512,512]{2,1,0:T(8,128)(2,1)S(1)}, bf16[2,512,512]{2,1,0:T(8,128)(2,1)S(1)}, u32[]{:S(2)}, u32[]{:S(2)}) collective-permute-start(bf16[2,512,512]{2,1,0:T(8,128)(2,1)S(1)} %pad_maximum_fusion), channel_id=1, source_target_pairs={{0,4},{4,8},{8,12},{1,5},{5,9},{9,13},{2,6},{6,10},{10,14},{3,7},{... | collective-permute-start | bytes 3145736 | tf_op jit(solution)/shard_map/ppermute | solution.py:355
  24.7 17.3 %copy-start.2 = (f32[32,10,3,128]{3,0,2,1:T(8,128)S(1)}, f32[32,10,3,128]{3,0,2,1:T(8,128)}, u32[]{:S(2)}) copy-start(f32[32,10,3,128]{3,0,2,1:T(8,128)} %param.11) | copy-start | bytes 1474564
  24.7 31.0 %collective-permute-start.3 = (bf16[32,3840]{1,0:T(8,128)(2,1)}, bf16[32,3840]{1,0:T(8,128)(2,1)}, u32[]{:S(2)}, u32[]{:S(2)}) collective-permute-start(bf16[32,3840]{1,0:T(8,128)(2,1)} %get-tuple-element.10), channel_id=1, source_target_pairs={{0,4},{4,0},{8,12},{12,8},{1,5},{5,1},{9,13},{13,9},{2,6},{6,2},{1... | collective-permute-start | bytes 737288 | tf_op jit(solution)/shard_map/ppermute | solution.py:359
  36.8 79.1 %collective-permute-start.2 = (bf16[528,768]{1,0:T(8,128)(2,1)}, bf16[528,768]{1,0:T(8,128)(2,1)}, u32[]{:S(2)}, u32[]{:S(2)}) collective-permute-start(bf16[528,768]{1,0:T(8,128)(2,1)} %next_part.1), channel_id=1, source_target_pairs={{0,4},{4,8},{8,12},{1,5},{5,9},{9,13},{2,6},{6,10},{10,14},{3,7},{... | collective-permute-start | bytes 2433032 | tf_op jit(solution)/shard_map/ppermute | solution.py:355
  41.5 35.8 %collective-permute-start.5 = (bf16[32,3840]{1,0:T(8,128)(2,1)}, bf16[32,3840]{1,0:T(8,128)(2,1)}, u32[]{:S(2)}, u32[]{:S(2)}) collective-permute-start(bf16[32,3840]{1,0:T(8,128)(2,1)} %add_convert_fusion), channel_id=1, source_target_pairs={{0,8},{4,12},{8,0},{12,4},{1,9},{5,13},{9,1},{13,5},{2,10},{6,14},... | collective-permute-start | bytes 737288 | tf_op jit(solution)/shard_map/ppermute | solution.py:359
  79.9 11.0 %copy-start.1 = (bf16[32,3840]{1,0:T(8,128)(2,1)S(1)}, bf16[32,3840]{1,0:T(8,128)(2,1)}, u32[]{:S(2)}) copy-start(bf16[32,3840]{1,0:T(8,128)(2,1)} %get-tuple-element.13.refs_0_) | copy-start | bytes 737284
  79.9 13.0 %collective-permute-start.7 = (bf16[32,3840]{1,0:T(8,128)(2,1)}, bf16[32,3840]{1,0:T(8,128)(2,1)}, u32[]{:S(2)}, u32[]{:S(2)}) collective-permute-start(bf16[32,3840]{1,0:T(8,128)(2,1)} %get-tuple-element.13.refs_0_), channel_id=1, source_target_pairs={{0,8},{4,12},{8,0},{12,4},{1,9},{5,13},{9,1},{13,5},{2,10},{6,14},... | collective-permute-start | bytes 737288 | tf_op jit(solution)/shard_map/ppermute | solution.py:359
  90.9 25.0 %collective-permute-start.6 = (bf16[32,3840]{1,0:T(8,128)(2,1)S(1)}, bf16[32,3840]{1,0:T(8,128)(2,1)}, u32[]{:S(2)}, u32[]{:S(2)}) collective-permute-start(bf16[32,3840]{1,0:T(8,128)(2,1)S(1)} %copy-done.1), channel_id=1, source_target_pairs={{0,4},{4,0},{8,12},{12,8},{1,5},{5,1},{9,13},{13,9},{2,6},{6,2},{1... | collective-permute-start | bytes 737288 | tf_op jit(solution)/shard_map/ppermute | solution.py:359
  92.9 23.0 %collective-permute-start.8 = (bf16[32,3840]{1,0:T(8,128)(2,1)}, bf16[32,3840]{1,0:T(8,128)(2,1)}, u32[]{:S(2)}, u32[]{:S(2)}) collective-permute-start(bf16[32,3840]{1,0:T(8,128)(2,1)} %collective-permute-done.7.refs_2_), channel_id=1, source_target_pairs={{0,4},{4,0},{8,12},{12,8},{1,5},{5,1},{9,13},{13,9},{2,6},{6,2},{1... | collective-permute-start | bytes 737288 | tf_op jit(solution)/shard_map/ppermute | solution.py:359
  108.7 1.0 copy-start

commit v2 on v0

v2 whole, which is shorter than its diff:
```python
import functools
import math

import jax
import jax.numpy as jnp
from jax import lax
from jax.experimental import pallas as pl
from jax.experimental.pallas import tpu as pltpu
from jax.sharding import PartitionSpec as P

WIN = 512
TILE = 256

momentum_keep = 0.9
epsilon = 1e-06
MASKED = -1e30
LOG2E = math.log2(math.e)
NT = (((1,), (1,)), ((), ()))


def call(body, name, grid, in_specs, out_specs, out_shape, scratch=(), prefetch=0, flops=0, nbytes=0):
    return pl.pallas_call(
        body,
        name=name,
        out_shape=out_shape,
        grid_spec=pltpu.PrefetchScalarGridSpec(
            num_scalar_prefetch=prefetch,
            grid=grid,
            in_specs=in_specs,
            out_specs=out_specs,
            scratch_shapes=list(scratch),
        ),
        cost_estimate=pl.CostEstimate(flops=flops, bytes_accessed=nbytes, transcendentals=0),
    )


def sigmoid(x):
    return 0.5 * jnp.tanh(0.5 * x) + 0.5


def dot(a, b, dims=None):
    if dims is None:
        return jnp.dot(a, b, preferred_element_type=jnp.float32)
    return lax.dot_general(a, b, dims, preferred_element_type=jnp.float32)


def steps_of(heads, most=5):
    return next(n for n in range(min(heads, most), 0, -1) if heads % n == 0)


def grad_body(peers, group, chunk, z_ref, k_ref, v_ref, r_ref, w_ref, *refs):
    outs, total = refs[:peers], refs[peers]
    size = w_ref.shape[2]
    rows = k_ref.shape[0]
    own = outs[0].shape[2]
    first = pl.program_id(0) * group
    tasks = [(g, c) for g in range(group) for c in range(0, rows, chunk)]
    turned = {}

    def products(g, c):
        if g not in turned:
            flipped = [jnp.transpose(w_ref[g, m]) for m in range(3)]
            turned[g] = (jnp.concatenate(flipped[:2], axis=0), flipped[2])
        cols, span = slice(g * size, (g + 1) * size), slice(c, c + chunk)
        inner = dot(turned[g][0], k_ref[span, cols], NT)
        return inner, dot(turned[g][1], v_ref[span, cols], NT)

    def finish(g, c, inner, back, sums):
        cols, span = slice(g * size, (g + 1) * size), slice(c, c + chunk)
        rate = r_ref[pl.ds(first + g, 1), span]
        gate, up = inner[:size], inner[size:]
        back = back * rate
        sig = sigmoid(gate)
        silu = gate * sig
        hidden = (silu * (up * rate)).astype(jnp.bfloat16)
        gate_grad = (back * up * (sig + silu * (1.0 - sig))).astype(jnp.bfloat16)
        up_grad = (back * silu).astype(jnp.bfloat16)
        found = [
            dot(jnp.concatenate([gate_grad, up_grad], axis=0), k_ref[span, cols]),
            dot(hidden, v_ref[span, cols]),
        ]
        sums = found if sums is None else [a + b for a, b in zip(sums, found)]
        if c + chunk < rows:
            return sums
        total[g % 2, 0] = jnp.transpose(sums[0][:size])
        total[g % 2, 1] = jnp.transpose(sums[0][size:])
        total[g % 2, 2] = jnp.transpose(sums[1])
        for m in range(peers):
            row = pl.multiple_of((z_ref[0] ^ m) * own, own)
            outs[m][g] = total[g % 2, :, pl.ds(row, own), :].astype(outs[m].dtype)
        return None

    sums = None
    ready = products(*tasks[0])
    for i, task in enumerate(tasks):
        following = products(*tasks[i + 1]) if i + 1 < len(tasks) else None
        sums = finish(*task, *ready, sums)
        ready = following


def partial_grads(z, keys, values, rates, weights, peers, kinds):
    rows = keys.shape[0]
    heads, _, size, _ = weights.shape
    own = size // peers
    group = steps_of(heads)
    column = pl.BlockSpec((rows, group * size), lambda h, z: (0, h))
    return call(
        functools.partial(grad_body, peers, group, min(rows, 512)),
        "grads",
        (heads // group,),
        [
            column,
            column,
            pl.BlockSpec((heads, rows), lambda h, z: (0, 0)),
            pl.BlockSpec((group, 3, size, size), lambda h, z: (h, 0, 0, 0)),
        ],
        [pl.BlockSpec((group, 3, own, size), lambda h, z: (h, 0, 0, 0))] * peers,
        [jax.ShapeDtypeStruct((heads, 3, own, size), kind) for kind in kinds],
        [pltpu.VMEM((2, 3, size, size), jnp.float32)],
        1,
        12 * rows * heads * size * size,
        4 * rows * heads * size,
    )(z, keys, values, rates, weights)


def update_body(count, z_ref, w_ref, m_ref, *refs):
    terms, w_out, m_out = refs[:count], refs[count], refs[count + 1]
    for g in range(w_ref.shape[0]):
        new = momentum_keep * m_ref[g]
        for term in terms:
            new = new + term[g].astype(jnp.float32)
        before = w_ref[g].astype(jnp.float32)
        moved = before + new
        ratio = jnp.sqrt(
            (jnp.mean(before * before, axis=-1, keepdims=True) + epsilon)
            / (jnp.mean(moved * moved, axis=-1, keepdims=True) + epsilon)
        )
        m_out[g] = new
        w_out[g] = (moved * ratio).astype(w_out.dtype)


def updated(z, weights, momentum, terms):
    shape = momentum.shape
    whole = pl.BlockSpec(shape, lambda i, z: (0, 0, 0, 0))
    count = momentum.size
    return call(
        functools.partial(update_body, len(terms)),
        "update",
        (1,),
        [pl.BlockSpec(shape, lambda i, z: (0, 0, z[0], 0)), whole] + [whole] * len(terms),
        [whole, whole],
        [jax.ShapeDtypeStruct(shape, jnp.bfloat16), jax.ShapeDtypeStruct(shape, jnp.float32)],
        (),
        1,
        20 * count,
        16 * count,
    )(z, weights, momentum, *terms)


def attend(tasks, s_ref):
    def scores(i):
        query, segments, _ = tasks[i]
        query = query()
        top = None
        for j, (key, _, mask) in enumerate(segments):
            score = dot(key(), query, NT)
            if mask is not None:
                score = jnp.where(mask, score, MASKED)
            s_ref[i % 2, j * TILE : (j + 1) * TILE, :] = score
            most = jnp.max(score.reshape(TILE // 8, 8, TILE), axis=0)
            top = most if top is None else jnp.maximum(top, most)
        return jnp.max(top, axis=0, keepdims=True)

    def weigh(i, top):
        _, segments, emit = tasks[i]
        factor = segments[0][0]().shape[1] ** (-0.5)
        out = total = None
        for j, (_, value, _) in enumerate(segments):
            score = s_ref[i % 2, j * TILE : (j + 1) * TILE, :]
            weight = jnp.exp2((score - top) * (factor * LOG2E))
            part = jnp.sum(weight.reshape(TILE // 8, 8, TILE), axis=0)
            product = dot(value(), weight.astype(jnp.bfloat16))
            total = part if total is None else total + part
            out = product if out is None else out + product
        total = jnp.sum(total, axis=0, keepdims=True)
        emit(out * (1.0 / total), top * factor + jnp.log(total))

    top = scores(0)
    for i in range(len(tasks)):
        following = scores(i + 1) if i + 1 < len(tasks) else None
        weigh(i, top)
        top = following


def masks():
    row = lax.broadcasted_iota(jnp.int32, (TILE, TILE), 0)
    col = lax.broadcasted_iota(jnp.int32, (TILE, TILE), 1)
    return row <= col, row > col


def spans(ref, t, cols):
    return lambda: ref[t * TILE : (t + 1) * TILE, cols]


def turned(memo, ref, t, cols, key):
    def load():
        if (key, t) not in memo:
            memo[key, t] = jnp.transpose(ref[t * TILE : (t + 1) * TILE, cols])
        return memo[key, t]

    return load


def put(o_ref, t, cols):
    def emit(out, level):
        o_ref[t * TILE : (t + 1) * TILE, cols] = jnp.transpose(out).astype(o_ref.dtype)

    return emit


SCORES = (WIN // TILE + 1) * TILE


def later_body(group, q_ref, k_ref, v_ref, o_ref, s_ref):
    size = q_ref.shape[1] // group
    causal, late = masks()
    depth = WIN // TILE
    tasks = []
    for g in range(group):
        cols = slice(g * size, (g + 1) * size)
        memo = {}
        for t in range(depth, q_ref.shape[0] // TILE):
            found = [
                (
                    spans(k_ref, j, cols),
                    turned(memo, v_ref, j, cols, 0),
                    causal if j == t else late if j == t - depth else None,
                )
                for j in range(t - depth, t + 1)
            ]
            tasks.append((spans(q_ref, t, cols), found, put(o_ref, t - depth, cols)))
    attend(tasks, s_ref)


def later_blocks(queries, keys, values, heads, size, first, group):
    rows = queries.shape[0]
    column = pl.BlockSpec((rows, group * size), lambda h: (0, first // group + h))
    return call(
        functools.partial(later_body, group),
        "later",
        (heads // group,),
        [column] * 3,
        pl.BlockSpec((rows - WIN, group * size), lambda h: (0, h)),
        jax.ShapeDtypeStruct((rows - WIN, heads * size), jnp.bfloat16),
        [pltpu.VMEM((2, SCORES, TILE), jnp.float32)],
        0,
        6 * (rows - WIN) * WIN * size * heads,
        8 * rows * size * heads,
    )(queries, keys, values)


def carried_body(group, z_ref, q_ref, k_ref, v_ref, pk_ref, pv_ref, o_ref, s_ref):
    size = q_ref.shape[1] // group
    causal, late = masks()
    depth = WIN // TILE
    there = jnp.broadcast_to(z_ref[0] > 0, causal.shape)
    tasks = []
    for g in range(group):
        cols = slice(g * size, (g + 1) * size)
        memo = {}
        for t in range(depth):
            found = [
                (spans(pk_ref, j, cols), turned(memo, pv_ref, j, cols, 1), late & there if j == t else there)
                for j in range(t, depth)
            ]
            found += [
                (spans(k_ref, j, cols), turned(memo, v_ref, j, cols, 0), causal if j == t else None)
                for j in range(t + 1)
            ]
            tasks.append((spans(q_ref, t, cols), found, put(o_ref, t, cols)))
    attend(tasks, s_ref)


def carried_block(z, queries, keys, values, carried, size):
    heads = carried.shape[2] // size
    group = steps_of(heads, 4)
    width = queries.shape[1]
    column = pl.BlockSpec((WIN, group * size), lambda h, z: (0, h))
    return call(
        functools.partial(carried_body, group),
        "carried",
        (heads // group,),
        [column] * 3
        + [pl.BlockSpec((None, WIN, group * size), lambda h, z, c=c: (c, 0, h)) for c in range(2)],
        column,
        jax.ShapeDtypeStruct((WIN, width), jnp.bfloat16),
        [pltpu.VMEM((2, SCORES, TILE), jnp.float32)],
        1,
        6 * WIN * WIN * size * heads,
        10 * WIN * size * heads,
    )(z, queries, keys, values, carried, carried)


EXTRA = 16


def put_partial(o_ref, g, t, size):
    def emit(out, level):
        span = slice(t * TILE, (t + 1) * TILE)
        o_ref[g, :size, span] = out.astype(o_ref.dtype)
        rest, parts = level, []
        for _ in range(3):
            term = rest.astype(jnp.bfloat16).astype(jnp.float32)
            parts.append(term)
            rest = rest - term
        parts.append(jnp.zeros((EXTRA - 3, TILE), jnp.float32))
        o_ref[g, size:, span] = jnp.concatenate(parts, axis=0).astype(o_ref.dtype)

    return emit


def next_part_body(group, q_ref, k_ref, v_ref, o_ref, s_ref):
    size = q_ref.shape[1] // group
    _, late = masks()
    depth = WIN // TILE
    tasks = []
    for g in range(group):
        cols = slice(g * size, (g + 1) * size)
        memo = {}
        for t in range(depth):
            found = [
                (spans(k_ref, j, cols), turned(memo, v_ref, j, cols, 0), late if j == t else None)
                for j in range(t, depth)
            ]
            tasks.append((spans(q_ref, t, cols), found, put_partial(o_ref, g, t, size)))
    attend(tasks, s_ref)


def next_part(asked, keys, values, first, size):
    heads = asked.shape[1] // size
    block = keys.shape[0] // WIN - 1
    group = math.gcd(heads, first)
    column = pl.BlockSpec((WIN, group * size), lambda h: (block, h + first // group))
    return call(
        functools.partial(next_part_body, group),
        "next_part",
        (heads // group,),
        [pl.BlockSpec((WIN, group * size), lambda h: (0, h)), column, column],
        pl.BlockSpec((group, size + EXTRA, WIN), lambda h: (h, 0, 0)),
        jax.ShapeDtypeStruct((heads, size + EXTRA, WIN), jnp.bfloat16),
        [pltpu.VMEM((2, WIN, TILE), jnp.float32)],
        0,
        4 * WIN * WIN * size * heads,
        8 * WIN * size * heads,
    )(asked, keys, values)


def joined_body(group, z_ref, q_ref, k_ref, v_ref, p_ref, _, o_ref, s_ref):
    size = q_ref.shape[1] // group
    causal, _ = masks()
    depth = WIN // TILE

    def join(g, t, cols):
        def emit(out, level):
            span = slice(t * TILE, (t + 1) * TILE)
            terms = p_ref[g, size:, span].astype(jnp.float32)
            other = terms[0:1] + (terms[1:2] + terms[2:3])
            share = jnp.where(z_ref[0] > 0, jax.nn.sigmoid(other - level), 0.0)
            out = out + share * (p_ref[g, :size, span].astype(jnp.float32) - out)
            o_ref[span, cols] = jnp.transpose(out).astype(o_ref.dtype)

        return emit

    tasks = []
    for g in range(group):
        cols = slice(g * size, (g + 1) * size)
        memo = {}
        for t in range(depth):
            found = [
                (spans(k_ref, j, cols), turned(memo, v_ref, j, cols, 0), causal if j == t else None)
                for j in range(t + 1)
            ]
            tasks.append((spans(q_ref, t, cols), found, join(g, t, cols)))
    attend(tasks, s_ref)


def joined_block(z, queries, keys, values, given, partly, first, size):
    heads = given.shape[0]
    group = math.gcd(heads, first)
    column = pl.BlockSpec((WIN, group * size), lambda h, z: (0, h + first // group))
    return pl.pallas_call(
        functools.partial(joined_body, group),
        name="joined",
        out_shape=jax.ShapeDtypeStruct(partly.shape, partly.dtype),
        grid_spec=pltpu.PrefetchScalarGridSpec(
            num_scalar_prefetch=1,
            grid=(heads // group,),
            in_specs=[
                column,
                column,
                column,
                pl.BlockSpec((group, size + EXTRA, WIN), lambda h, z: (h, 0, 0)),
                pl.BlockSpec(memory_space=pl.ANY),
            ],
            out_specs=column,
            scratch_shapes=[pltpu.VMEM((2, WIN, TILE), jnp.float32)],
        ),
        input_output_aliases={5: 0},
        cost_estimate=pl.CostEstimate(
            flops=4 * WIN * WIN * size * heads, bytes_accessed=10 * WIN * size * heads, transcendentals=0
        ),
    )(z, queries, keys, values, given, partly)


def final_body(peers, group, z_ref, q_ref, first_ref, later_ref, *refs):
    blocks, o_ref, whole = refs[:peers], refs[peers], refs[peers + 1]
    size = q_ref.shape[1] // group
    own = blocks[0].shape[2]
    for m in range(peers):
        row = pl.multiple_of((z_ref[0] ^ m) * own, own)
        whole[:, :, pl.ds(row, own), :] = blocks[m][...].astype(whole.dtype)
    tasks = [(g, c) for g in range(group) for c in range(0, q_ref.shape[0], WIN)]

    def products(g, c):
        query = q_ref[c : c + WIN, g * size : (g + 1) * size]
        both = jnp.concatenate([whole[g, 0], whole[g, 1]], axis=1).astype(jnp.bfloat16)
        return dot(query, both)

    def finish(g, c, inner):
        cols = slice(g * size, (g + 1) * size)
        gate, up = inner[:, :size], inner[:, size:]
        hidden = (gate * sigmoid(gate) * up).astype(jnp.bfloat16)
        fast = dot(hidden, whole[g, 2].astype(jnp.bfloat16), NT)
        kept = first_ref[:, cols] if c == 0 else later_ref[c - WIN : c, cols]
        o_ref[c : c + WIN, cols] = (fast + kept.astype(jnp.float32)).astype(o_ref.dtype)

    ready = products(*tasks[0])
    for i, task in enumerate(tasks):
        following = products(*tasks[i + 1]) if i + 1 < len(tasks) else None
        finish(*task, ready)
        ready = following


def final(z, queries, first, later, blocks, size):
    rows, width = queries.shape
    heads = width // size
    group = steps_of(heads)
    peers, own = len(blocks), blocks[0].shape[2]
    column = pl.BlockSpec((rows, group * size), lambda h, z: (0, h))
    kind = jnp.bfloat16 if own % 16 == 0 else jnp.float32
    return call(
        functools.partial(final_body, peers, group),
        "final",
        (heads // group,),
        [
            column,
            pl.BlockSpec((WIN, group * size), lambda h, z: (0, h)),
            pl.BlockSpec((rows - WIN, group * size), lambda h, z: (0, h)),
        ]
        + [pl.BlockSpec((group, 3, own, size), lambda h, z: (h, 0, 0, 0))] * peers,
        column,
        jax.ShapeDtypeStruct((rows, width), jnp.bfloat16),
        [pltpu.VMEM((group, 3, size, size), kind)],
        1,
        6 * rows * width * size,
        6 * rows * width,
    )(z, queries, first, later, *blocks)


def moved_by(value, by):
    peers = lax.axis_size("seq")
    pairs = [(i, i + by) for i in range(peers) if 0 <= i + by < peers]
    return lax.ppermute(value, "seq", pairs)


def swapped(value, mask):
    return lax.ppermute(value, "seq", [(i, i ^ mask) for i in range(lax.axis_size("seq"))])


def shards(queries, keys, values, rates, fast_weights, momentum):
    rows = queries.shape[0]
    heads = rates.shape[0]
    size = fast_weights.shape[0]
    peers = lax.axis_size("seq")
    kept = heads * 2 // 5
    z = lax.axis_index("seq").astype(jnp.int32).reshape(1)
    cut = kept * size

    carried = moved_by(jnp.stack([keys[rows - WIN :, :cut], values[rows - WIN :, :cut]]), 1)
    asked = moved_by(queries[:WIN, cut:], -1)

    weights = jnp.transpose(fast_weights, (1, 2, 0, 3))
    own_momentum = jnp.transpose(momentum, (1, 2, 0, 3))
    kinds = [jnp.bfloat16 if m % 2 else jnp.float32 for m in range(peers)]
    sums = [[block] for block in partial_grads(z, keys, values, rates, weights, peers, kinds)]

    step = 1
    while step < peers:
        for m in reversed(range(peers)):
            if m % (2 * step) == step:
                terms = sums[m]
                block = functools.reduce(jnp.add, [t.astype(jnp.float32) for t in terms])
                sums[m - step].append(swapped(block.astype(jnp.bfloat16), step))
        step *= 2

    later = later_blocks(queries, keys, values, heads, size, 0, steps_of(heads))
    given = moved_by(next_part(asked, keys, values, kept, size), 1)
    first = carried_block(z, queries, keys, values, carried, size)
    first = joined_block(z, queries, keys, values, given, first, kept, size)

    new_rows, new_momentum = updated(z, weights, own_momentum, sums[0])
    blocks = {0: new_rows}
    step = peers // 2
    while step:
        for m in sorted(blocks):
            blocks[m + step] = swapped(blocks[m], step)
        step //= 2
    blocks = [blocks[m] for m in range(peers)]

    mixed = final(z, queries, first, later, blocks, size)
    return (mixed, jnp.transpose(new_rows, (2, 0, 1, 3)), jnp.transpose(new_momentum, (2, 0, 1, 3)))


def solution(mesh):
    return jax.shard_map(
        shards,
        mesh=mesh,
        in_specs=(
            P(("groups", "seq"), ("head", "rep")),
            P(("groups", "seq"), ("head", "rep")),
            P(("groups", "seq"), ("head", "rep")),
            P(("head", "rep"), ("groups", "seq")),
            P(None, ("head", "rep"), None, None),
            P("seq", ("head", "rep"), None, None),
        ),
        out_specs=(
            P(("groups", "seq"), ("head", "rep")),
            P(("groups", "seq"), ("head", "rep"), None, None),
            P(("groups", "seq"), ("head", "rep"), None, None),
        ),
        check_vma=False,
    )
```

time: 393 us -> 117 us (0.30); the launches traced: 386 us -> 117 us
  local copies, waits for them, and re-layouts: 144 us -> 5.75 us
  blocking collectives: 135 us -> 0 us
  matrix products: 72.4 us -> 0 us
  waiting for transfers between devices: 0.02 us -> 44.7 us
  Pallas kernels: 0 us -> 41.8 us
  starting transfers between devices: 6.47 us -> 22.5 us
  between operations: 14.2 us -> 0.74 us
  other arithmetic: 11.8 us -> 1.1 us
    all_gather x1 -> x0, blocking collectives: 135 us -> none  [shards(): lax.all_gather(momentum.astype(jnp.bfloat16), 'seq', axis=0, tiled=True)]
    dynamic_update_slice x4 -> x0, local copies, waits for them, and re-layouts: 99.9 us -> none  [shards(): lax.map(one_block, jnp.arange(tok_rows // WIN, dtype=jnp.int32))]
    dot_general x8 -> x0, matrix products: 46.1 us -> none  [the longest x2 19.5 us: window_block(): jnp.einsum('hqk,khd->qhd', probabilities, value_block, preferred_element_...]
    ppermute x1 -> x9, waiting for transfers between devices: 0.01 us -> 44.7 us  [the longest x6 43.8 us: swapped(): lax.ppermute(value, 'seq', [(i, i ^ mask) for i in range(lax.axis_size('s...]
    pallas_call x0 -> x7, Pallas kernels: none -> 41.8 us  [the longest x1 9.75 us: partial_grads(): call(functools.partial(grad_body, peers, group, min(rows, 512)), 'grads',...]
    sub x2 -> x0, matrix products: 26.3 us -> none  [window_block(): weights = jnp.exp(scores - row_max)]
    unnamed x21 -> x12, local copies, waits for them, and re-layouts: 24.7 us -> 3.29 us
    ppermute x1 -> x9, starting transfers between devices: 6.43 us -> 22.5 us  [the longest x6 16.3 us: swapped(): lax.ppermute(value, 'seq', [(i, i ^ mask) for i in range(lax.axis_size('s...]
  transfers between devices with their start and end apart: 2 -> 9, of which waited for: 0 -> 4; matrix products, arithmetic and copies ran while one was open for 8% -> 2% of each run, Pallas kernels for 0% -> 31%
where the time goes in v2:
time: 117 us
  waiting for transfers between devices  44.7 us (38%)
  Pallas kernels  41.8 us (36%)
  starting transfers between devices  22.5 us (19%)
  local copies, waits for them, and re-layouts  5.75 us (5%)
    ppermute x6, waiting for transfers between devices, swapped(): lax.ppermute(value, 'seq', [(i, i ^ mask) for i in range(lax.axis_size('s...  43.8 us
    ppermute x6, starting transfers between devices, swapped(): lax.ppermute(value, 'seq', [(i, i ^ mask) for i in range(lax.axis_size('s...  16.3 us
    pallas_call x1, Pallas kernels, partial_grads(): call(functools.partial(grad_body, peers, group, min(rows, 512)), 'grads',...  9.75 us
    pallas_call x1, Pallas kernels, later_blocks(): call(functools.partial(later_body, group), 'later', (heads // group,), [c...  8.44 us
    ppermute x3, starting transfers between devices, moved_by(): return lax.ppermute(value, 'seq', pairs)  6.28 us
    pallas_call x1, Pallas kernels, final(): call(functools.partial(final_body, peers, group), 'final', (heads // grou...  6.05 us
    pallas_call x1, Pallas kernels, joined_block(): pl.pallas_call(functools.partial(joined_body, group), name='joined', out_...  5.23 us
    pallas_call x1, Pallas kernels, next_part(): call(functools.partial(next_part_body, group), 'next_part', (heads // gro...  4.91 us
  transfers between devices with their start and end apart: 9, of which 4 were waited for; matrix products, arithmetic and copies ran while one was open for 2% of the time, Pallas kernels for 31%

profile of v2, /device:TPU:0, one launch (start us, length us, event | category | flops | bytes accessed | tf_op | source)
XLA Modules:
  0.0 116.6 jit_solution(2730494805169132211)
XLA Ops:
  0.6 1.2 %slice.9 = bf16[512,768]{1,0:T(8,128)(2,1)S(1)} slice(bf16[1024,1280]{1,0:T(8,128)(2,1)} %q_ref.7), slice={[0:512], [512:1280]} | slice | bytes 1572864 | tf_op jit(solution)/shard_map/slice | solution.py:490
  1.8 1.3 %collective-permute-start = (bf16[512,768]{1,0:T(8,128)(2,1)S(1)}, bf16[512,768]{1,0:T(8,128)(2,1)}, u32[]{:S(2)}, u32[]{:S(2)}) collective-permute-start(bf16[512,768]{1,0:T(8,128)(2,1)S(1)} %slice.9), channel_id=1, source_target_pairs={{4,0},{8,4},{12,8},{5,1},{9,5},{13,9},{6,2},{10,6},{14,10},{7,3},{... | collective-permute-start | bytes 2359304 | tf_op jit(solution)/shard_map/ppermute | solution.py:473
  3.1 9.8 %grads.1 = (f32[10,3,32,128]{3,2,1,0:T(8,128)}, bf16[10,3,32,128]{3,2,1,0:T(8,128)(2,1)}, f32[10,3,32,128]{3,2,1,0:T(8,128)}, bf16[10,3,32,128]{3,2,1,0:T(8,128)(2,1)}) custom-call(s32[1]{0:T(128)} %bitcast.z_ref, bf16[1024,1280]{1,0:T(8,128)(2,1)} %k_ref.9, bf16[1024,1280]{1,0:T(8,128)(2,1)} %v_ref.9, f32[10,1024]{1,0:T(8,128)} %r_ref.1, ...), custom_call_target="tpu_custom_call" | custom-call | flops 2013265920 | bytes 5242880 | tf_op jit(solution)/shard_map/grads/pallas_call | solution.py:107
  12.9 3.7 %collective-permute-start.4 = (bf16[10,3,32,128]{3,2,1,0:T(8,128)(2,1)}, bf16[10,3,32,128]{3,2,1,0:T(8,128)(2,1)}, u32[]{:S(2)}, u32[]{:S(2)}) collective-permute-start(bf16[10,3,32,128]{3,2,1,0:T(8,128)(2,1)} %get-tuple-element.12), channel_id=1, source_target_pairs={{0,4},{4,0},{8,12},{12,8},{1,5},{5,1},{9,13},{13,9},{2,6},{6,2},{1... | collective-permute-start | bytes 737288 | tf_op jit(solution)/shard_map/ppermute | solution.py:477
  16.6 1.3 %slice_bitcast_fusion = (bf16[1,512,512]{2,1,0:T(8,128)(2,1)S(1)}, bf16[1,512,512]{2,1,0:T(8,128)(2,1)S(1)}) fusion(bf16[1024,1280]{1,0:T(8,128)(2,1)} %v_ref.9, bf16[1024,1280]{1,0:T(8,128)(2,1)} %k_ref.9), kind=kLoop, calls=%fused_computation.1 | loop fusion | bytes 2097152 | tf_op jit(solution)/shard_map/stack | solution.py:489
  17.8 0.1 pad_maximum_fusion
  17.9 2.0 %collective-permute-start.2 = (bf16[2,512,512]{2,1,0:T(8,128)(2,1)S(1)}, bf16[2,512,512]{2,1,0:T(8,128)(2,1)S(1)}, u32[]{:S(2)}, u32[]{:S(2)}) collective-permute-start(bf16[2,512,512]{2,1,0:T(8,128)(2,1)S(1)} %pad_maximum_fusion), channel_id=1, source_target_pairs={{0,4},{4,8},{8,12},{1,5},{5,9},{9,13},{2,6},{6,10},{10,14},{3,7},{... | collective-permute-start | bytes 3145736 | tf_op jit(solution)/shard_map/ppermute | solution.py:473
  19.9 0.0 copy-start.2
  19.9 4.5 %collective-permute-start.3 = (bf16[10,3,32,128]{3,2,1,0:T(8,128)(2,1)}, bf16[10,3,32,128]{3,2,1,0:T(8,128)(2,1)}, u32[]{:S(2)}, u32[]{:S(2)}) collective-permute-start(bf16[10,3,32,128]{3,2,1,0:T(8,128)(2,1)} %get-tuple-element.10), channel_id=1, source_target_pairs={{0,4},{4,0},{8,12},{12,8},{1,5},{5,1},{9,13},{13,9},{2,6},{6,2},{1... | collective-permute-start | bytes 737288 | tf_op jit(solution)/shard_map/ppermute | solution.py:477
  24.4 0.9 collective-permute-done.q_ref
  25.3 4.9 %next_part.1 = bf16[6,144,512]{2,1,0:T(8,128)(2,1)} custom-call(bf16[512,768]{1,0:T(8,128)(2,1)} %collective-permute-done.q_ref, bf16[1024,1280]{1,0:T(8,128)(2,1)} %k_ref.9, bf16[1024,1280]{1,0:T(8,128)(2,1)} %v_ref.9), custom_call_target="tpu_custom_call" | custom-call | flops 805306368 | bytes 3145728 | tf_op jit(solution)/shard_map/next_part/pallas_call | solution.py:344
  30.2 3.0 %collective-permute-start.1 = (bf16[6,144,512]{2,1,0:T(8,128)(2,1)}, bf16[6,144,512]{2,1,0:T(8,128)(2,1)S(1)}, u32[]{:S(2)}, u32[]{:S(2)}) collective-permute-start(bf16[6,144,512]{2,1,0:T(8,128)(2,1)} %next_part.1), channel_id=1, source_target_pairs={{0,4},{4,8},{8,12},{1,5},{5,9},{9,13},{2,6},{6,10},{10,14},{3,7},{... | collective-permute-start | bytes 2654216 | tf_op jit(solution)/shard_map/ppermute | solution.py:473
  33.2 1.0 add_convert_fusion
  34.2 2.2 %collective-permute-start.5 = (bf16[10,3,32,128]{3,2,1,0:T(8,128)(2,1)S(1)}, bf16[10,3,32,128]{3,2,1,0:T(8,128)(2,1)S(1)}, u32[]{:S(2)}, u32[]{:S(2)}) collective-permute-start(bf16[10,3,32,128]{3,2,1,0:T(8,128)(2,1)S(1)} %add_convert_fusion), channel_id=1, source_target_pairs={{0,8},{4,12},{8,0},{12,4},{1,9},{5,13},{9,1},{13,5},{2,10},{6,14},... | collective-permute-start | bytes 737288 | tf_op jit(solution)/shard_map/ppermute | solution.py:477
  36.4 14.6 %collective-permute-done.3.refs_1_ = bf16[10,3,32,128]{3,2,1,0:T(8,128)(2,1)} collective-permute-done((bf16[10,3,32,128]{3,2,1,0:T(8,128)(2,1)}, bf16[10,3,32,128]{3,2,1,0:T(8,128)(2,1)}, u32[]{:S(2)}, u32[]{:S(2)}) %collective-permute-start.3) | collective-permute-done | bytes 245792 | tf_op jit(solution)/shard_map/ppermute | solution.py:477
  51.0 23.0 %collective-permute-done.5.refs_2_ = bf16[10,3,32,128]{3,2,1,0:T(8,128)(2,1)S(1)} collective-permute-done((bf16[10,3,32,128]{3,2,1,0:T(8,128)(2,1)S(1)}, bf16[10,3,32,128]{3,2,1,0:T(8,128)(2,1)S(1)}, u32[]{:S(2)}, u32[]{:S(2)}) %collective-permute-start.5) | collective-permute-done | bytes 245792 | tf_op jit(solution)/shard_map/ppermute | solution.py:477
  74.0 0.7 copy-done.5
  74.7 2.6 %update.1 = (bf16[10,3,32,128]{3,2,1,0:T(8,128)(2,1)}, f32[10,3,32,128]{3,2,1,0:T(8,128)}) custom-call(s32[1]{0:T(128)} %bitcast.z_ref, bf16[10,3,128,128]{3,2,1,0:T(8,128)(2,1)} %bitcast.10, f32[10,3,32,128]{3,2,1,0:T(8,128)} %bitcast.11, f32[10,3,32,128]{3,2,1,0:T(8,128)} %get-tuple-element.9.refs_0_, ...), custom_call_target="tpu_custom_call" | custom-call | flops 2457600 | bytes 1966080 | tf_op jit(solution)/shard_map/update/pallas_call | solution.py:146
  77.3 3.4 %collective-permute-start.7 = (bf16[10,3,32,128]{3,2,1,0:T(8,128)(2,1)}, bf16[10,3,32,128]{3,2,1,0:T(8,128)(2,1)S(1)}, u32[]{:S(2)}, u32[]{:S(2)}) collective-permute-start(bf16[10,3,32,128]{3,2,1,0:T(8,128)(2,1)} %get-tuple-element.13.refs_0_), channel_id=1, source_target_pairs={{0,8},{4,12},{8,0},{12,4},{1,9},{5,13},{9,1},{13,5},{2,10},{6,14},... | collective-permute-start | bytes 737288 | tf_op jit(solution)/shard_map/ppermute | solution.py:477
  80.7 1.7 %collective-permute-start.6 = (bf16[10,3,32,128]{3,2,1,0:T(8,128)(2,1)}, bf16[10,3,32,128]{3,2,1,0:T(8,128)(2,1)S(1)}, u32[]{:S(2)}, u32[]{:S(2)}) collective-permute-start(bf16[10,3,32,128]{3,2,1,0:T(8,128)(2,1)} %get-tuple-element.13.refs_0_), channel_id=1, source_target_pairs={{0,4},{4,0},{8,12},{12,8},{1,5},{5,1},{9,13},{13,9},{2,6},{6,2},{1... | collective-permute-start | bytes 737288 | tf_op jit(solution)/shard_map/ppermute | solution.py:477
  82.5 6.2 %collective-permute-done.7.refs_2_ = bf16[10,3,32,128]{3,2,1,0:T(8,128)(2,1)S(1)} collective-permute-done((bf16[10,3,32,128]{3,2,1,0:T(8,128)(2,1)}, bf16[10,3,32,128]{3,2,1,0:T(8,128)(2,1)S(1)}, u32[]{:S(2)}, u32[]{:S(2)}) %collective-permute-start.7) | collective-permute-done | bytes 245792 | tf_op jit(solution)/shard_map/ppermute | solution.py:477
  88.7 0.8 collective-permute-start.8
  89.4 8.4 %later.1.later_ref = bf16[512,1280]{1,0:T(8,128)(2,1)} custom-call(bf16[1024,1280]{1,0:T(8,128)(2,1)} %q_ref.7, bf16[1024,1280]{1,0:T(8,128)(2,1)} %k_ref.9, bf16[1024,1280]{1,0:T(8,128)(2,1)} %v_ref.9), custom_call_target="tpu_custom_call" | custom-call | flops 2013265920 | bytes 10485760 | tf_op jit(solution)/shard_map/later/pallas_call | solution.py:248
  97.9 0.0 collective-permute-done.2.pk_ref.pv_ref
  97.9 0.0 copy-start
  97.9 1.0 copy-done
  98.9 4.8 %carried.1._ = bf16[512,1280]{1,0:T(8,128)(2,1)} custom-call(s32[1]{0:T(128)} %bitcast.z_ref, bf16[1024,1280]{1,0:T(8,128)(2,1)} %q_ref.7, bf16[1024,1280]{1,0:T(8,128)(2,1)} %k_ref.9, bf16[1024,1280]{1,0:T(8,128)(2,1)} %v_ref.9, bf16[2,512,512]{2,1,0:T(8,128)(2,1)} %copy-done, bf16[2,512,512]{2,1,0:T(8,128)(2,1)} %copy-done), custom_call_target="tpu_custom_call" | custom-call | flops 805306368 | bytes 2621440 | tf_op jit(solution)/shard_map/carried/pallas_call | solution.py:289
  103.7 0.9 copy-done.1
  104.6 5.2 %joined.1.first_ref = bf16[512,1280]{1,0:T(8,128)(2,1)} custom-call(s32[1]{0:T(128)} %bitcast.z_ref, bf16[1024,1280]{1,0:T(8,128)(2,1)} %q_ref.7, bf16[1024,1280]{1,0:T(8,128)(2,1)} %k_ref.9, bf16[1024,1280]{1,0:T(8,128)(2,1)} %v_ref.9, bf16[6,144,512]{2,1,0:T(8,128)(2,1)} %copy-done.1, bf16[512,1280]{1,0:T(8,128)(2,1)} %carried.1._), custom_call_target="tpu_custom_call", output_to_operand_aliasing={{}: (5, {})} | custom-call | flops 805306368 | bytes 3932160 | tf_op jit(solution)/shard_map/joined/pallas_call | solution.py:391
  109.8 0.0 collective-permute-done.6.refs_1_
  109.8 0.7 copy-done.4
  110.5 6.0 %final.1 = bf16[1024,1280]{1,0:T(8,128)(2,1)} custom-call(s32[1]{0:T(128)} %bitcast.z_ref, bf16[1024,1280]{1,0:T(8,128)(2,1)} %q_ref.7, bf16[512,1280]{1,0:T(8,128)(2,1)} %joined.1.first_ref, bf16[512,1280]{1,0:T(8,128)(2,1)} %later.1.later_ref, bf16[10,3,32,128]{3,2,1,0:T(8,128)(2,1)} %get-tuple-element.13.refs_0_, bf16[10,3,32,128]{3,2,1,0:T(8,128)(2,1)} %copy-done.4, ...), custom_call_target="tpu_custom_call" | custom-call | flops 1006632960 | bytes 7864320 | tf_op jit(solution)/shard_map/final/pallas_call | solution.py:451
  (9 shorter events, 0.0 us)
Async XLA Ops:
  1.8 23.4 %collective-permute-start = (bf16[512,768]{1,0:T(8,128)(2,1)S(1)}, bf16[512,768]{1,0:T(8,128)(2,1)}, u32[]{:S(2)}, u32[]{:S(2)}) collective-permute-start(bf16[512,768]{1,0:T(8,128)(2,1)S(1)} %slice.9), channel_id=1, source_target_pairs={{4,0},{8,4},{12,8},{5,1},{9,5},{13,9},{6,2},{10,6},{14,10},{7,3},{... | collective-permute-start | bytes 2359304 | tf_op jit(solution)/shard_map/ppermute | solution.py:473
  12.9 20.3 %collective-permute-start.4 = (bf16[10,3,32,128]{3,2,1,0:T(8,128)(2,1)}, bf16[10,3,32,128]{3,2,1,0:T(8,128)(2,1)}, u32[]{:S(2)}, u32[]{:S(2)}) collective-permute-start(bf16[10,3,32,128]{3,2,1,0:T(8,128)(2,1)} %get-tuple-element.12), channel_id=1, source_target_pairs={{0,4},{4,0},{8,12},{12,8},{1,5},{5,1},{9,13},{13,9},{2,6},{6,2},{1... | collective-permute-start | bytes 737288 | tf_op jit(solution)/shard_map/ppermute | solution.py:477
  17.9 80.0 %collective-permute-start.2 = (bf16[2,512,512]{2,1,0:T(8,128)(2,1)S(1)}, bf16[2,512,512]{2,1,0:T(8,128)(2,1)S(1)}, u32[]{:S(2)}, u32[]{:S(2)}) collective-permute-start(bf16[2,512,512]{2,1,0:T(8,128)(2,1)S(1)} %pad_maximum_fusion), channel_id=1, source_target_pairs={{0,4},{4,8},{8,12},{1,5},{5,9},{9,13},{2,6},{6,10},{10,14},{3,7},{... | collective-permute-start | bytes 3145736 | tf_op jit(solution)/shard_map/ppermute | solution.py:473
  19.9 13.3 %copy-start.2 = (f32[10,3,32,128]{3,2,1,0:T(8,128)S(1)}, f32[10,3,32,128]{3,2,1,0:T(8,128)}, u32[]{:S(2)}) copy-start(f32[10,3,32,128]{3,2,1,0:T(8,128)} %get-tuple-element.11) | copy-start | bytes 1474564
  19.9 31.0 %collective-permute-start.3 = (bf16[10,3,32,128]{3,2,1,0:T(8,128)(2,1)}, bf16[10,3,32,128]{3,2,1,0:T(8,128)(2,1)}, u32[]{:S(2)}, u32[]{:S(2)}) collective-permute-start(bf16[10,3,32,128]{3,2,1,0:T(8,128)(2,1)} %get-tuple-element.10), channel_id=1, source_target_pairs={{0,4},{4,0},{8,12},{12,8},{1,5},{5,1},{9,13},{13,9},{2,6},{6,2},{1... | collective-permute-start | bytes 737288 | tf_op jit(solution)/shard_map/ppermute | solution.py:477
  30.2 73.5 %collective-permute-start.1 = (bf16[6,144,512]{2,1,0:T(8,128)(2,1)}, bf16[6,144,512]{2,1,0:T(8,128)(2,1)S(1)}, u32[]{:S(2)}, u32[]{:S(2)}) collective-permute-start(bf16[6,144,512]{2,1,0:T(8,128)(2,1)} %next_part.1), channel_id=1, source_target_pairs={{0,4},{4,8},{8,12},{1,5},{5,9},{9,13},{2,6},{6,10},{10,14},{3,7},{... | collective-permute-start | bytes 2654216 | tf_op jit(solution)/shard_map/ppermute | solution.py:473
  34.2 39.8 %collective-permute-start.5 = (bf16[10,3,32,128]{3,2,1,0:T(8,128)(2,1)S(1)}, bf16[10,3,32,128]{3,2,1,0:T(8,128)(2,1)S(1)}, u32[]{:S(2)}, u32[]{:S(2)}) collective-permute-start(bf16[10,3,32,128]{3,2,1,0:T(8,128)(2,1)S(1)} %add_convert_fusion), channel_id=1, source_target_pairs={{0,8},{4,12},{8,0},{12,4},{1,9},{5,13},{9,1},{13,5},{2,10},{6,14},... | collective-permute-start | bytes 737288 | tf_op jit(solution)/shard_map/ppermute | solution.py:477
  74.0 0.7 copy-start.5
  77.3 11.4 %collective-permute-start.7 = (bf16[10,3,32,128]{3,2,1,0:T(8,128)(2,1)}, bf16[10,3,32,128]{3,2,1,0:T(8,128)(2,1)S(1)}, u32[]{:S(2)}, u32[]{:S(2)}) collective-permute-start(bf16[10,3,32,128]{3,2,1,0:T(8,128)(2,1)} %get-tuple-element.13.refs_0_), channel_id=1, source_target_pairs={{0,8},{4,12},{8,0},{12,4},{1,9},{5,13},{9,1},{13,5},{2,10},{6,14},... | collective-permute-start | bytes 737288 | tf_op jit(solution)/shard_map/ppermute | solution.py:477
  80.7 29.1 %collective-permute-start.6 = (bf16[10,3,32,128]{3,2,1,0:T(8,128)(2,1)}, bf16[10,3,32,128]{3,2,1,0:T(8,128)(2,1)S(1)}, u32[]{:S(2)}, u32[]{:S(2)}) collective-permute-start(bf16[10,3,32,128]{3,2,1,0:T(8,128)(2,1)} %get-tuple-element.13.refs_0_), channel_id=1, source_target_pairs={{0,4},{4,0},{8,12},{12,8},{1,5},{5,1},{9,13},{13,9},{2,6},{6,2},{1... | collective-permute-start | bytes 737288 | tf_op jit(solution)/shard_map/ppermute | solution.py:477
  88.7 9.2 %copy-start.3 = (bf16[10,3,32,128]{3,2,1,0:T(8,128)(2,1)}, bf16[10,3,32,128]{3,2,1,0:T(8,128)(2,1)S(1)}, u32[]{:S(2)}) copy-start(bf16[10,3,32,128]{3,2,1,0:T(8,128)(2,1)S(1)} %collective-permute-done.7.refs_2_) | copy-start | bytes 737284
  88.7 21.1 %collective-permute-start.8 = (bf16[10,3,32,128]{3,2,1,0:T(8,128)(2,1)S(1)}, bf16[10,3,32,128]{3,2,1,0:T(8,128)(2,1)}, u32[]{:S(2)}, u32[]{:S(2)}) collective-permute-start(bf16[10,3,32,128]{3,2,1,0:T(8,128)(2,1)S(1)} %collective-permute-done.7.refs_2_), channel_id=1, source_target_pairs={{0,4},{4,0},{8,12},{12,8},{1,5},{5,1},{9,13},{13,9},{2,6},{6,2},{1... | collective-permute-start | bytes 737288 | tf_op jit(solution)/shard_map/ppermute | solution.py:477
  97.9 1.0 copy-start
  103.7 0.9 copy-start.1
  109.8 0.7 copy-start.4

commit v3 on v2

--- a/solution.py
+++ b/solution.py
@@ -8,6 +8,7 @@
 from jax.experimental.pallas import tpu as pltpu
 from jax.sharding import PartitionSpec as P
 
+
 WIN = 512
 TILE = 256
 
@@ -15,13 +16,13 @@
 epsilon = 1e-06
 MASKED = -1e30
 LOG2E = math.log2(math.e)
+VMEM = pl.BlockSpec(memory_space=pltpu.VMEM)
 NT = (((1,), (1,)), ((), ()))
 
 
-def call(body, name, grid, in_specs, out_specs, out_shape, scratch=(), prefetch=0, flops=0, nbytes=0):
+def call(body, grid, in_specs, out_specs, out_shape, scratch=(), prefetch=0, flops=0, nbytes=0):
     return pl.pallas_call(
         body,
-        name=name,
         out_shape=out_shape,
         grid_spec=pltpu.PrefetchScalarGridSpec(
             num_scalar_prefetch=prefetch,
@@ -106,7 +107,6 @@
     column = pl.BlockSpec((rows, group * size), lambda h, z: (0, h))
     return call(
         functools.partial(grad_body, peers, group, min(rows, 512)),
-        "grads",
         (heads // group,),
         [
             column,
@@ -145,10 +145,9 @@
     count = momentum.size
     return call(
         functools.partial(update_body, len(terms)),
-        "update",
         (1,),
-        [pl.BlockSpec(shape, lambda i, z: (0, 0, z[0], 0)), whole] + [whole] * len(terms),
-        [whole, whole],
+        [pl.BlockSpec(shape, lambda i, z: (0, 0, z[0], 0)), whole] + [VMEM] * len(terms),
+        [VMEM, whole],
         [jax.ShapeDtypeStruct(shape, jnp.bfloat16), jax.ShapeDtypeStruct(shape, jnp.float32)],
         (),
         1,
@@ -221,7 +220,8 @@
 SCORES = (WIN // TILE + 1) * TILE
 
 
-def later_body(group, q_ref, k_ref, v_ref, o_ref, s_ref):
+def later_body(group, q_ref, k_ref, v_ref, *refs):
+    o_ref, s_ref = refs[-2:]
     size = q_ref.shape[1] // group
     causal, late = masks()
     depth = WIN // TILE
@@ -242,24 +242,31 @@
     attend(tasks, s_ref)
 
 
-def later_blocks(queries, keys, values, heads, size, first, group):
-    rows = queries.shape[0]
-    column = pl.BlockSpec((rows, group * size), lambda h: (0, first // group + h))
-    return call(
+def later_blocks(queries, keys, values, size, step, group, partly):
+    rows, width = queries.shape
+    column = pl.BlockSpec((rows, group * size), lambda h: (0, step))
+    more = [] if partly is None else [partly]
+    return pl.pallas_call(
         functools.partial(later_body, group),
-        "later",
-        (heads // group,),
-        [column] * 3,
-        pl.BlockSpec((rows - WIN, group * size), lambda h: (0, h)),
-        jax.ShapeDtypeStruct((rows - WIN, heads * size), jnp.bfloat16),
-        [pltpu.VMEM((2, SCORES, TILE), jnp.float32)],
-        0,
-        6 * (rows - WIN) * WIN * size * heads,
-        8 * rows * size * heads,
-    )(queries, keys, values)
-
-
-def carried_body(group, z_ref, q_ref, k_ref, v_ref, pk_ref, pv_ref, o_ref, s_ref):
+        name="later",
+        out_shape=jax.ShapeDtypeStruct((rows - WIN, width), jnp.bfloat16),
+        grid_spec=pltpu.PrefetchScalarGridSpec(
+            num_scalar_prefetch=0,
+            grid=(1,),
+            in_specs=[column] * 3 + [pl.BlockSpec(memory_space=pl.ANY)] * len(more),
+            out_specs=pl.BlockSpec((rows - WIN, group * size), lambda h: (0, step)),
+            scratch_shapes=[pltpu.VMEM((2, SCORES, TILE), jnp.float32)],
+        ),
+        input_output_aliases={3: 0} if more else {},
+        cost_estimate=pl.CostEstimate(
+            flops=6 * (rows - WIN) * WIN * size * group,
+            bytes_accessed=8 * rows * size * group,
+            transcendentals=0,
+        ),
+    )(queries, keys, values, *more)
+
+
+def carried_body(group, z_ref, q_ref, k_ref, v_ref, p_ref, o_ref, s_ref):
     size = q_ref.shape[1] // group
     causal, late = masks()
     depth = WIN // TILE
@@ -270,7 +277,7 @@
         memo = {}
         for t in range(depth):
             found = [
-                (spans(pk_ref, j, cols), turned(memo, pv_ref, j, cols, 1), late & there if j == t else there)
+                (spans(p_ref.at[0], j, cols), turned(memo, p_ref.at[1], j, cols, 1), late & there if j == t else there)
                 for j in range(t, depth)
             ]
             found += [
@@ -283,22 +290,20 @@
 
 def carried_block(z, queries, keys, values, carried, size):
     heads = carried.shape[2] // size
-    group = steps_of(heads, 4)
+    group = heads
     width = queries.shape[1]
     column = pl.BlockSpec((WIN, group * size), lambda h, z: (0, h))
     return call(
         functools.partial(carried_body, group),
-        "carried",
         (heads // group,),
-        [column] * 3
-        + [pl.BlockSpec((None, WIN, group * size), lambda h, z, c=c: (c, 0, h)) for c in range(2)],
+        [column] * 3 + [VMEM],
         column,
         jax.ShapeDtypeStruct((WIN, width), jnp.bfloat16),
         [pltpu.VMEM((2, SCORES, TILE), jnp.float32)],
         1,
         6 * WIN * WIN * size * heads,
         10 * WIN * size * heads,
-    )(z, queries, keys, values, carried, carried)
+    )(z, queries, keys, values, carried)
 
 
 EXTRA = 16
@@ -343,7 +348,6 @@
     column = pl.BlockSpec((WIN, group * size), lambda h: (block, h + first // group))
     return call(
         functools.partial(next_part_body, group),
-        "next_part",
         (heads // group,),
         [pl.BlockSpec((WIN, group * size), lambda h: (0, h)), column, column],
         pl.BlockSpec((group, size + EXTRA, WIN), lambda h: (h, 0, 0)),
@@ -359,14 +363,15 @@
     size = q_ref.shape[1] // group
     causal, _ = masks()
     depth = WIN // TILE
+    step = pl.program_id(0) * group
 
     def join(g, t, cols):
         def emit(out, level):
             span = slice(t * TILE, (t + 1) * TILE)
-            terms = p_ref[g, size:, span].astype(jnp.float32)
+            terms = p_ref[step + g, size:, span].astype(jnp.float32)
             other = terms[0:1] + (terms[1:2] + terms[2:3])
             share = jnp.where(z_ref[0] > 0, jax.nn.sigmoid(other - level), 0.0)
-            out = out + share * (p_ref[g, :size, span].astype(jnp.float32) - out)
+            out = out + share * (p_ref[step + g, :size, span].astype(jnp.float32) - out)
             o_ref[span, cols] = jnp.transpose(out).astype(o_ref.dtype)
 
         return emit
@@ -399,7 +404,7 @@
                 column,
                 column,
                 column,
-                pl.BlockSpec((group, size + EXTRA, WIN), lambda h, z: (h, 0, 0)),
+                VMEM,
                 pl.BlockSpec(memory_space=pl.ANY),
             ],
             out_specs=column,
@@ -416,9 +421,10 @@
     blocks, o_ref, whole = refs[:peers], refs[peers], refs[peers + 1]
     size = q_ref.shape[1] // group
     own = blocks[0].shape[2]
+    start = pl.program_id(0) * group
     for m in range(peers):
         row = pl.multiple_of((z_ref[0] ^ m) * own, own)
-        whole[:, :, pl.ds(row, own), :] = blocks[m][...].astype(whole.dtype)
+        whole[:, :, pl.ds(row, own), :] = blocks[m][pl.ds(start, group)].astype(whole.dtype)
     tasks = [(g, c) for g in range(group) for c in range(0, q_ref.shape[0], WIN)]
 
     def products(g, c):
@@ -450,14 +456,13 @@
     kind = jnp.bfloat16 if own % 16 == 0 else jnp.float32
     return call(
         functools.partial(final_body, peers, group),
-        "final",
         (heads // group,),
         [
             column,
             pl.BlockSpec((WIN, group * size), lambda h, z: (0, h)),
             pl.BlockSpec((rows - WIN, group * size), lambda h, z: (0, h)),
         ]
-        + [pl.BlockSpec((group, 3, own, size), lambda h, z: (h, 0, 0, 0))] * peers,
+        + [VMEM] * peers,
         column,
         jax.ShapeDtypeStruct((rows, width), jnp.bfloat16),
         [pltpu.VMEM((group, 3, size, size), kind)],
@@ -477,17 +482,21 @@
     return lax.ppermute(value, "seq", [(i, i ^ mask) for i in range(lax.axis_size("seq"))])
 
 
+def kept_of(heads):
+    return max(1, heads * 4 // 10)
+
+
 def shards(queries, keys, values, rates, fast_weights, momentum):
     rows = queries.shape[0]
     heads = rates.shape[0]
     size = fast_weights.shape[0]
     peers = lax.axis_size("seq")
-    kept = heads * 2 // 5
+    kept = kept_of(heads)
     z = lax.axis_index("seq").astype(jnp.int32).reshape(1)
     cut = kept * size
 
+    asked = moved_by(queries[:WIN, cut:], -1)
     carried = moved_by(jnp.stack([keys[rows - WIN :, :cut], values[rows - WIN :, :cut]]), 1)
-    asked = moved_by(queries[:WIN, cut:], -1)
 
     weights = jnp.transpose(fast_weights, (1, 2, 0, 3))
     own_momentum = jnp.transpose(momentum, (1, 2, 0, 3))
@@ -503,8 +512,12 @@
                 sums[m - step].append(swapped(block.astype(jnp.bfloat16), step))
         step *= 2
 
-    later = later_blocks(queries, keys, values, heads, size, 0, steps_of(heads))
-    given = moved_by(next_part(asked, keys, values, kept, size), 1)
+    group = steps_of(heads)
+    later = None
+    for part in range(heads // group):
+        later = later_blocks(queries, keys, values, size, part, group, later)
+    given = next_part(asked, keys, values, kept, size)
+    given = moved_by(given, 1)
     first = carried_block(z, queries, keys, values, carried, size)
     first = joined_block(z, queries, keys, values, given, first, kept, size)
 

time: 117 us -> 121 us (1.034)
  Pallas kernels: 41.8 us -> 45.3 us
    pallas_call x6 -> x7, Pallas kernels: 36.5 us -> 39.8 us  [the longest x2 11.3 us: later_blocks(): pl.pallas_call(functools.partial(later_body, group), name='later', out_sh...]
  transfers between devices with their start and end apart: 9 -> 9, of which waited for: 4 -> 4; matrix products, arithmetic and copies ran while one was open for 2% -> 2% of each run, Pallas kernels for 31% -> 32%
where the time goes in v3:
time: 121 us; the launch traced here: 120 us
  Pallas kernels  45.3 us (37%)
  waiting for transfers between devices  44.7 us (37%)
  starting transfers between devices  22.5 us (19%)
  local copies, waits for them, and re-layouts  5.75 us (5%)
    ppermute x6, waiting for transfers between devices, swapped(): lax.ppermute(value, 'seq', [(i, i ^ mask) for i in range(lax.axis_size('s...  43.8 us
    ppermute x6, starting transfers between devices, swapped(): lax.ppermute(value, 'seq', [(i, i ^ mask) for i in range(lax.axis_size('s...  16.3 us
    pallas_call x2, Pallas kernels, later_blocks(): pl.pallas_call(functools.partial(later_body, group), name='later', out_sh...  11.3 us
    pallas_call x1, Pallas kernels, partial_grads(): call(functools.partial(grad_body, peers, group, min(rows, 512)), (heads /...  9.75 us
    pallas_call x1, Pallas kernels, final(): call(functools.partial(final_body, peers, group), (heads // group,), [col...  6.4 us
    ppermute x3, starting transfers between devices, moved_by(): return lax.ppermute(value, 'seq', pairs)  6.28 us
    pallas_call x1, Pallas kernels, joined_block(): pl.pallas_call(functools.partial(joined_body, group), name='joined', out_...  5.49 us
    pallas_call x1, Pallas kernels, next_part(): call(functools.partial(next_part_body, group), (heads // group,), [pl.Blo...  4.91 us
  transfers between devices with their start and end apart: 9, of which 4 were waited for; matrix products, arithmetic and copies ran while one was open for 2% of the time, Pallas kernels for 32%

profile of v3, /device:TPU:0, one launch (start us, length us, event | category | flops | bytes accessed | tf_op | source)
XLA Modules:
  0.0 120.1 jit_solution(10156134610968840759)
XLA Ops:
  0.6 1.2 slice.9
  1.8 1.3 %collective-permute-start = (bf16[512,768]{1,0:T(8,128)(2,1)S(1)}, bf16[512,768]{1,0:T(8,128)(2,1)}, u32[]{:S(2)}, u32[]{:S(2)}) collective-permute-start(bf16[512,768]{1,0:T(8,128)(2,1)S(1)} %slice.9), channel_id=1, source_target_pairs={{4,0},{8,4},{12,8},{5,1},{9,5},{13,9},{6,2},{10,6},{14,10},{7,3},{... | collective-permute-start | bytes 2359304 | tf_op jit(solution)/shard_map/ppermute | solution.py:478
  3.1 9.8 %shard_map.87 = (f32[10,3,32,128]{3,2,1,0:T(8,128)}, bf16[10,3,32,128]{3,2,1,0:T(8,128)(2,1)}, f32[10,3,32,128]{3,2,1,0:T(8,128)}, bf16[10,3,32,128]{3,2,1,0:T(8,128)(2,1)}) custom-call(s32[1]{0:T(128)} %bitcast.z_ref, bf16[1024,1280]{1,0:T(8,128)(2,1)} %k_ref.11, bf16[1024,1280]{1,0:T(8,128)(2,1)} %v_ref.11, f32[10,1024]{1,0:T(8,128)} %r_ref.1, ...), custom_call_target="tpu_custom_call" | custom-call | flops 2013265920 | bytes 5242880 | tf_op jit(solution)/shard_map/pallas_call | solution.py:108
  12.9 3.7 %collective-permute-start.4 = (bf16[10,3,32,128]{3,2,1,0:T(8,128)(2,1)}, bf16[10,3,32,128]{3,2,1,0:T(8,128)(2,1)}, u32[]{:S(2)}, u32[]{:S(2)}) collective-permute-start(bf16[10,3,32,128]{3,2,1,0:T(8,128)(2,1)} %get-tuple-element.12), channel_id=1, source_target_pairs={{0,4},{4,0},{8,12},{12,8},{1,5},{5,1},{9,13},{13,9},{2,6},{6,2},{1... | collective-permute-start | bytes 737288 | tf_op jit(solution)/shard_map/ppermute | solution.py:482
  16.6 1.3 %slice_bitcast_fusion = (bf16[1,512,512]{2,1,0:T(8,128)(2,1)S(1)}, bf16[1,512,512]{2,1,0:T(8,128)(2,1)S(1)}) fusion(bf16[1024,1280]{1,0:T(8,128)(2,1)} %v_ref.11, bf16[1024,1280]{1,0:T(8,128)(2,1)} %k_ref.11), kind=kLoop, calls=%fused_computation.1 | loop fusion | bytes 2097152 | tf_op jit(solution)/shard_map/stack | solution.py:499
  17.8 0.1 pad_maximum_fusion
  17.9 2.0 %collective-permute-start.2 = (bf16[2,512,512]{2,1,0:T(8,128)(2,1)S(1)}, bf16[2,512,512]{2,1,0:T(8,128)(2,1)S(1)}, u32[]{:S(2)}, u32[]{:S(2)}) collective-permute-start(bf16[2,512,512]{2,1,0:T(8,128)(2,1)S(1)} %pad_maximum_fusion), channel_id=1, source_target_pairs={{0,4},{4,8},{8,12},{1,5},{5,9},{9,13},{2,6},{6,10},{10,14},{3,7},{... | collective-permute-start | bytes 3145736 | tf_op jit(solution)/shard_map/ppermute | solution.py:478
  19.9 0.0 copy-start.2
  19.9 4.5 %collective-permute-start.3 = (bf16[10,3,32,128]{3,2,1,0:T(8,128)(2,1)}, bf16[10,3,32,128]{3,2,1,0:T(8,128)(2,1)}, u32[]{:S(2)}, u32[]{:S(2)}) collective-permute-start(bf16[10,3,32,128]{3,2,1,0:T(8,128)(2,1)} %get-tuple-element.10), channel_id=1, source_target_pairs={{0,4},{4,0},{8,12},{12,8},{1,5},{5,1},{9,13},{13,9},{2,6},{6,2},{1... | collective-permute-start | bytes 737288 | tf_op jit(solution)/shard_map/ppermute | solution.py:482
  24.4 0.9 collective-permute-done.q_ref
  25.3 4.9 %shard_map.85 = bf16[6,144,512]{2,1,0:T(8,128)(2,1)} custom-call(bf16[512,768]{1,0:T(8,128)(2,1)} %collective-permute-done.q_ref, bf16[1024,1280]{1,0:T(8,128)(2,1)} %k_ref.11, bf16[1024,1280]{1,0:T(8,128)(2,1)} %v_ref.11), custom_call_target="tpu_custom_call" | custom-call | flops 805306368 | bytes 3145728 | tf_op jit(solution)/shard_map/pallas_call | solution.py:349
  30.2 3.0 %collective-permute-start.1 = (bf16[6,144,512]{2,1,0:T(8,128)(2,1)}, bf16[6,144,512]{2,1,0:T(8,128)(2,1)S(1)}, u32[]{:S(2)}, u32[]{:S(2)}) collective-permute-start(bf16[6,144,512]{2,1,0:T(8,128)(2,1)} %shard_map.85), channel_id=1, source_target_pairs={{0,4},{4,8},{8,12},{1,5},{5,9},{9,13},{2,6},{6,10},{10,14},{3,7},{... | collective-permute-start | bytes 2654216 | tf_op jit(solution)/shard_map/ppermute | solution.py:478
  33.2 1.0 add_convert_fusion
  34.2 2.2 %collective-permute-start.5 = (bf16[10,3,32,128]{3,2,1,0:T(8,128)(2,1)S(1)}, bf16[10,3,32,128]{3,2,1,0:T(8,128)(2,1)S(1)}, u32[]{:S(2)}, u32[]{:S(2)}) collective-permute-start(bf16[10,3,32,128]{3,2,1,0:T(8,128)(2,1)S(1)} %add_convert_fusion), channel_id=1, source_target_pairs={{0,8},{4,12},{8,0},{12,4},{1,9},{5,13},{9,1},{13,5},{2,10},{6,14},... | collective-permute-start | bytes 737288 | tf_op jit(solution)/shard_map/ppermute | solution.py:482
  36.4 14.6 %collective-permute-done.3.refs_1_ = bf16[10,3,32,128]{3,2,1,0:T(8,128)(2,1)} collective-permute-done((bf16[10,3,32,128]{3,2,1,0:T(8,128)(2,1)}, bf16[10,3,32,128]{3,2,1,0:T(8,128)(2,1)}, u32[]{:S(2)}, u32[]{:S(2)}) %collective-permute-start.3) | collective-permute-done | bytes 245792 | tf_op jit(solution)/shard_map/ppermute | solution.py:482
  51.0 23.0 %collective-permute-done.5.refs_2_ = bf16[10,3,32,128]{3,2,1,0:T(8,128)(2,1)S(1)} collective-permute-done((bf16[10,3,32,128]{3,2,1,0:T(8,128)(2,1)S(1)}, bf16[10,3,32,128]{3,2,1,0:T(8,128)(2,1)S(1)}, u32[]{:S(2)}, u32[]{:S(2)}) %collective-permute-start.5) | collective-permute-done | bytes 245792 | tf_op jit(solution)/shard_map/ppermute | solution.py:482
  74.0 0.7 copy-done.5
  74.7 2.6 %shard_map.88 = (bf16[10,3,32,128]{3,2,1,0:T(8,128)(2,1)}, f32[10,3,32,128]{3,2,1,0:T(8,128)}) custom-call(s32[1]{0:T(128)} %bitcast.z_ref, bf16[10,3,128,128]{3,2,1,0:T(8,128)(2,1)} %bitcast.10, f32[10,3,32,128]{3,2,1,0:T(8,128)} %bitcast.11, f32[10,3,32,128]{3,2,1,0:T(8,128)} %get-tuple-element.9.refs_0_, ...), custom_call_target="tpu_custom_call" | custom-call | flops 2457600 | bytes 1966080 | tf_op jit(solution)/shard_map/pallas_call | solution.py:146
  77.3 3.4 %collective-permute-start.7 = (bf16[10,3,32,128]{3,2,1,0:T(8,128)(2,1)}, bf16[10,3,32,128]{3,2,1,0:T(8,128)(2,1)S(1)}, u32[]{:S(2)}, u32[]{:S(2)}) collective-permute-start(bf16[10,3,32,128]{3,2,1,0:T(8,128)(2,1)} %get-tuple-element.13.refs_0_), channel_id=1, source_target_pairs={{0,8},{4,12},{8,0},{12,4},{1,9},{5,13},{9,1},{13,5},{2,10},{6,14},... | collective-permute-start | bytes 737288 | tf_op jit(solution)/shard_map/ppermute | solution.py:482
  80.7 1.7 %collective-permute-start.6 = (bf16[10,3,32,128]{3,2,1,0:T(8,128)(2,1)}, bf16[10,3,32,128]{3,2,1,0:T(8,128)(2,1)S(1)}, u32[]{:S(2)}, u32[]{:S(2)}) collective-permute-start(bf16[10,3,32,128]{3,2,1,0:T(8,128)(2,1)} %get-tuple-element.13.refs_0_), channel_id=1, source_target_pairs={{0,4},{4,0},{8,12},{12,8},{1,5},{5,1},{9,13},{13,9},{2,6},{6,2},{1... | collective-permute-start | bytes 737288 | tf_op jit(solution)/shard_map/ppermute | solution.py:482
  82.5 6.2 %collective-permute-done.7.refs_2_ = bf16[10,3,32,128]{3,2,1,0:T(8,128)(2,1)S(1)} collective-permute-done((bf16[10,3,32,128]{3,2,1,0:T(8,128)(2,1)}, bf16[10,3,32,128]{3,2,1,0:T(8,128)(2,1)S(1)}, u32[]{:S(2)}, u32[]{:S(2)}) %collective-permute-start.7) | collective-permute-done | bytes 245792 | tf_op jit(solution)/shard_map/ppermute | solution.py:482
  88.7 0.8 collective-permute-start.8
  89.4 5.7 %later.2.refs_0_ = bf16[512,1280]{1,0:T(8,128)(2,1)} custom-call(bf16[1024,1280]{1,0:T(8,128)(2,1)} %q_ref.9, bf16[1024,1280]{1,0:T(8,128)(2,1)} %k_ref.11, bf16[1024,1280]{1,0:T(8,128)(2,1)} %v_ref.11), custom_call_target="tpu_custom_call" | custom-call | flops 1006632960 | bytes 5242880 | tf_op jit(solution)/shard_map/later/pallas_call | solution.py:249
  95.1 5.7 %later.3.later_ref = bf16[512,1280]{1,0:T(8,128)(2,1)} custom-call(bf16[1024,1280]{1,0:T(8,128)(2,1)} %q_ref.9, bf16[1024,1280]{1,0:T(8,128)(2,1)} %k_ref.11, bf16[1024,1280]{1,0:T(8,128)(2,1)} %v_ref.11, bf16[512,1280]{1,0:T(8,128)(2,1)} %later.2.refs_0_), custom_call_target="tpu_custom_call", output_to_operand_aliasing={{}: (3, {})} | custom-call | flops 1006632960 | bytes 5242880 | tf_op jit(solution)/shard_map/later/pallas_call | solution.py:249
  100.8 0.0 collective-permute-done.2.p_ref
  100.8 1.0 copy-done
  101.8 4.8 %shard_map.86._ = bf16[512,1280]{1,0:T(8,128)(2,1)} custom-call(s32[1]{0:T(128)} %bitcast.z_ref, bf16[1024,1280]{1,0:T(8,128)(2,1)} %q_ref.9, bf16[1024,1280]{1,0:T(8,128)(2,1)} %k_ref.11, bf16[1024,1280]{1,0:T(8,128)(2,1)} %v_ref.11, bf16[2,512,512]{2,1,0:T(8,128)(2,1)} %copy-done), custom_call_target="tpu_custom_call" | custom-call | flops 805306368 | bytes 2621440 | tf_op jit(solution)/shard_map/pallas_call | solution.py:296
  106.5 0.0 collective-permute-done.1.p_ref
  106.6 0.9 copy-done.1
  107.5 5.5 %joined.1.first_ref = bf16[512,1280]{1,0:T(8,128)(2,1)} custom-call(s32[1]{0:T(128)} %bitcast.z_ref, bf16[1024,1280]{1,0:T(8,128)(2,1)} %q_ref.9, bf16[1024,1280]{1,0:T(8,128)(2,1)} %k_ref.11, bf16[1024,1280]{1,0:T(8,128)(2,1)} %v_ref.11, bf16[6,144,512]{2,1,0:T(8,128)(2,1)} %copy-done.1, bf16[512,1280]{1,0:T(8,128)(2,1)} %shard_map.86._), custom_call_target="tpu_custom_call", output_to_operand_aliasing={{}: (5, {})} | custom-call | flops 805306368 | bytes 3932160 | tf_op jit(solution)/shard_map/joined/pallas_call | solution.py:396
  113.0 0.7 copy-done.4
  113.7 6.4 %shard_map.89 = bf16[1024,1280]{1,0:T(8,128)(2,1)} custom-call(s32[1]{0:T(128)} %bitcast.z_ref, bf16[1024,1280]{1,0:T(8,128)(2,1)} %q_ref.9, bf16[512,1280]{1,0:T(8,128)(2,1)} %joined.1.first_ref, bf16[512,1280]{1,0:T(8,128)(2,1)} %later.3.later_ref, bf16[10,3,32,128]{3,2,1,0:T(8,128)(2,1)} %get-tuple-element.13.refs_0_, bf16[10,3,32,128]{3,2,1,0:T(8,128)(2,1)} %copy-done.4, ...), custom_call_target="tpu_custom_call" | custom-call | flops 1006632960 | bytes 7864320 | tf_op jit(solution)/shard_map/pallas_call | solution.py:457
  (10 shorter events, 0.0 us)
Async XLA Ops:
  1.8 23.4 %collective-permute-start = (bf16[512,768]{1,0:T(8,128)(2,1)S(1)}, bf16[512,768]{1,0:T(8,128)(2,1)}, u32[]{:S(2)}, u32[]{:S(2)}) collective-permute-start(bf16[512,768]{1,0:T(8,128)(2,1)S(1)} %slice.9), channel_id=1, source_target_pairs={{4,0},{8,4},{12,8},{5,1},{9,5},{13,9},{6,2},{10,6},{14,10},{7,3},{... | collective-permute-start | bytes 2359304 | tf_op jit(solution)/shard_map/ppermute | solution.py:478
  12.9 20.3 %collective-permute-start.4 = (bf16[10,3,32,128]{3,2,1,0:T(8,128)(2,1)}, bf16[10,3,32,128]{3,2,1,0:T(8,128)(2,1)}, u32[]{:S(2)}, u32[]{:S(2)}) collective-permute-start(bf16[10,3,32,128]{3,2,1,0:T(8,128)(2,1)} %get-tuple-element.12), channel_id=1, source_target_pairs={{0,4},{4,0},{8,12},{12,8},{1,5},{5,1},{9,13},{13,9},{2,6},{6,2},{1... | collective-permute-start | bytes 737288 | tf_op jit(solution)/shard_map/ppermute | solution.py:482
  17.9 82.9 %collective-permute-start.2 = (bf16[2,512,512]{2,1,0:T(8,128)(2,1)S(1)}, bf16[2,512,512]{2,1,0:T(8,128)(2,1)S(1)}, u32[]{:S(2)}, u32[]{:S(2)}) collective-permute-start(bf16[2,512,512]{2,1,0:T(8,128)(2,1)S(1)} %pad_maximum_fusion), channel_id=1, source_target_pairs={{0,4},{4,8},{8,12},{1,5},{5,9},{9,13},{2,6},{6,10},{10,14},{3,7},{... | collective-permute-start | bytes 3145736 | tf_op jit(solution)/shard_map/ppermute | solution.py:478
  19.9 13.3 %copy-start.2 = (f32[10,3,32,128]{3,2,1,0:T(8,128)S(1)}, f32[10,3,32,128]{3,2,1,0:T(8,128)}, u32[]{:S(2)}) copy-start(f32[10,3,32,128]{3,2,1,0:T(8,128)} %get-tuple-element.11) | copy-start | bytes 1474564
  19.9 31.0 %collective-permute-start.3 = (bf16[10,3,32,128]{3,2,1,0:T(8,128)(2,1)}, bf16[10,3,32,128]{3,2,1,0:T(8,128)(2,1)}, u32[]{:S(2)}, u32[]{:S(2)}) collective-permute-start(bf16[10,3,32,128]{3,2,1,0:T(8,128)(2,1)} %get-tuple-element.10), channel_id=1, source_target_pairs={{0,4},{4,0},{8,12},{12,8},{1,5},{5,1},{9,13},{13,9},{2,6},{6,2},{1... | collective-permute-start | bytes 737288 | tf_op jit(solution)/shard_map/ppermute | solution.py:482
  30.2 76.4 %collective-permute-start.1 = (bf16[6,144,512]{2,1,0:T(8,128)(2,1)}, bf16[6,144,512]{2,1,0:T(8,128)(2,1)S(1)}, u32[]{:S(2)}, u32[]{:S(2)}) collective-permute-start(bf16[6,144,512]{2,1,0:T(8,128)(2,1)} %shard_map.85), channel_id=1, source_target_pairs={{0,4},{4,8},{8,12},{1,5},{5,9},{9,13},{2,6},{6,10},{10,14},{3,7},{... | collective-permute-start | bytes 2654216 | tf_op jit(solution)/shard_map/ppermute | solution.py:478
  34.2 39.8 %collective-permute-start.5 = (bf16[10,3,32,128]{3,2,1,0:T(8,128)(2,1)S(1)}, bf16[10,3,32,128]{3,2,1,0:T(8,128)(2,1)S(1)}, u32[]{:S(2)}, u32[]{:S(2)}) collective-permute-start(bf16[10,3,32,128]{3,2,1,0:T(8,128)(2,1)S(1)} %add_convert_fusion), channel_id=1, source_target_pairs={{0,8},{4,12},{8,0},{12,4},{1,9},{5,13},{9,1},{13,5},{2,10},{6,14},... | collective-permute-start | bytes 737288 | tf_op jit(solution)/shard_map/ppermute | solution.py:482
  74.0 0.7 copy-start.5
  77.3 11.4 %collective-permute-start.7 = (bf16[10,3,32,128]{3,2,1,0:T(8,128)(2,1)}, bf16[10,3,32,128]{3,2,1,0:T(8,128)(2,1)S(1)}, u32[]{:S(2)}, u32[]{:S(2)}) collective-permute-start(bf16[10,3,32,128]{3,2,1,0:T(8,128)(2,1)} %get-tuple-element.13.refs_0_), channel_id=1, source_target_pairs={{0,8},{4,12},{8,0},{12,4},{1,9},{5,13},{9,1},{13,5},{2,10},{6,14},... | collective-permute-start | bytes 737288 | tf_op jit(solution)/shard_map/ppermute | solution.py:482
  80.7 32.2 %collective-permute-start.6 = (bf16[10,3,32,128]{3,2,1,0:T(8,128)(2,1)}, bf16[10,3,32,128]{3,2,1,0:T(8,128)(2,1)S(1)}, u32[]{:S(2)}, u32[]{:S(2)}) collective-permute-start(bf16[10,3,32,128]{3,2,1,0:T(8,128)(2,1)} %get-tuple-element.13.refs_0_), channel_id=1, source_target_pairs={{0,4},{4,0},{8,12},{12,8},{1,5},{5,1},{9,13},{13,9},{2,6},{6,2},{1... | collective-permute-start | bytes 737288 | tf_op jit(solution)/shard_map/ppermute | solution.py:482
  88.7 6.5 %copy-start.3 = (bf16[10,3,32,128]{3,2,1,0:T(8,128)(2,1)}, bf16[10,3,32,128]{3,2,1,0:T(8,128)(2,1)S(1)}, u32[]{:S(2)}) copy-start(bf16[10,3,32,128]{3,2,1,0:T(8,128)(2,1)S(1)} %collective-permute-done.7.refs_2_) | copy-start | bytes 737284
  88.7 24.3 %collective-permute-start.8 = (bf16[10,3,32,128]{3,2,1,0:T(8,128)(2,1)S(1)}, bf16[10,3,32,128]{3,2,1,0:T(8,128)(2,1)}, u32[]{:S(2)}, u32[]{:S(2)}) collective-permute-start(bf16[10,3,32,128]{3,2,1,0:T(8,128)(2,1)S(1)} %collective-permute-done.7.refs_2_), channel_id=1, source_target_pairs={{0,4},{4,0},{8,12},{12,8},{1,5},{5,1},{9,13},{13,9},{2,6},{6,2},{1... | collective-permute-start | bytes 737288 | tf_op jit(solution)/shard_map/ppermute | solution.py:482
  100.8 1.0 copy-start
  106.5 0.9 copy-start.1
  113.0 0.7 copy-start.4

commit v4 on v3

--- a/solution.py
+++ b/solution.py
@@ -16,6 +16,7 @@
 epsilon = 1e-06
 MASKED = -1e30
 LOG2E = math.log2(math.e)
+PARAMS = pltpu.CompilerParams(vmem_limit_bytes=24 * 2**20)
 VMEM = pl.BlockSpec(memory_space=pltpu.VMEM)
 NT = (((1,), (1,)), ((), ()))
 
@@ -31,8 +32,13 @@
             out_specs=out_specs,
             scratch_shapes=list(scratch),
         ),
+        compiler_params=PARAMS,
         cost_estimate=pl.CostEstimate(flops=flops, bytes_accessed=nbytes, transcendentals=0),
     )
+
+
+def far(x):
+    return pltpu.with_memory_space_constraint(x, pltpu.HBM)
 
 
 def sigmoid(x):
@@ -120,7 +126,7 @@
         1,
         12 * rows * heads * size * size,
         4 * rows * heads * size,
-    )(z, keys, values, rates, weights)
+    )(z, far(keys), far(values), far(rates), far(weights))
 
 
 def update_body(count, z_ref, w_ref, m_ref, *refs):
@@ -257,6 +263,7 @@
             out_specs=pl.BlockSpec((rows - WIN, group * size), lambda h: (0, step)),
             scratch_shapes=[pltpu.VMEM((2, SCORES, TILE), jnp.float32)],
         ),
+        compiler_params=PARAMS,
         input_output_aliases={3: 0} if more else {},
         cost_estimate=pl.CostEstimate(
             flops=6 * (rows - WIN) * WIN * size * group,
@@ -307,6 +314,7 @@
 
 
 EXTRA = 16
+KEPT = 3
 
 
 def put_partial(o_ref, g, t, size):
@@ -410,6 +418,7 @@
             out_specs=column,
             scratch_shapes=[pltpu.VMEM((2, WIN, TILE), jnp.float32)],
         ),
+        compiler_params=PARAMS,
         input_output_aliases={5: 0},
         cost_estimate=pl.CostEstimate(
             flops=4 * WIN * WIN * size * heads, bytes_accessed=10 * WIN * size * heads, transcendentals=0
@@ -472,6 +481,41 @@
     )(z, queries, first, later, *blocks)
 
 
+def pack_body(cut, q_ref, k_ref, v_ref, ask_ref, carry_ref, sems):
+    rows = q_ref.shape[0]
+    tail = pl.ds(rows - WIN, WIN)
+    copies = [
+        pltpu.make_async_copy(
+            q_ref.at[pl.ds(0, WIN), pl.ds(cut, q_ref.shape[1] - cut)], ask_ref, sems.at[0]
+        ),
+        pltpu.make_async_copy(k_ref.at[tail, pl.ds(0, cut)], carry_ref.at[0], sems.at[1]),
+        pltpu.make_async_copy(v_ref.at[tail, pl.ds(0, cut)], carry_ref.at[1], sems.at[2]),
+    ]
+    for copy in copies:
+        copy.start()
+    for copy in copies:
+        copy.wait()
+
+
+def packed(queries, keys, values, cut):
+    width = queries.shape[1]
+    here = pl.BlockSpec(memory_space=pltpu.HBM)
+    return call(
+        functools.partial(pack_body, cut),
+        (),
+        [here] * 3,
+        [VMEM] * 2,
+        [
+            jax.ShapeDtypeStruct((WIN, width - cut), queries.dtype),
+            jax.ShapeDtypeStruct((2, WIN, cut), keys.dtype),
+        ],
+        [pltpu.SemaphoreType.DMA((3,))],
+        0,
+        0,
+        4 * WIN * (width + cut),
+    )(far(queries), far(keys), far(values))
+
+
 def moved_by(value, by):
     peers = lax.axis_size("seq")
     pairs = [(i, i + by) for i in range(peers) if 0 <= i + by < peers]
@@ -483,11 +527,10 @@
 
 
 def kept_of(heads):
-    return max(1, heads * 4 // 10)
+    return max(1, heads * KEPT // 10)
 
 
 def shards(queries, keys, values, rates, fast_weights, momentum):
-    rows = queries.shape[0]
     heads = rates.shape[0]
     size = fast_weights.shape[0]
     peers = lax.axis_size("seq")
@@ -495,8 +538,9 @@
     z = lax.axis_index("seq").astype(jnp.int32).reshape(1)
     cut = kept * size
 
-    asked = moved_by(queries[:WIN, cut:], -1)
-    carried = moved_by(jnp.stack([keys[rows - WIN :, :cut], values[rows - WIN :, :cut]]), 1)
+    asked, carried = packed(queries, keys, values, cut)
+    asked = moved_by(asked, -1)
+    carried = moved_by(carried, 1)
 
     weights = jnp.transpose(fast_weights, (1, 2, 0, 3))
     own_momentum = jnp.transpose(momentum, (1, 2, 0, 3))

time: 121 us -> 115 us (0.950)
  waiting for transfers between devices: 44.7 us -> 60 us
  Pallas kernels: 45.3 us -> 33.4 us
  local copies, waits for them, and re-layouts: 5.75 us -> 0.04 us
  starting transfers between devices: 22.5 us -> 20.7 us
    ppermute x3, waiting for transfers between devices: 0.88 us -> 12.4 us  [moved_by(): return lax.ppermute(value, 'seq', pairs)]
    pallas_call x2, Pallas kernels: 11.3 us -> 5.95 us  [later_blocks(): pl.pallas_call(functools.partial(later_body, group), name='later', out_sh...]
    ppermute x6, waiting for transfers between devices: 43.8 us -> 47.6 us  [swapped(): lax.ppermute(value, 'seq', [(i, i ^ mask) for i in range(lax.axis_size('s...]
    unnamed x12, local copies, waits for them, and re-layouts: 3.29 us -> 0.04 us
    pallas_call x1, Pallas kernels: 4.77 us -> 1.92 us  [carried_block(): call(functools.partial(carried_body, group), (heads // group,), [column]...]
    ppermute x6, starting transfers between devices: 16.3 us -> 14.2 us  [swapped(): lax.ppermute(value, 'seq', [(i, i ^ mask) for i in range(lax.axis_size('s...]
    pallas_call x1, Pallas kernels: 6.4 us -> 4.71 us  [final(): call(functools.partial(final_body, peers, group), (heads // group,), [col...]
    pallas_call x0 -> x1, Pallas kernels: none -> 1.43 us  [packed(): call(functools.partial(pack_body, cut), (), [here] * 3, [VMEM] * 2, [jax....]
  transfers between devices with their start and end apart: 9 -> 9, of which waited for: 4 -> 4; matrix products, arithmetic and copies ran while one was open for 2% -> 0% of each run, Pallas kernels for 32% -> 24%
where the time goes in v4:
time: 115 us
  waiting for transfers between devices  60 us (52%)
  Pallas kernels  33.4 us (29%)
  starting transfers between devices  20.7 us (18%)
    ppermute x6, waiting for transfers between devices, swapped(): lax.ppermute(value, 'seq', [(i, i ^ mask) for i in range(lax.axis_size('s...  47.6 us
    ppermute x6, starting transfers between devices, swapped(): lax.ppermute(value, 'seq', [(i, i ^ mask) for i in range(lax.axis_size('s...  14.2 us
    ppermute x3, waiting for transfers between devices, moved_by(): return lax.ppermute(value, 'seq', pairs)  12.4 us
    pallas_call x1, Pallas kernels, partial_grads(): call(functools.partial(grad_body, peers, group, min(rows, 512)), (heads /...  8.65 us
    ppermute x3, starting transfers between devices, moved_by(): return lax.ppermute(value, 'seq', pairs)  6.56 us
    pallas_call x2, Pallas kernels, later_blocks(): pl.pallas_call(functools.partial(later_body, group), name='later', out_sh...  5.95 us
    pallas_call x1, Pallas kernels, joined_block(): pl.pallas_call(functools.partial(joined_body, group), name='joined', out_...  5.17 us
    pallas_call x1, Pallas kernels, final(): call(functools.partial(final_body, peers, group), (heads // group,), [col...  4.71 us
  transfers between devices with their start and end apart: 9, of which 4 were waited for; matrix products, arithmetic and copies ran while one was open for 0% of the time, Pallas kernels for 24%

profile of v4, /device:TPU:0, one launch (start us, length us, event | category | flops | bytes accessed | tf_op | source)
XLA Modules:
  0.0 115.0 jit_solution(3073098062338979)
XLA Ops:
  0.6 1.4 %shard_map.85 = (bf16[512,896]{1,0:T(8,128)(2,1)S(1)}, bf16[2,512,384]{2,1,0:T(8,128)(2,1)S(1)}) custom-call(bf16[1024,1280]{1,0:T(8,128)(2,1)} %q_ref.11, bf16[1024,1280]{1,0:T(8,128)(2,1)} %k_ref.13, bf16[1024,1280]{1,0:T(8,128)(2,1)} %v_ref.13), custom_call_target="tpu_custom_call" | custom-call | bytes 3407872 | tf_op jit(solution)/shard_map/pallas_call | solution.py:503
  2.1 1.3 %collective-permute-start = (bf16[512,896]{1,0:T(8,128)(2,1)S(1)}, bf16[512,896]{1,0:T(8,128)(2,1)S(1)}, u32[]{:S(2)}, u32[]{:S(2)}) collective-permute-start(bf16[512,896]{1,0:T(8,128)(2,1)S(1)} %get-tuple-element.11), channel_id=1, source_target_pairs={{4,0},{8,4},{12,8},{5,1},{9,5},{13,9},{6,2},{10,6},{14,10},{7,3},{... | collective-permute-start | bytes 2752520 | tf_op jit(solution)/shard_map/ppermute | solution.py:522
  3.4 0.0 copy-start
  3.4 0.0 copy-start.1
  3.4 8.7 %shard_map.88 = (f32[10,3,32,128]{3,2,1,0:T(8,128)S(1)}, bf16[10,3,32,128]{3,2,1,0:T(8,128)(2,1)S(1)}, f32[10,3,32,128]{3,2,1,0:T(8,128)S(1)}, bf16[10,3,32,128]{3,2,1,0:T(8,128)(2,1)S(1)}) custom-call(s32[1]{0:T(128)} %bitcast.z_ref, bf16[1024,1280]{1,0:T(8,128)(2,1)} %k_ref.13, bf16[1024,1280]{1,0:T(8,128)(2,1)} %v_ref.13, f32[10,1024]{1,0:T(8,128)} %r_ref.1, ...), custom_call_target="tpu_custom_call" | custom-call | flops 2013265920 | bytes 5242880 | tf_op jit(solution)/shard_map/pallas_call | solution.py:114
  12.1 0.0 copy-start.3
  12.1 0.0 copy-start.4
  12.1 3.7 %collective-permute-start.4 = (bf16[10,3,32,128]{3,2,1,0:T(8,128)(2,1)S(1)}, bf16[10,3,32,128]{3,2,1,0:T(8,128)(2,1)S(1)}, u32[]{:S(2)}, u32[]{:S(2)}) collective-permute-start(bf16[10,3,32,128]{3,2,1,0:T(8,128)(2,1)S(1)} %get-tuple-element.16), channel_id=1, source_target_pairs={{0,4},{4,0},{8,12},{12,8},{1,5},{5,1},{9,13},{13,9},{2,6},{6,2},{1... | collective-permute-start | bytes 737288 | tf_op jit(solution)/shard_map/ppermute | solution.py:526
  15.8 12.4 %collective-permute-done.q_ref = bf16[512,896]{1,0:T(8,128)(2,1)S(1)} collective-permute-done((bf16[512,896]{1,0:T(8,128)(2,1)S(1)}, bf16[512,896]{1,0:T(8,128)(2,1)S(1)}, u32[]{:S(2)}, u32[]{:S(2)}) %collective-permute-start) | collective-permute-done | bytes 917536 | tf_op jit(solution)/shard_map/ppermute | solution.py:522
  28.2 4.4 %shard_map.86 = bf16[7,144,512]{2,1,0:T(8,128)(2,1)S(1)} custom-call(bf16[512,896]{1,0:T(8,128)(2,1)S(1)} %collective-permute-done.q_ref, bf16[1024,1280]{1,0:T(8,128)(2,1)S(1)} %copy-done, bf16[1024,1280]{1,0:T(8,128)(2,1)S(1)} %copy-done.1), custom_call_target="tpu_custom_call" | custom-call | flops 939524096 | bytes 3670016 | tf_op jit(solution)/shard_map/pallas_call | solution.py:357
  32.6 0.0 copy-start.2
  32.6 3.1 %collective-permute-start.1 = (bf16[7,144,512]{2,1,0:T(8,128)(2,1)S(1)}, bf16[7,144,512]{2,1,0:T(8,128)(2,1)S(1)}, u32[]{:S(2)}, u32[]{:S(2)}) collective-permute-start(bf16[7,144,512]{2,1,0:T(8,128)(2,1)S(1)} %shard_map.86), channel_id=1, source_target_pairs={{0,4},{4,8},{8,12},{1,5},{5,9},{9,13},{2,6},{6,10},{10,14},{3,7},{... | collective-permute-start | bytes 3096584 | tf_op jit(solution)/shard_map/ppermute | solution.py:522
  35.8 2.7 %collective-permute-start.3 = (bf16[10,3,32,128]{3,2,1,0:T(8,128)(2,1)S(1)}, bf16[10,3,32,128]{3,2,1,0:T(8,128)(2,1)S(1)}, u32[]{:S(2)}, u32[]{:S(2)}) collective-permute-start(bf16[10,3,32,128]{3,2,1,0:T(8,128)(2,1)S(1)} %get-tuple-element.14), channel_id=1, source_target_pairs={{0,4},{4,0},{8,12},{12,8},{1,5},{5,1},{9,13},{13,9},{2,6},{6,2},{1... | collective-permute-start | bytes 737288 | tf_op jit(solution)/shard_map/ppermute | solution.py:526
  38.5 2.1 %collective-permute-start.2 = (bf16[2,512,384]{2,1,0:T(8,128)(2,1)S(1)}, bf16[2,512,384]{2,1,0:T(8,128)(2,1)S(1)}, u32[]{:S(2)}, u32[]{:S(2)}) collective-permute-start(bf16[2,512,384]{2,1,0:T(8,128)(2,1)S(1)} %get-tuple-element.12), channel_id=1, source_target_pairs={{0,4},{4,8},{8,12},{1,5},{5,9},{9,13},{2,6},{6,10},{10,14},{3,7},{... | collective-permute-start | bytes 2359304 | tf_op jit(solution)/shard_map/ppermute | solution.py:522
  40.6 0.0 collective-permute-done.4
  40.6 0.1 add_convert_fusion
  40.7 1.5 %collective-permute-start.5 = (bf16[10,3,32,128]{3,2,1,0:T(8,128)(2,1)S(1)}, bf16[10,3,32,128]{3,2,1,0:T(8,128)(2,1)S(1)}, u32[]{:S(2)}, u32[]{:S(2)}) collective-permute-start(bf16[10,3,32,128]{3,2,1,0:T(8,128)(2,1)S(1)} %add_convert_fusion), channel_id=1, source_target_pairs={{0,8},{4,12},{8,0},{12,4},{1,9},{5,13},{9,1},{13,5},{2,10},{6,14},... | collective-permute-start | bytes 737288 | tf_op jit(solution)/shard_map/ppermute | solution.py:526
  42.2 22.0 %collective-permute-done.3.refs_1_ = bf16[10,3,32,128]{3,2,1,0:T(8,128)(2,1)S(1)} collective-permute-done((bf16[10,3,32,128]{3,2,1,0:T(8,128)(2,1)S(1)}, bf16[10,3,32,128]{3,2,1,0:T(8,128)(2,1)S(1)}, u32[]{:S(2)}, u32[]{:S(2)}) %collective-permute-start.3) | collective-permute-done | bytes 245792 | tf_op jit(solution)/shard_map/ppermute | solution.py:526
  64.1 20.2 %collective-permute-done.5.refs_2_ = bf16[10,3,32,128]{3,2,1,0:T(8,128)(2,1)S(1)} collective-permute-done((bf16[10,3,32,128]{3,2,1,0:T(8,128)(2,1)S(1)}, bf16[10,3,32,128]{3,2,1,0:T(8,128)(2,1)S(1)}, u32[]{:S(2)}, u32[]{:S(2)}) %collective-permute-start.5) | collective-permute-done | bytes 245792 | tf_op jit(solution)/shard_map/ppermute | solution.py:526
  84.3 1.2 %shard_map.89 = (bf16[10,3,32,128]{3,2,1,0:T(8,128)(2,1)}, f32[10,3,32,128]{3,2,1,0:T(8,128)}) custom-call(s32[1]{0:T(128)} %bitcast.z_ref, bf16[10,3,128,128]{3,2,1,0:T(8,128)(2,1)S(1)} %bitcast.6, f32[10,3,32,128]{3,2,1,0:T(8,128)S(1)} %bitcast.7, f32[10,3,32,128]{3,2,1,0:T(8,128)S(1)} %get-tuple-element.13.refs_0_, ...), custom_call_target="tpu_custom_call" | custom-call | flops 2457600 | bytes 1966080 | tf_op jit(solution)/shard_map/pallas_call | solution.py:152
  85.5 3.4 %collective-permute-start.7 = (bf16[10,3,32,128]{3,2,1,0:T(8,128)(2,1)}, bf16[10,3,32,128]{3,2,1,0:T(8,128)(2,1)S(1)}, u32[]{:S(2)}, u32[]{:S(2)}) collective-permute-start(bf16[10,3,32,128]{3,2,1,0:T(8,128)(2,1)} %get-tuple-element.17.refs_0_), channel_id=1, source_target_pairs={{0,8},{4,12},{8,0},{12,4},{1,9},{5,13},{9,1},{13,5},{2,10},{6,14},... | collective-permute-start | bytes 737288 | tf_op jit(solution)/shard_map/ppermute | solution.py:526
  88.9 1.7 %collective-permute-start.6 = (bf16[10,3,32,128]{3,2,1,0:T(8,128)(2,1)}, bf16[10,3,32,128]{3,2,1,0:T(8,128)(2,1)S(1)}, u32[]{:S(2)}, u32[]{:S(2)}) collective-permute-start(bf16[10,3,32,128]{3,2,1,0:T(8,128)(2,1)} %get-tuple-element.17.refs_0_), channel_id=1, source_target_pairs={{0,4},{4,0},{8,12},{12,8},{1,5},{5,1},{9,13},{13,9},{2,6},{6,2},{1... | collective-permute-start | bytes 737288 | tf_op jit(solution)/shard_map/ppermute | solution.py:526
  90.7 5.4 %collective-permute-done.7.refs_2_ = bf16[10,3,32,128]{3,2,1,0:T(8,128)(2,1)S(1)} collective-permute-done((bf16[10,3,32,128]{3,2,1,0:T(8,128)(2,1)}, bf16[10,3,32,128]{3,2,1,0:T(8,128)(2,1)S(1)}, u32[]{:S(2)}, u32[]{:S(2)}) %collective-permute-start.7) | collective-permute-done | bytes 245792 | tf_op jit(solution)/shard_map/ppermute | solution.py:526
  96.1 1.1 collective-permute-start.8
  97.2 3.0 %later.2.refs_0_ = bf16[512,1280]{1,0:T(8,128)(2,1)S(1)} custom-call(bf16[1024,1280]{1,0:T(8,128)(2,1)S(1)} %copy-done.2, bf16[1024,1280]{1,0:T(8,128)(2,1)S(1)} %copy-done, bf16[1024,1280]{1,0:T(8,128)(2,1)S(1)} %copy-done.1), custom_call_target="tpu_custom_call" | custom-call | flops 1006632960 | bytes 5242880 | tf_op jit(solution)/shard_map/later/pallas_call | solution.py:255
  100.2 3.0 %later.3.later_ref = bf16[512,1280]{1,0:T(8,128)(2,1)S(1)} custom-call(bf16[1024,1280]{1,0:T(8,128)(2,1)S(1)} %copy-done.2, bf16[1024,1280]{1,0:T(8,128)(2,1)S(1)} %copy-done, bf16[1024,1280]{1,0:T(8,128)(2,1)S(1)} %copy-done.1, bf16[512,1280]{1,0:T(8,128)(2,1)S(1)} %later.2.refs_0_), custom_call_target="tpu_custom_call", output_to_operand_aliasing={{}: (3, {})} | custom-call | flops 1006632960 | bytes 5242880 | tf_op jit(solution)/shard_map/later/pallas_call | solution.py:255
  103.2 0.0 collective-permute-done.2.p_ref
  103.2 1.9 %shard_map.87._ = bf16[512,1280]{1,0:T(8,128)(2,1)S(1)} custom-call(s32[1]{0:T(128)} %bitcast.z_ref, bf16[1024,1280]{1,0:T(8,128)(2,1)S(1)} %copy-done.2, bf16[1024,1280]{1,0:T(8,128)(2,1)S(1)} %copy-done, bf16[1024,1280]{1,0:T(8,128)(2,1)S(1)} %copy-done.1, bf16[2,512,384]{2,1,0:T(8,128)(2,1)S(1)} %collective-permute-done.2.p_ref), custom_call_target="tpu_custom_call" | custom-call | flops 603979776 | bytes 1966080 | tf_op jit(solution)/shard_map/pallas_call | solution.py:303
  105.1 0.0 copy-start.5
  105.1 5.2 %joined.1.first_ref = bf16[512,1280]{1,0:T(8,128)(2,1)S(1)} custom-call(s32[1]{0:T(128)} %bitcast.z_ref, bf16[1024,1280]{1,0:T(8,128)(2,1)S(1)} %copy-done.2, bf16[1024,1280]{1,0:T(8,128)(2,1)S(1)} %copy-done, bf16[1024,1280]{1,0:T(8,128)(2,1)S(1)} %copy-done.1, ...), custom_call_target="tpu_custom_call", output_to_operand_aliasing={{}: (5, {})} | custom-call | flops 939524096 | bytes 4587520 | tf_op jit(solution)/shard_map/joined/pallas_call | solution.py:404
  110.3 0.0 collective-permute-done.6.refs_1_
  110.3 4.7 %shard_map.90 = bf16[1024,1280]{1,0:T(8,128)(2,1)} custom-call(s32[1]{0:T(128)} %bitcast.z_ref, bf16[1024,1280]{1,0:T(8,128)(2,1)S(1)} %copy-done.2, bf16[512,1280]{1,0:T(8,128)(2,1)S(1)} %joined.1.first_ref, bf16[512,1280]{1,0:T(8,128)(2,1)S(1)} %later.3.later_ref, bf16[10,3,32,128]{3,2,1,0:T(8,128)(2,1)S(1)} %copy-done.5, ...), custom_call_target="tpu_custom_call" | custom-call | flops 1006632960 | bytes 7864320 | tf_op jit(solution)/shard_map/pallas_call | solution.py:466
  (8 shorter events, 0.0 us)
Async XLA Ops:
  2.1 26.2 %collective-permute-start = (bf16[512,896]{1,0:T(8,128)(2,1)S(1)}, bf16[512,896]{1,0:T(8,128)(2,1)S(1)}, u32[]{:S(2)}, u32[]{:S(2)}) collective-permute-start(bf16[512,896]{1,0:T(8,128)(2,1)S(1)} %get-tuple-element.11), channel_id=1, source_target_pairs={{4,0},{8,4},{12,8},{5,1},{9,5},{13,9},{6,2},{10,6},{14,10},{7,3},{... | collective-permute-start | bytes 2752520 | tf_op jit(solution)/shard_map/ppermute | solution.py:522
  3.4 24.9 %copy-start = (bf16[1024,1280]{1,0:T(8,128)(2,1)S(1)}, bf16[1024,1280]{1,0:T(8,128)(2,1)}, u32[]{:S(2)}) copy-start(bf16[1024,1280]{1,0:T(8,128)(2,1)} %k_ref.13) | copy-start | bytes 7864324
  3.4 24.8 %copy-start.1 = (bf16[1024,1280]{1,0:T(8,128)(2,1)S(1)}, bf16[1024,1280]{1,0:T(8,128)(2,1)}, u32[]{:S(2)}) copy-start(bf16[1024,1280]{1,0:T(8,128)(2,1)} %v_ref.13) | copy-start | bytes 7864324
  12.1 72.3 %copy-start.3 = (bf16[128,10,3,128]{3,0,2,1:T(8,128)(2,1)S(1)}, bf16[128,10,3,128]{3,0,2,1:T(8,128)(2,1)}, u32[]{:S(2)}) copy-start(bf16[128,10,3,128]{3,0,2,1:T(8,128)(2,1)} %param.10) | copy-start | bytes 2949124
  12.1 72.3 %copy-start.4 = (f32[32,10,3,128]{3,0,2,1:T(8,128)S(1)}, f32[32,10,3,128]{3,0,2,1:T(8,128)}, u32[]{:S(2)}) copy-start(f32[32,10,3,128]{3,0,2,1:T(8,128)} %param.11) | copy-start | bytes 1474564
  12.1 28.6 %collective-permute-start.4 = (bf16[10,3,32,128]{3,2,1,0:T(8,128)(2,1)S(1)}, bf16[10,3,32,128]{3,2,1,0:T(8,128)(2,1)S(1)}, u32[]{:S(2)}, u32[]{:S(2)}) collective-permute-start(bf16[10,3,32,128]{3,2,1,0:T(8,128)(2,1)S(1)} %get-tuple-element.16), channel_id=1, source_target_pairs={{0,4},{4,0},{8,12},{12,8},{1,5},{5,1},{9,13},{13,9},{2,6},{6,2},{1... | collective-permute-start | bytes 737288 | tf_op jit(solution)/shard_map/ppermute | solution.py:526
  32.6 64.6 %copy-start.2 = (bf16[1024,1280]{1,0:T(8,128)(2,1)S(1)}, bf16[1024,1280]{1,0:T(8,128)(2,1)}, u32[]{:S(2)}) copy-start(bf16[1024,1280]{1,0:T(8,128)(2,1)} %q_ref.11) | copy-start | bytes 7864324
  32.6 72.5 %collective-permute-start.1 = (bf16[7,144,512]{2,1,0:T(8,128)(2,1)S(1)}, bf16[7,144,512]{2,1,0:T(8,128)(2,1)S(1)}, u32[]{:S(2)}, u32[]{:S(2)}) collective-permute-start(bf16[7,144,512]{2,1,0:T(8,128)(2,1)S(1)} %shard_map.86), channel_id=1, source_target_pairs={{0,4},{4,8},{8,12},{1,5},{5,9},{9,13},{2,6},{6,10},{10,14},{3,7},{... | collective-permute-start | bytes 3096584 | tf_op jit(solution)/shard_map/ppermute | solution.py:522
  35.8 28.4 %collective-permute-start.3 = (bf16[10,3,32,128]{3,2,1,0:T(8,128)(2,1)S(1)}, bf16[10,3,32,128]{3,2,1,0:T(8,128)(2,1)S(1)}, u32[]{:S(2)}, u32[]{:S(2)}) collective-permute-start(bf16[10,3,32,128]{3,2,1,0:T(8,128)(2,1)S(1)} %get-tuple-element.14), channel_id=1, source_target_pairs={{0,4},{4,0},{8,12},{12,8},{1,5},{5,1},{9,13},{13,9},{2,6},{6,2},{1... | collective-permute-start | bytes 737288 | tf_op jit(solution)/shard_map/ppermute | solution.py:526
  38.5 64.7 %collective-permute-start.2 = (bf16[2,512,384]{2,1,0:T(8,128)(2,1)S(1)}, bf16[2,512,384]{2,1,0:T(8,128)(2,1)S(1)}, u32[]{:S(2)}, u32[]{:S(2)}) collective-permute-start(bf16[2,512,384]{2,1,0:T(8,128)(2,1)S(1)} %get-tuple-element.12), channel_id=1, source_target_pairs={{0,4},{4,8},{8,12},{1,5},{5,9},{9,13},{2,6},{6,10},{10,14},{3,7},{... | collective-permute-start | bytes 2359304 | tf_op jit(solution)/shard_map/ppermute | solution.py:522
  40.7 43.6 %collective-permute-start.5 = (bf16[10,3,32,128]{3,2,1,0:T(8,128)(2,1)S(1)}, bf16[10,3,32,128]{3,2,1,0:T(8,128)(2,1)S(1)}, u32[]{:S(2)}, u32[]{:S(2)}) collective-permute-start(bf16[10,3,32,128]{3,2,1,0:T(8,128)(2,1)S(1)} %add_convert_fusion), channel_id=1, source_target_pairs={{0,8},{4,12},{8,0},{12,4},{1,9},{5,13},{9,1},{13,5},{2,10},{6,14},... | collective-permute-start | bytes 737288 | tf_op jit(solution)/shard_map/ppermute | solution.py:526
  85.5 10.6 %collective-permute-start.7 = (bf16[10,3,32,128]{3,2,1,0:T(8,128)(2,1)}, bf16[10,3,32,128]{3,2,1,0:T(8,128)(2,1)S(1)}, u32[]{:S(2)}, u32[]{:S(2)}) collective-permute-start(bf16[10,3,32,128]{3,2,1,0:T(8,128)(2,1)} %get-tuple-element.17.refs_0_), channel_id=1, source_target_pairs={{0,8},{4,12},{8,0},{12,4},{1,9},{5,13},{9,1},{13,5},{2,10},{6,14},... | collective-permute-start | bytes 737288 | tf_op jit(solution)/shard_map/ppermute | solution.py:526
  88.9 21.4 %collective-permute-start.6 = (bf16[10,3,32,128]{3,2,1,0:T(8,128)(2,1)}, bf16[10,3,32,128]{3,2,1,0:T(8,128)(2,1)S(1)}, u32[]{:S(2)}, u32[]{:S(2)}) collective-permute-start(bf16[10,3,32,128]{3,2,1,0:T(8,128)(2,1)} %get-tuple-element.17.refs_0_), channel_id=1, source_target_pairs={{0,4},{4,0},{8,12},{12,8},{1,5},{5,1},{9,13},{13,9},{2,6},{6,2},{1... | collective-permute-start | bytes 737288 | tf_op jit(solution)/shard_map/ppermute | solution.py:526
  96.1 14.2 %collective-permute-start.8 = (bf16[10,3,32,128]{3,2,1,0:T(8,128)(2,1)S(1)}, bf16[10,3,32,128]{3,2,1,0:T(8,128)(2,1)S(1)}, u32[]{:S(2)}, u32[]{:S(2)}) collective-permute-start(bf16[10,3,32,128]{3,2,1,0:T(8,128)(2,1)S(1)} %collective-permute-done.7.refs_2_), channel_id=1, source_target_pairs={{0,4},{4,0},{8,12},{12,8},{1,5},{5,1},{9,13},{13,9},{2,6},{6,2},{1... | collective-permute-start | bytes 737288 | tf_op jit(solution)/shard_map/ppermute | solution.py:526
  105.1 5.2 %copy-start.5 = (bf16[10,3,32,128]{3,2,1,0:T(8,128)(2,1)S(1)}, bf16[10,3,32,128]{3,2,1,0:T(8,128)(2,1)}, u32[]{:S(2)}) copy-start(bf16[10,3,32,128]{3,2,1,0:T(8,128)(2,1)} %get-tuple-element.17.refs_0_) | copy-start | bytes 737284

commit v5 on v4

--- a/solution.py
+++ b/solution.py
@@ -126,7 +126,7 @@
         1,
         12 * rows * heads * size * size,
         4 * rows * heads * size,
-    )(z, far(keys), far(values), far(rates), far(weights))
+    )(z, keys, far(values), far(rates), far(weights))
 
 
 def update_body(count, z_ref, w_ref, m_ref, *refs):
@@ -313,8 +313,9 @@
     )(z, queries, keys, values, carried)
 
 
-EXTRA = 16
+EXTRA = 8
 KEPT = 3
+EARLY = 4
 
 
 def put_partial(o_ref, g, t, size):
@@ -481,38 +482,34 @@
     )(z, queries, first, later, *blocks)
 
 
-def pack_body(cut, q_ref, k_ref, v_ref, ask_ref, carry_ref, sems):
-    rows = q_ref.shape[0]
-    tail = pl.ds(rows - WIN, WIN)
+def pack_body(first, q_ref, k_ref, v_ref, ask_ref, carry_ref, sems):
+    cut = carry_ref.shape[2]
+    tail = pl.ds(q_ref.shape[0] - WIN, WIN)
     copies = [
-        pltpu.make_async_copy(
-            q_ref.at[pl.ds(0, WIN), pl.ds(cut, q_ref.shape[1] - cut)], ask_ref, sems.at[0]
-        ),
-        pltpu.make_async_copy(k_ref.at[tail, pl.ds(0, cut)], carry_ref.at[0], sems.at[1]),
-        pltpu.make_async_copy(v_ref.at[tail, pl.ds(0, cut)], carry_ref.at[1], sems.at[2]),
+        (k_ref.at[tail, pl.ds(0, cut)], carry_ref.at[0]),
+        (v_ref.at[tail, pl.ds(0, cut)], carry_ref.at[1]),
+        (q_ref.at[pl.ds(0, WIN), pl.ds(first, ask_ref.shape[1])], ask_ref),
     ]
+    copies = [pltpu.make_async_copy(*c, sems.at[i]) for i, c in enumerate(copies)]
     for copy in copies:
         copy.start()
     for copy in copies:
         copy.wait()
 
 
-def packed(queries, keys, values, cut):
-    width = queries.shape[1]
+def packed(queries, keys, values, cut, asked):
     here = pl.BlockSpec(memory_space=pltpu.HBM)
+    shapes = [(WIN, asked[1]), (2, WIN, cut)]
     return call(
-        functools.partial(pack_body, cut),
+        functools.partial(pack_body, asked[0]),
         (),
         [here] * 3,
         [VMEM] * 2,
-        [
-            jax.ShapeDtypeStruct((WIN, width - cut), queries.dtype),
-            jax.ShapeDtypeStruct((2, WIN, cut), keys.dtype),
-        ],
+        [jax.ShapeDtypeStruct(shape, queries.dtype) for shape in shapes],
         [pltpu.SemaphoreType.DMA((3,))],
         0,
         0,
-        4 * WIN * (width + cut),
+        4 * WIN * (2 * cut + asked[1]),
     )(far(queries), far(keys), far(values))
 
 
@@ -536,10 +533,12 @@
     peers = lax.axis_size("seq")
     kept = kept_of(heads)
     z = lax.axis_index("seq").astype(jnp.int32).reshape(1)
-    cut = kept * size
-
-    asked, carried = packed(queries, keys, values, cut)
-    asked = moved_by(asked, -1)
+    early = max(1, heads * EARLY // 10)
+    groups = [(kept, early), (kept + early, heads - kept - early)]
+
+    asked, carried = packed(queries, keys, values, kept * size, (kept * size, early * size))
+    asked = [moved_by(asked, -1)]
+    asked.append(moved_by(queries[:WIN, (kept + early) * size :], -1))
     carried = moved_by(carried, 1)
 
     weights = jnp.transpose(fast_weights, (1, 2, 0, 3))
@@ -560,10 +559,13 @@
     later = None
     for part in range(heads // group):
         later = later_blocks(queries, keys, values, size, part, group, later)
-    given = next_part(asked, keys, values, kept, size)
-    given = moved_by(given, 1)
+    given = []
+    for i, (place, _) in enumerate(groups):
+        part = next_part(asked[i], keys, values, place, size)
+        given.append(moved_by(part, 1))
     first = carried_block(z, queries, keys, values, carried, size)
-    first = joined_block(z, queries, keys, values, given, first, kept, size)
+    for i, (place, _) in enumerate(groups):
+        first = joined_block(z, queries, keys, values, given[i], first, place, size)
 
     new_rows, new_momentum = updated(z, weights, own_momentum, sums[0])
     blocks = {0: new_rows}

time: 115 us -> 94.2 us (0.82)
  waiting for transfers between devices: 60 us -> 26.6 us
  starting transfers between devices: 20.7 us -> 31.7 us
  local copies, waits for them, and re-layouts: 0.04 us -> 1.81 us
    ppermute x6, waiting for transfers between devices: 47.6 us -> 20.7 us  [swapped(): lax.ppermute(value, 'seq', [(i, i ^ mask) for i in range(lax.axis_size('s...]
    ppermute x3 -> x5, starting transfers between devices: 6.56 us -> 15.2 us  [moved_by(): return lax.ppermute(value, 'seq', pairs)]
    ppermute x3 -> x5, waiting for transfers between devices: 12.4 us -> 5.99 us  [moved_by(): return lax.ppermute(value, 'seq', pairs)]
    ppermute x6, starting transfers between devices: 14.2 us -> 16.6 us  [swapped(): lax.ppermute(value, 'seq', [(i, i ^ mask) for i in range(lax.axis_size('s...]
    unnamed x12 -> x14, local copies, waits for them, and re-layouts: 0.04 us -> 1.77 us
    pallas_call x1 -> x2, Pallas kernels: 4.4 us -> 4.44 us  [next_part(): call(functools.partial(next_part_body, group), (heads // group,), [pl.Blo...]
    pallas_call x1 -> x2, Pallas kernels: 5.17 us -> 5.21 us  [joined_block(): pl.pallas_call(functools.partial(joined_body, group), name='joined', out_...]
  transfers between devices with their start and end apart: 9 -> 11, of which waited for: 4 -> 4; matrix products, arithmetic and copies ran while one was open for 0% -> 0% of each run, Pallas kernels for 24% -> 22%
where the time goes in v5:
time: 94.2 us; the launch traced here: 93.9 us
  Pallas kernels  32.8 us (35%)
  starting transfers between devices  31.7 us (34%)
  waiting for transfers between devices  26.6 us (28%)
  local copies, waits for them, and re-layouts  1.81 us (2%)
    ppermute x6, waiting for transfers between devices, swapped(): lax.ppermute(value, 'seq', [(i, i ^ mask) for i in range(lax.axis_size('s...  20.7 us
    ppermute x6, starting transfers between devices, swapped(): lax.ppermute(value, 'seq', [(i, i ^ mask) for i in range(lax.axis_size('s...  16.6 us
    ppermute x5, starting transfers between devices, moved_by(): return lax.ppermute(value, 'seq', pairs)  15.2 us
    pallas_call x1, Pallas kernels, partial_grads(): call(functools.partial(grad_body, peers, group, min(rows, 512)), (heads /...  7.84 us
    pallas_call x2, Pallas kernels, later_blocks(): pl.pallas_call(functools.partial(later_body, group), name='later', out_sh...  6.04 us
    ppermute x5, waiting for transfers between devices, moved_by(): return lax.ppermute(value, 'seq', pairs)  5.99 us
    pallas_call x2, Pallas kernels, joined_block(): pl.pallas_call(functools.partial(joined_body, group), name='joined', out_...  5.21 us
    pallas_call x1, Pallas kernels, final(): call(functools.partial(final_body, peers, group), (heads // group,), [col...  4.71 us
  transfers between devices with their start and end apart: 11, of which 4 were waited for; matrix products, arithmetic and copies ran while one was open for 0% of the time, Pallas kernels for 22%

profile of v5, /device:TPU:0, one launch (start us, length us, event | category | flops | bytes accessed | tf_op | source)
XLA Modules:
  0.0 93.9 jit_solution(750012264415103702)
XLA Ops:
  0.6 0.0 copy-start
  0.6 1.7 %copy-done = bf16[1024,1280]{1,0:T(8,128)(2,1)S(1)} copy-done((bf16[1024,1280]{1,0:T(8,128)(2,1)S(1)}, bf16[1024,1280]{1,0:T(8,128)(2,1)}, u32[]{:S(2)}) %copy-start) | copy-done | bytes 2621464
  2.4 7.8 %shard_map.89 = (f32[10,3,32,128]{3,2,1,0:T(8,128)S(1)}, bf16[10,3,32,128]{3,2,1,0:T(8,128)(2,1)S(1)}, f32[10,3,32,128]{3,2,1,0:T(8,128)S(1)}, bf16[10,3,32,128]{3,2,1,0:T(8,128)(2,1)S(1)}) custom-call(s32[1]{0:T(128)} %bitcast.z_ref, bf16[1024,1280]{1,0:T(8,128)(2,1)S(1)} %copy-done, bf16[1024,1280]{1,0:T(8,128)(2,1)} %v_ref.17, f32[10,1024]{1,0:T(8,128)} %r_ref.1, ...), custom_call_target="tpu_custom_call" | custom-call | flops 2013265920 | bytes 5242880 | tf_op jit(solution)/shard_map/pallas_call | solution.py:114
  10.2 0.0 copy-start.3
  10.2 3.1 %collective-permute-start.6 = (bf16[10,3,32,128]{3,2,1,0:T(8,128)(2,1)S(1)}, bf16[10,3,32,128]{3,2,1,0:T(8,128)(2,1)S(1)}, u32[]{:S(2)}, u32[]{:S(2)}) collective-permute-start(bf16[10,3,32,128]{3,2,1,0:T(8,128)(2,1)S(1)} %get-tuple-element.16), channel_id=1, source_target_pairs={{0,4},{4,0},{8,12},{12,8},{1,5},{5,1},{9,13},{13,9},{2,6},{6,2},{1... | collective-permute-start | bytes 737288 | tf_op jit(solution)/shard_map/ppermute | solution.py:523
  13.4 1.5 %shard_map.86 = (bf16[512,512]{1,0:T(8,128)(2,1)S(1)}, bf16[2,512,384]{2,1,0:T(8,128)(2,1)S(1)}) custom-call(bf16[1024,1280]{1,0:T(8,128)(2,1)} %q_ref.13, bf16[1024,1280]{1,0:T(8,128)(2,1)} %k_ref.17, bf16[1024,1280]{1,0:T(8,128)(2,1)} %v_ref.17), custom_call_target="tpu_custom_call" | custom-call | bytes 2621440 | tf_op jit(solution)/shard_map/pallas_call | solution.py:503
  14.8 1.4 %collective-permute-start.2 = (bf16[512,512]{1,0:T(8,128)(2,1)S(1)}, bf16[512,512]{1,0:T(8,128)(2,1)S(1)}, u32[]{:S(2)}, u32[]{:S(2)}) collective-permute-start(bf16[512,512]{1,0:T(8,128)(2,1)S(1)} %get-tuple-element.11), channel_id=1, source_target_pairs={{4,0},{8,4},{12,8},{5,1},{9,5},{13,9},{6,2},{10,6},{14,10},{7,3},{... | collective-permute-start | bytes 1572872 | tf_op jit(solution)/shard_map/ppermute | solution.py:519
  16.3 1.3 %collective-permute-start = (bf16[512,384]{1,0:T(8,128)(2,1)S(1)}, bf16[512,384]{1,0:T(8,128)(2,1)S(1)}, u32[]{:S(2)}, u32[]{:S(2)}) collective-permute-start(bf16[512,384]{1,0:T(8,128)(2,1)S(1)} %slice.3), channel_id=1, source_target_pairs={{4,0},{8,4},{12,8},{5,1},{9,5},{13,9},{6,2},{10,6},{14,10},{7,3},{... | collective-permute-start | bytes 1179656 | tf_op jit(solution)/shard_map/ppermute | solution.py:519
  17.6 5.2 %collective-permute-start.4 = (bf16[2,512,384]{2,1,0:T(8,128)(2,1)S(1)}, bf16[2,512,384]{2,1,0:T(8,128)(2,1)S(1)}, u32[]{:S(2)}, u32[]{:S(2)}) collective-permute-start(bf16[2,512,384]{2,1,0:T(8,128)(2,1)S(1)} %get-tuple-element.12), channel_id=1, source_target_pairs={{0,4},{4,8},{8,12},{1,5},{5,9},{9,13},{2,6},{6,10},{10,14},{3,7},{... | collective-permute-start | bytes 2359304 | tf_op jit(solution)/shard_map/ppermute | solution.py:519
  22.9 2.0 %collective-permute-start.5 = (bf16[10,3,32,128]{3,2,1,0:T(8,128)(2,1)S(1)}, bf16[10,3,32,128]{3,2,1,0:T(8,128)(2,1)S(1)}, u32[]{:S(2)}, u32[]{:S(2)}) collective-permute-start(bf16[10,3,32,128]{3,2,1,0:T(8,128)(2,1)S(1)} %get-tuple-element.14), channel_id=1, source_target_pairs={{0,4},{4,0},{8,12},{12,8},{1,5},{5,1},{9,13},{13,9},{2,6},{6,2},{1... | collective-permute-start | bytes 737288 | tf_op jit(solution)/shard_map/ppermute | solution.py:523
  24.9 0.1 add_convert_fusion
  25.0 0.0 copy-start.4
  25.0 0.0 copy-start.5
  25.0 0.7 collective-permute-start.7
  25.7 6.0 %collective-permute-done.2.q_ref = bf16[512,512]{1,0:T(8,128)(2,1)S(1)} collective-permute-done((bf16[512,512]{1,0:T(8,128)(2,1)S(1)}, bf16[512,512]{1,0:T(8,128)(2,1)S(1)}, u32[]{:S(2)}, u32[]{:S(2)}) %collective-permute-start.2) | collective-permute-done | bytes 524320 | tf_op jit(solution)/shard_map/ppermute | solution.py:519
  31.7 2.5 %shard_map.87 = bf16[4,136,512]{2,1,0:T(8,128)(2,1)S(1)} custom-call(bf16[512,512]{1,0:T(8,128)(2,1)S(1)} %collective-permute-done.2.q_ref, bf16[1024,1280]{1,0:T(8,128)(2,1)S(1)} %copy-done.1, bf16[1024,1280]{1,0:T(8,128)(2,1)S(1)} %copy-done.2), custom_call_target="tpu_custom_call" | custom-call | flops 536870912 | bytes 2097152 | tf_op jit(solution)/shard_map/pallas_call | solution.py:358
  34.2 3.1 %collective-permute-start.3 = (bf16[4,136,512]{2,1,0:T(8,128)(2,1)S(1)}, bf16[4,136,512]{2,1,0:T(8,128)(2,1)S(1)}, u32[]{:S(2)}, u32[]{:S(2)}) collective-permute-start(bf16[4,136,512]{2,1,0:T(8,128)(2,1)S(1)} %shard_map.87), channel_id=1, source_target_pairs={{0,4},{4,8},{8,12},{1,5},{5,9},{9,13},{2,6},{6,10},{10,14},{3,7},{... | collective-permute-start | bytes 1671176 | tf_op jit(solution)/shard_map/ppermute | solution.py:519
  37.3 12.2 %collective-permute-done.5.refs_1_ = bf16[10,3,32,128]{3,2,1,0:T(8,128)(2,1)S(1)} collective-permute-done((bf16[10,3,32,128]{3,2,1,0:T(8,128)(2,1)S(1)}, bf16[10,3,32,128]{3,2,1,0:T(8,128)(2,1)S(1)}, u32[]{:S(2)}, u32[]{:S(2)}) %collective-permute-start.5) | collective-permute-done | bytes 245792 | tf_op jit(solution)/shard_map/ppermute | solution.py:523
  49.5 1.8 %collective-permute-done.7.refs_2_ = bf16[10,3,32,128]{3,2,1,0:T(8,128)(2,1)S(1)} collective-permute-done((bf16[10,3,32,128]{3,2,1,0:T(8,128)(2,1)S(1)}, bf16[10,3,32,128]{3,2,1,0:T(8,128)(2,1)S(1)}, u32[]{:S(2)}, u32[]{:S(2)}) %collective-permute-start.7) | collective-permute-done | bytes 245792 | tf_op jit(solution)/shard_map/ppermute | solution.py:523
  51.3 1.2 %shard_map.90 = (bf16[10,3,32,128]{3,2,1,0:T(8,128)(2,1)}, f32[10,3,32,128]{3,2,1,0:T(8,128)}) custom-call(s32[1]{0:T(128)} %bitcast.z_ref, bf16[10,3,128,128]{3,2,1,0:T(8,128)(2,1)S(1)} %bitcast.6, f32[10,3,32,128]{3,2,1,0:T(8,128)S(1)} %bitcast.7, f32[10,3,32,128]{3,2,1,0:T(8,128)S(1)} %get-tuple-element.13.refs_0_, ...), custom_call_target="tpu_custom_call" | custom-call | flops 2457600 | bytes 1966080 | tf_op jit(solution)/shard_map/pallas_call | solution.py:152
  52.5 3.4 %collective-permute-start.9 = (bf16[10,3,32,128]{3,2,1,0:T(8,128)(2,1)}, bf16[10,3,32,128]{3,2,1,0:T(8,128)(2,1)S(1)}, u32[]{:S(2)}, u32[]{:S(2)}) collective-permute-start(bf16[10,3,32,128]{3,2,1,0:T(8,128)(2,1)} %get-tuple-element.17.refs_0_), channel_id=1, source_target_pairs={{0,8},{4,12},{8,0},{12,4},{1,9},{5,13},{9,1},{13,5},{2,10},{6,14},... | collective-permute-start | bytes 737288 | tf_op jit(solution)/shard_map/ppermute | solution.py:523
  55.9 1.9 %shard_map.85 = bf16[3,136,512]{2,1,0:T(8,128)(2,1)S(1)} custom-call(bf16[512,384]{1,0:T(8,128)(2,1)S(1)} %collective-permute-done.q_ref, bf16[1024,1280]{1,0:T(8,128)(2,1)S(1)} %copy-done.1, bf16[1024,1280]{1,0:T(8,128)(2,1)S(1)} %copy-done.2), custom_call_target="tpu_custom_call" | custom-call | flops 402653184 | bytes 1572864 | tf_op jit(solution)/shard_map/pallas_call | solution.py:358
  57.8 4.1 %collective-permute-start.1 = (bf16[3,136,512]{2,1,0:T(8,128)(2,1)S(1)}, bf16[3,136,512]{2,1,0:T(8,128)(2,1)S(1)}, u32[]{:S(2)}, u32[]{:S(2)}) collective-permute-start(bf16[3,136,512]{2,1,0:T(8,128)(2,1)S(1)} %shard_map.85), channel_id=1, source_target_pairs={{0,4},{4,8},{8,12},{1,5},{5,9},{9,13},{2,6},{6,10},{10,14},{3,7},{... | collective-permute-start | bytes 1253384 | tf_op jit(solution)/shard_map/ppermute | solution.py:519
  61.9 0.1 collective-permute-start.8
  62.0 6.6 %collective-permute-done.9.refs_2_ = bf16[10,3,32,128]{3,2,1,0:T(8,128)(2,1)S(1)} collective-permute-done((bf16[10,3,32,128]{3,2,1,0:T(8,128)(2,1)}, bf16[10,3,32,128]{3,2,1,0:T(8,128)(2,1)S(1)}, u32[]{:S(2)}, u32[]{:S(2)}) %collective-permute-start.9) | collective-permute-done | bytes 245792 | tf_op jit(solution)/shard_map/ppermute | solution.py:523
  68.7 7.3 %collective-permute-start.10 = (bf16[10,3,32,128]{3,2,1,0:T(8,128)(2,1)S(1)}, bf16[10,3,32,128]{3,2,1,0:T(8,128)(2,1)S(1)}, u32[]{:S(2)}, u32[]{:S(2)}) collective-permute-start(bf16[10,3,32,128]{3,2,1,0:T(8,128)(2,1)S(1)} %collective-permute-done.9.refs_2_), channel_id=1, source_target_pairs={{0,4},{4,0},{8,12},{12,8},{1,5},{5,1},{9,13},{13,9},{2,6},{6,2},{1... | collective-permute-start | bytes 737288 | tf_op jit(solution)/shard_map/ppermute | solution.py:523
  75.9 3.0 %later.2.refs_0_ = bf16[512,1280]{1,0:T(8,128)(2,1)S(1)} custom-call(bf16[1024,1280]{1,0:T(8,128)(2,1)S(1)} %copy-done.3, bf16[1024,1280]{1,0:T(8,128)(2,1)S(1)} %copy-done.1, bf16[1024,1280]{1,0:T(8,128)(2,1)S(1)} %copy-done.2), custom_call_target="tpu_custom_call" | custom-call | flops 1006632960 | bytes 5242880 | tf_op jit(solution)/shard_map/later/pallas_call | solution.py:255
  79.0 3.0 %later.3.later_ref = bf16[512,1280]{1,0:T(8,128)(2,1)S(1)} custom-call(bf16[1024,1280]{1,0:T(8,128)(2,1)S(1)} %copy-done.3, bf16[1024,1280]{1,0:T(8,128)(2,1)S(1)} %copy-done.1, bf16[1024,1280]{1,0:T(8,128)(2,1)S(1)} %copy-done.2, bf16[512,1280]{1,0:T(8,128)(2,1)S(1)} %later.2.refs_0_), custom_call_target="tpu_custom_call", output_to_operand_aliasing={{}: (3, {})} | custom-call | flops 1006632960 | bytes 5242880 | tf_op jit(solution)/shard_map/later/pallas_call | solution.py:255
  82.0 1.9 %shard_map.88._ = bf16[512,1280]{1,0:T(8,128)(2,1)S(1)} custom-call(s32[1]{0:T(128)} %bitcast.z_ref, bf16[1024,1280]{1,0:T(8,128)(2,1)S(1)} %copy-done.3, bf16[1024,1280]{1,0:T(8,128)(2,1)S(1)} %copy-done.1, bf16[1024,1280]{1,0:T(8,128)(2,1)S(1)} %copy-done.2, bf16[2,512,384]{2,1,0:T(8,128)(2,1)S(1)} %collective-permute-done.4.p_ref), custom_call_target="tpu_custom_call" | custom-call | flops 603979776 | bytes 1966080 | tf_op jit(solution)/shard_map/pallas_call | solution.py:303
  84.0 3.0 %joined.2._ = bf16[512,1280]{1,0:T(8,128)(2,1)S(1)} custom-call(s32[1]{0:T(128)} %bitcast.z_ref, bf16[1024,1280]{1,0:T(8,128)(2,1)S(1)} %copy-done.3, bf16[1024,1280]{1,0:T(8,128)(2,1)S(1)} %copy-done.1, bf16[1024,1280]{1,0:T(8,128)(2,1)S(1)} %copy-done.2, bf16[4,136,512]{2,1,0:T(8,128)(2,1)S(1)} %collective-permute-done.3.p_ref, ...), custom_call_target="tpu_custom_call", output_to_operand_aliasing={{}: (5, {})} | custom-call | flops 536870912 | bytes 2621440 | tf_op jit(solution)/shard_map/joined/pallas_call | solution.py:405
  87.0 2.2 %joined.3.first_ref = bf16[512,1280]{1,0:T(8,128)(2,1)S(1)} custom-call(s32[1]{0:T(128)} %bitcast.z_ref, bf16[1024,1280]{1,0:T(8,128)(2,1)S(1)} %copy-done.3, bf16[1024,1280]{1,0:T(8,128)(2,1)S(1)} %copy-done.1, bf16[1024,1280]{1,0:T(8,128)(2,1)S(1)} %copy-done.2, ...), custom_call_target="tpu_custom_call", output_to_operand_aliasing={{}: (5, {})} | custom-call | flops 402653184 | bytes 1966080 | tf_op jit(solution)/shard_map/joined/pallas_call | solution.py:405
  89.2 4.7 %shard_map.91 = bf16[1024,1280]{1,0:T(8,128)(2,1)} custom-call(s32[1]{0:T(128)} %bitcast.z_ref, bf16[1024,1280]{1,0:T(8,128)(2,1)S(1)} %copy-done.3, bf16[512,1280]{1,0:T(8,128)(2,1)S(1)} %joined.3.first_ref, bf16[512,1280]{1,0:T(8,128)(2,1)S(1)} %later.3.later_ref, bf16[10,3,32,128]{3,2,1,0:T(8,128)(2,1)S(1)} %copy-done.6, ...), custom_call_target="tpu_custom_call" | custom-call | flops 1006632960 | bytes 7864320 | tf_op jit(solution)/shard_map/pallas_call | solution.py:467
  (17 shorter events, 0.1 us)
Async XLA Ops:
  0.6 1.7 %copy-start = (bf16[1024,1280]{1,0:T(8,128)(2,1)S(1)}, bf16[1024,1280]{1,0:T(8,128)(2,1)}, u32[]{:S(2)}) copy-start(bf16[1024,1280]{1,0:T(8,128)(2,1)} %k_ref.17) | copy-start | bytes 7864324
  10.2 6.0 %copy-start.3 = (bf16[1024,1280]{1,0:T(8,128)(2,1)S(1)}, bf16[1024,1280]{1,0:T(8,128)(2,1)}, u32[]{:S(2)}) copy-start(bf16[1024,1280]{1,0:T(8,128)(2,1)} %q_ref.13) | copy-start | bytes 7864324
  10.2 14.6 %collective-permute-start.6 = (bf16[10,3,32,128]{3,2,1,0:T(8,128)(2,1)S(1)}, bf16[10,3,32,128]{3,2,1,0:T(8,128)(2,1)S(1)}, u32[]{:S(2)}, u32[]{:S(2)}) collective-permute-start(bf16[10,3,32,128]{3,2,1,0:T(8,128)(2,1)S(1)} %get-tuple-element.16), channel_id=1, source_target_pairs={{0,4},{4,0},{8,12},{12,8},{1,5},{5,1},{9,13},{13,9},{2,6},{6,2},{1... | collective-permute-start | bytes 737288 | tf_op jit(solution)/shard_map/ppermute | solution.py:523
  13.4 18.3 %copy-start.1 = (bf16[1024,1280]{1,0:T(8,128)(2,1)S(1)}, bf16[1024,1280]{1,0:T(8,128)(2,1)}, u32[]{:S(2)}) copy-start(bf16[1024,1280]{1,0:T(8,128)(2,1)} %k_ref.17) | copy-start | bytes 7864324
  13.4 18.3 %copy-start.2 = (bf16[1024,1280]{1,0:T(8,128)(2,1)S(1)}, bf16[1024,1280]{1,0:T(8,128)(2,1)}, u32[]{:S(2)}) copy-start(bf16[1024,1280]{1,0:T(8,128)(2,1)} %v_ref.17) | copy-start | bytes 7864324
  14.8 16.8 %collective-permute-start.2 = (bf16[512,512]{1,0:T(8,128)(2,1)S(1)}, bf16[512,512]{1,0:T(8,128)(2,1)S(1)}, u32[]{:S(2)}, u32[]{:S(2)}) collective-permute-start(bf16[512,512]{1,0:T(8,128)(2,1)S(1)} %get-tuple-element.11), channel_id=1, source_target_pairs={{4,0},{8,4},{12,8},{5,1},{9,5},{13,9},{6,2},{10,6},{14,10},{7,3},{... | collective-permute-start | bytes 1572872 | tf_op jit(solution)/shard_map/ppermute | solution.py:519
  16.3 39.5 %collective-permute-start = (bf16[512,384]{1,0:T(8,128)(2,1)S(1)}, bf16[512,384]{1,0:T(8,128)(2,1)S(1)}, u32[]{:S(2)}, u32[]{:S(2)}) collective-permute-start(bf16[512,384]{1,0:T(8,128)(2,1)S(1)} %slice.3), channel_id=1, source_target_pairs={{4,0},{8,4},{12,8},{5,1},{9,5},{13,9},{6,2},{10,6},{14,10},{7,3},{... | collective-permute-start | bytes 1179656 | tf_op jit(solution)/shard_map/ppermute | solution.py:519
  17.6 64.4 %collective-permute-start.4 = (bf16[2,512,384]{2,1,0:T(8,128)(2,1)S(1)}, bf16[2,512,384]{2,1,0:T(8,128)(2,1)S(1)}, u32[]{:S(2)}, u32[]{:S(2)}) collective-permute-start(bf16[2,512,384]{2,1,0:T(8,128)(2,1)S(1)} %get-tuple-element.12), channel_id=1, source_target_pairs={{0,4},{4,8},{8,12},{1,5},{5,9},{9,13},{2,6},{6,10},{10,14},{3,7},{... | collective-permute-start | bytes 2359304 | tf_op jit(solution)/shard_map/ppermute | solution.py:519
  22.9 26.7 %collective-permute-start.5 = (bf16[10,3,32,128]{3,2,1,0:T(8,128)(2,1)S(1)}, bf16[10,3,32,128]{3,2,1,0:T(8,128)(2,1)S(1)}, u32[]{:S(2)}, u32[]{:S(2)}) collective-permute-start(bf16[10,3,32,128]{3,2,1,0:T(8,128)(2,1)S(1)} %get-tuple-element.14), channel_id=1, source_target_pairs={{0,4},{4,0},{8,12},{12,8},{1,5},{5,1},{9,13},{13,9},{2,6},{6,2},{1... | collective-permute-start | bytes 737288 | tf_op jit(solution)/shard_map/ppermute | solution.py:523
  25.0 26.3 %copy-start.4 = (bf16[128,10,3,128]{3,0,2,1:T(8,128)(2,1)S(1)}, bf16[128,10,3,128]{3,0,2,1:T(8,128)(2,1)}, u32[]{:S(2)}) copy-start(bf16[128,10,3,128]{3,0,2,1:T(8,128)(2,1)} %param.10) | copy-start | bytes 2949124
  25.0 26.3 %copy-start.5 = (f32[32,10,3,128]{3,0,2,1:T(8,128)S(1)}, f32[32,10,3,128]{3,0,2,1:T(8,128)}, u32[]{:S(2)}) copy-start(f32[32,10,3,128]{3,0,2,1:T(8,128)} %param.11) | copy-start | bytes 1474564
  25.0 26.3 %collective-permute-start.7 = (bf16[10,3,32,128]{3,2,1,0:T(8,128)(2,1)S(1)}, bf16[10,3,32,128]{3,2,1,0:T(8,128)(2,1)S(1)}, u32[]{:S(2)}, u32[]{:S(2)}) collective-permute-start(bf16[10,3,32,128]{3,2,1,0:T(8,128)(2,1)S(1)} %add_convert_fusion), channel_id=1, source_target_pairs={{0,8},{4,12},{8,0},{12,4},{1,9},{5,13},{9,1},{13,5},{2,10},{6,14},... | collective-permute-start | bytes 737288 | tf_op jit(solution)/shard_map/ppermute | solution.py:523
  34.2 49.7 %collective-permute-start.3 = (bf16[4,136,512]{2,1,0:T(8,128)(2,1)S(1)}, bf16[4,136,512]{2,1,0:T(8,128)(2,1)S(1)}, u32[]{:S(2)}, u32[]{:S(2)}) collective-permute-start(bf16[4,136,512]{2,1,0:T(8,128)(2,1)S(1)} %shard_map.87), channel_id=1, source_target_pairs={{0,4},{4,8},{8,12},{1,5},{5,9},{9,13},{2,6},{6,10},{10,14},{3,7},{... | collective-permute-start | bytes 1671176 | tf_op jit(solution)/shard_map/ppermute | solution.py:519
  52.5 9.4 %copy-start.6 = (bf16[10,3,32,128]{3,2,1,0:T(8,128)(2,1)S(1)}, bf16[10,3,32,128]{3,2,1,0:T(8,128)(2,1)}, u32[]{:S(2)}) copy-start(bf16[10,3,32,128]{3,2,1,0:T(8,128)(2,1)} %get-tuple-element.17.refs_0_) | copy-start | bytes 737284
  52.5 16.2 %collective-permute-start.9 = (bf16[10,3,32,128]{3,2,1,0:T(8,128)(2,1)}, bf16[10,3,32,128]{3,2,1,0:T(8,128)(2,1)S(1)}, u32[]{:S(2)}, u32[]{:S(2)}) collective-permute-start(bf16[10,3,32,128]{3,2,1,0:T(8,128)(2,1)} %get-tuple-element.17.refs_0_), channel_id=1, source_target_pairs={{0,8},{4,12},{8,0},{12,4},{1,9},{5,13},{9,1},{13,5},{2,10},{6,14},... | collective-permute-start | bytes 737288 | tf_op jit(solution)/shard_map/ppermute | solution.py:523
  57.8 29.2 %collective-permute-start.1 = (bf16[3,136,512]{2,1,0:T(8,128)(2,1)S(1)}, bf16[3,136,512]{2,1,0:T(8,128)(2,1)S(1)}, u32[]{:S(2)}, u32[]{:S(2)}) collective-permute-start(bf16[3,136,512]{2,1,0:T(8,128)(2,1)S(1)} %shard_map.85), channel_id=1, source_target_pairs={{0,4},{4,8},{8,12},{1,5},{5,9},{9,13},{2,6},{6,10},{10,14},{3,7},{... | collective-permute-start | bytes 1253384 | tf_op jit(solution)/shard_map/ppermute | solution.py:519
  61.9 27.3 %collective-permute-start.8 = (bf16[10,3,32,128]{3,2,1,0:T(8,128)(2,1)S(1)}, bf16[10,3,32,128]{3,2,1,0:T(8,128)(2,1)S(1)}, u32[]{:S(2)}, u32[]{:S(2)}) collective-permute-start(bf16[10,3,32,128]{3,2,1,0:T(8,128)(2,1)S(1)} %copy-done.6), channel_id=1, source_target_pairs={{0,4},{4,0},{8,12},{12,8},{1,5},{5,1},{9,13},{13,9},{2,6},{6,2},{1... | collective-permute-start | bytes 737288 | tf_op jit(solution)/shard_map/ppermute | solution.py:523
  68.7 20.6 %collective-permute-start.10 = (bf16[10,3,32,128]{3,2,1,0:T(8,128)(2,1)S(1)}, bf16[10,3,32,128]{3,2,1,0:T(8,128)(2,1)S(1)}, u32[]{:S(2)}, u32[]{:S(2)}) collective-permute-start(bf16[10,3,32,128]{3,2,1,0:T(8,128)(2,1)S(1)} %collective-permute-done.9.refs_2_), channel_id=1, source_target_pairs={{0,4},{4,0},{8,12},{12,8},{1,5},{5,1},{9,13},{13,9},{2,6},{6,2},{1... | collective-permute-start | bytes 737288 | tf_op jit(solution)/shard_map/ppermute | solution.py:523

commit v6 on v5

--- a/solution.py
+++ b/solution.py
@@ -112,7 +112,7 @@
     group = steps_of(heads)
     column = pl.BlockSpec((rows, group * size), lambda h, z: (0, h))
     return call(
-        functools.partial(grad_body, peers, group, min(rows, 512)),
+        functools.partial(grad_body, peers, group, min(rows, 256)),
         (heads // group,),
         [
             column,
@@ -126,7 +126,7 @@
         1,
         12 * rows * heads * size * size,
         4 * rows * heads * size,
-    )(z, keys, far(values), far(rates), far(weights))
+    )(z, far(keys), far(values), far(rates), far(weights))
 
 
 def update_body(count, z_ref, w_ref, m_ref, *refs):
@@ -270,7 +270,7 @@
             bytes_accessed=8 * rows * size * group,
             transcendentals=0,
         ),
-    )(queries, keys, values, *more)
+    )(far(queries), far(keys), far(values), *more)
 
 
 def carried_body(group, z_ref, q_ref, k_ref, v_ref, p_ref, o_ref, s_ref):
@@ -315,7 +315,7 @@
 
 EXTRA = 8
 KEPT = 3
-EARLY = 4
+EARLY = 5
 
 
 def put_partial(o_ref, g, t, size):
@@ -427,14 +427,14 @@
     )(z, queries, keys, values, given, partly)
 
 
-def final_body(peers, group, z_ref, q_ref, first_ref, later_ref, *refs):
-    blocks, o_ref, whole = refs[:peers], refs[peers], refs[peers + 1]
+def final_body(peers, group, start, z_ref, q_ref, first_ref, later_ref, *refs):
+    blocks, o_ref, whole = refs[:peers], refs[-2], refs[-1]
     size = q_ref.shape[1] // group
     own = blocks[0].shape[2]
-    start = pl.program_id(0) * group
     for m in range(peers):
         row = pl.multiple_of((z_ref[0] ^ m) * own, own)
-        whole[:, :, pl.ds(row, own), :] = blocks[m][pl.ds(start, group)].astype(whole.dtype)
+        base = start if m + 1 < peers else 0
+        whole[:, :, pl.ds(row, own), :] = blocks[m][base : base + group].astype(whole.dtype)
     tasks = [(g, c) for g in range(group) for c in range(0, q_ref.shape[0], WIN)]
 
     def products(g, c):
@@ -457,29 +457,36 @@
         ready = following
 
 
-def final(z, queries, first, later, blocks, size):
+def final(z, queries, first, later, blocks, size, step, group, partly):
     rows, width = queries.shape
-    heads = width // size
-    group = steps_of(heads)
     peers, own = len(blocks), blocks[0].shape[2]
-    column = pl.BlockSpec((rows, group * size), lambda h, z: (0, h))
     kind = jnp.bfloat16 if own % 16 == 0 else jnp.float32
-    return call(
-        functools.partial(final_body, peers, group),
-        (heads // group,),
-        [
-            column,
-            pl.BlockSpec((WIN, group * size), lambda h, z: (0, h)),
-            pl.BlockSpec((rows - WIN, group * size), lambda h, z: (0, h)),
-        ]
-        + [VMEM] * peers,
-        column,
-        jax.ShapeDtypeStruct((rows, width), jnp.bfloat16),
-        [pltpu.VMEM((group, 3, size, size), kind)],
-        1,
-        6 * rows * width * size,
-        6 * rows * width,
-    )(z, queries, first, later, *blocks)
+    more = [] if partly is None else [partly]
+    return pl.pallas_call(
+        functools.partial(final_body, peers, group, step * group),
+        name="final",
+        out_shape=jax.ShapeDtypeStruct((rows, width), jnp.bfloat16),
+        grid_spec=pltpu.PrefetchScalarGridSpec(
+            num_scalar_prefetch=1,
+            grid=(1,),
+            in_specs=[
+                pl.BlockSpec((rows, group * size), lambda h, z: (0, step)),
+                pl.BlockSpec((WIN, group * size), lambda h, z: (0, step)),
+                pl.BlockSpec((rows - WIN, group * size), lambda h, z: (0, step)),
+            ]
+            + [VMEM] * peers
+            + [pl.BlockSpec(memory_space=pl.ANY)] * len(more),
+            out_specs=pl.BlockSpec((rows, group * size), lambda h, z: (0, step)),
+            scratch_shapes=[pltpu.VMEM((group, 3, size, size), kind)],
+        ),
+        compiler_params=PARAMS,
+        input_output_aliases={4 + peers: 0} if more else {},
+        cost_estimate=pl.CostEstimate(
+            flops=6 * rows * group * size * size,
+            bytes_accessed=6 * rows * group * size,
+            transcendentals=0,
+        ),
+    )(z, queries, first, later, *blocks, *more)
 
 
 def pack_body(first, q_ref, k_ref, v_ref, ask_ref, carry_ref, sems):
@@ -572,11 +579,15 @@
     step = peers // 2
     while step:
         for m in sorted(blocks):
-            blocks[m + step] = swapped(blocks[m], step)
+            if m + step < peers - 1:
+                blocks[m + step] = swapped(blocks[m], step)
         step //= 2
-    blocks = [blocks[m] for m in range(peers)]
-
-    mixed = final(z, queries, first, later, blocks, size)
+
+    mixed = None
+    for part in range(heads // group):
+        last = swapped(blocks[peers - 2][part * group : (part + 1) * group], 1)
+        parts = [blocks[m] for m in range(peers - 1)] + [last]
+        mixed = final(z, queries, first, later, parts, size, part, group, mixed)
     return (mixed, jnp.transpose(new_rows, (2, 0, 1, 3)), jnp.transpose(new_momentum, (2, 0, 1, 3)))
 
 

time: 94.2 us -> 89.2 us (0.947)
  waiting for transfers between devices: 26.6 us -> 20.1 us
  Pallas kernels: 32.8 us -> 36.9 us
  starting transfers between devices: 31.7 us -> 29.8 us
    ppermute x5, waiting for transfers between devices: 5.99 us -> 0.01 us  [moved_by(): return lax.ppermute(value, 'seq', pairs)]
    ppermute x5, starting transfers between devices: 15.2 us -> 10.3 us  [moved_by(): return lax.ppermute(value, 'seq', pairs)]
    pallas_call x2, Pallas kernels: 6.04 us -> 9.88 us  [later_blocks(): pl.pallas_call(functools.partial(later_body, group), name='later', out_sh...]
    ppermute x6 -> x7, starting transfers between devices: 16.6 us -> 19.5 us  [swapped(): lax.ppermute(value, 'seq', [(i, i ^ mask) for i in range(lax.axis_size('s...]
    unnamed x14 -> x16, local copies, waits for them, and re-layouts: 1.77 us -> 0.05 us
    pallas_call x2 -> x3, Pallas kernels: 12.6 us -> 13.7 us  [the longest x1 8.3 us: partial_grads(): call(functools.partial(grad_body, peers, group, min(rows, 256)), (heads /...]
    ppermute x6 -> x7, waiting for transfers between devices: 20.7 us -> 20.1 us  [swapped(): lax.ppermute(value, 'seq', [(i, i ^ mask) for i in range(lax.axis_size('s...]
  transfers between devices with their start and end apart: 11 -> 12, of which waited for: 4 -> 5; matrix products, arithmetic and copies ran while one was open for 0% -> 1% of each run, Pallas kernels for 22% -> 37%
where the time goes in v6:
time: 89.2 us; the launch traced here: 88.9 us
  Pallas kernels  36.9 us (41%)
  starting transfers between devices  29.8 us (33%)
  waiting for transfers between devices  20.1 us (23%)
  local copies, waits for them, and re-layouts  1.04 us (1%)
    ppermute x7, waiting for transfers between devices, swapped(): lax.ppermute(value, 'seq', [(i, i ^ mask) for i in range(lax.axis_size('s...  20.1 us
    ppermute x7, starting transfers between devices, swapped(): lax.ppermute(value, 'seq', [(i, i ^ mask) for i in range(lax.axis_size('s...  19.5 us
    ppermute x5, starting transfers between devices, moved_by(): return lax.ppermute(value, 'seq', pairs)  10.3 us
    pallas_call x2, Pallas kernels, later_blocks(): pl.pallas_call(functools.partial(later_body, group), name='later', out_sh...  9.88 us
    pallas_call x1, Pallas kernels, partial_grads(): call(functools.partial(grad_body, peers, group, min(rows, 256)), (heads /...  8.3 us
    pallas_call x2, Pallas kernels, final(): pl.pallas_call(functools.partial(final_body, peers, group, step * group),...  5.43 us
    pallas_call x2, Pallas kernels, joined_block(): pl.pallas_call(functools.partial(joined_body, group), name='joined', out_...  4.73 us
    pallas_call x2, Pallas kernels, next_part(): call(functools.partial(next_part_body, group), (heads // group,), [pl.Blo...  4.11 us
  transfers between devices with their start and end apart: 12, of which 5 were waited for; matrix products, arithmetic and copies ran while one was open for 1% of the time, Pallas kernels for 37%

profile of v6, /device:TPU:0, one launch (start us, length us, event | category | flops | bytes accessed | tf_op | source)
XLA Modules:
  0.0 88.9 jit_solution(1015374605387754748)
XLA Ops:
  0.6 1.4 %shard_map.86 = (bf16[512,640]{1,0:T(8,128)(2,1)S(1)}, bf16[2,512,384]{2,1,0:T(8,128)(2,1)S(1)}) custom-call(bf16[1024,1280]{1,0:T(8,128)(2,1)} %q_ref.15, bf16[1024,1280]{1,0:T(8,128)(2,1)} %k_ref.17, bf16[1024,1280]{1,0:T(8,128)(2,1)} %v_ref.17), custom_call_target="tpu_custom_call" | custom-call | bytes 2883584 | tf_op jit(solution)/shard_map/pallas_call | solution.py:510
  2.0 1.3 %collective-permute-start.2 = (bf16[512,640]{1,0:T(8,128)(2,1)S(1)}, bf16[512,640]{1,0:T(8,128)(2,1)S(1)}, u32[]{:S(2)}, u32[]{:S(2)}) collective-permute-start(bf16[512,640]{1,0:T(8,128)(2,1)S(1)} %get-tuple-element.11), channel_id=1, source_target_pairs={{4,0},{8,4},{12,8},{5,1},{9,5},{13,9},{6,2},{10,6},{14,10},{7,3},{... | collective-permute-start | bytes 1966088 | tf_op jit(solution)/shard_map/ppermute | solution.py:526
  3.3 0.0 copy-start.3
  3.3 8.3 %shard_map.89 = (f32[10,3,32,128]{3,2,1,0:T(8,128)S(1)}, bf16[10,3,32,128]{3,2,1,0:T(8,128)(2,1)S(1)}, f32[10,3,32,128]{3,2,1,0:T(8,128)S(1)}, bf16[10,3,32,128]{3,2,1,0:T(8,128)(2,1)S(1)}) custom-call(s32[1]{0:T(128)} %bitcast.z_ref, bf16[1024,1280]{1,0:T(8,128)(2,1)} %k_ref.17, bf16[1024,1280]{1,0:T(8,128)(2,1)} %v_ref.17, f32[10,1024]{1,0:T(8,128)} %r_ref.1, ...), custom_call_target="tpu_custom_call" | custom-call | flops 2013265920 | bytes 5242880 | tf_op jit(solution)/shard_map/pallas_call | solution.py:114
  11.6 3.7 %collective-permute-start.6 = (bf16[10,3,32,128]{3,2,1,0:T(8,128)(2,1)S(1)}, bf16[10,3,32,128]{3,2,1,0:T(8,128)(2,1)S(1)}, u32[]{:S(2)}, u32[]{:S(2)}) collective-permute-start(bf16[10,3,32,128]{3,2,1,0:T(8,128)(2,1)S(1)} %get-tuple-element.16), channel_id=1, source_target_pairs={{0,4},{4,0},{8,12},{12,8},{1,5},{5,1},{9,13},{13,9},{2,6},{6,2},{1... | collective-permute-start | bytes 737288 | tf_op jit(solution)/shard_map/ppermute | solution.py:530
  15.4 2.0 %collective-permute-start.4 = (bf16[2,512,384]{2,1,0:T(8,128)(2,1)S(1)}, bf16[2,512,384]{2,1,0:T(8,128)(2,1)S(1)}, u32[]{:S(2)}, u32[]{:S(2)}) collective-permute-start(bf16[2,512,384]{2,1,0:T(8,128)(2,1)S(1)} %get-tuple-element.12), channel_id=1, source_target_pairs={{0,4},{4,8},{8,12},{1,5},{5,9},{9,13},{2,6},{6,10},{10,14},{3,7},{... | collective-permute-start | bytes 2359304 | tf_op jit(solution)/shard_map/ppermute | solution.py:526
  17.4 3.6 %collective-permute-start.5 = (bf16[10,3,32,128]{3,2,1,0:T(8,128)(2,1)S(1)}, bf16[10,3,32,128]{3,2,1,0:T(8,128)(2,1)S(1)}, u32[]{:S(2)}, u32[]{:S(2)}) collective-permute-start(bf16[10,3,32,128]{3,2,1,0:T(8,128)(2,1)S(1)} %get-tuple-element.14), channel_id=1, source_target_pairs={{0,4},{4,0},{8,12},{12,8},{1,5},{5,1},{9,13},{13,9},{2,6},{6,2},{1... | collective-permute-start | bytes 737288 | tf_op jit(solution)/shard_map/ppermute | solution.py:530
  21.0 6.8 %collective-permute-done.6 = bf16[10,3,32,128]{3,2,1,0:T(8,128)(2,1)S(1)} collective-permute-done((bf16[10,3,32,128]{3,2,1,0:T(8,128)(2,1)S(1)}, bf16[10,3,32,128]{3,2,1,0:T(8,128)(2,1)S(1)}, u32[]{:S(2)}, u32[]{:S(2)}) %collective-permute-start.6) | collective-permute-done | bytes 245792 | tf_op jit(solution)/shard_map/ppermute | solution.py:530
  27.8 0.1 add_convert_fusion
  27.9 3.1 %collective-permute-start.7 = (bf16[10,3,32,128]{3,2,1,0:T(8,128)(2,1)S(1)}, bf16[10,3,32,128]{3,2,1,0:T(8,128)(2,1)S(1)}, u32[]{:S(2)}, u32[]{:S(2)}) collective-permute-start(bf16[10,3,32,128]{3,2,1,0:T(8,128)(2,1)S(1)} %add_convert_fusion), channel_id=1, source_target_pairs={{0,8},{4,12},{8,0},{12,4},{1,9},{5,13},{9,1},{13,5},{2,10},{6,14},... | collective-permute-start | bytes 737288 | tf_op jit(solution)/shard_map/ppermute | solution.py:530
  31.0 3.2 %shard_map.87 = bf16[5,136,512]{2,1,0:T(8,128)(2,1)S(1)} custom-call(bf16[512,640]{1,0:T(8,128)(2,1)S(1)} %collective-permute-done.2.q_ref, bf16[1024,1280]{1,0:T(8,128)(2,1)S(1)} %copy-done.1, bf16[1024,1280]{1,0:T(8,128)(2,1)S(1)} %copy-done.3), custom_call_target="tpu_custom_call" | custom-call | flops 671088640 | bytes 2621440 | tf_op jit(solution)/shard_map/pallas_call | solution.py:358
  34.2 1.5 %collective-permute-start.3 = (bf16[5,136,512]{2,1,0:T(8,128)(2,1)S(1)}, bf16[5,136,512]{2,1,0:T(8,128)(2,1)S(1)}, u32[]{:S(2)}, u32[]{:S(2)}) collective-permute-start(bf16[5,136,512]{2,1,0:T(8,128)(2,1)S(1)} %shard_map.87), channel_id=1, source_target_pairs={{0,4},{4,8},{8,12},{1,5},{5,9},{9,13},{2,6},{6,10},{10,14},{3,7},{... | collective-permute-start | bytes 2088968 | tf_op jit(solution)/shard_map/ppermute | solution.py:526
  35.7 1.0 %slice.9 = bf16[512,256]{1,0:T(8,128)(2,1)S(1)} slice(bf16[1024,1280]{1,0:T(8,128)(2,1)} %q_ref.15), slice={[0:512], [1024:1280]} | slice | bytes 524288 | tf_op jit(solution)/shard_map/slice | solution.py:548
  36.6 1.3 %collective-permute-start = (bf16[512,256]{1,0:T(8,128)(2,1)S(1)}, bf16[512,256]{1,0:T(8,128)(2,1)S(1)}, u32[]{:S(2)}, u32[]{:S(2)}) collective-permute-start(bf16[512,256]{1,0:T(8,128)(2,1)S(1)} %slice.9), channel_id=1, source_target_pairs={{4,0},{8,4},{12,8},{5,1},{9,5},{13,9},{6,2},{10,6},{14,10},{7,3},{... | collective-permute-start | bytes 786440 | tf_op jit(solution)/shard_map/ppermute | solution.py:526
  37.9 5.9 %collective-permute-done.5.refs_1_ = bf16[10,3,32,128]{3,2,1,0:T(8,128)(2,1)S(1)} collective-permute-done((bf16[10,3,32,128]{3,2,1,0:T(8,128)(2,1)S(1)}, bf16[10,3,32,128]{3,2,1,0:T(8,128)(2,1)S(1)}, u32[]{:S(2)}, u32[]{:S(2)}) %collective-permute-start.5) | collective-permute-done | bytes 245792 | tf_op jit(solution)/shard_map/ppermute | solution.py:530
  43.9 5.3 %collective-permute-done.7.refs_2_ = bf16[10,3,32,128]{3,2,1,0:T(8,128)(2,1)S(1)} collective-permute-done((bf16[10,3,32,128]{3,2,1,0:T(8,128)(2,1)S(1)}, bf16[10,3,32,128]{3,2,1,0:T(8,128)(2,1)S(1)}, u32[]{:S(2)}, u32[]{:S(2)}) %collective-permute-start.7) | collective-permute-done | bytes 245792 | tf_op jit(solution)/shard_map/ppermute | solution.py:530
  49.2 1.2 %shard_map.90 = (bf16[10,3,32,128]{3,2,1,0:T(8,128)(2,1)}, f32[10,3,32,128]{3,2,1,0:T(8,128)}) custom-call(s32[1]{0:T(128)} %bitcast.z_ref, bf16[10,3,128,128]{3,2,1,0:T(8,128)(2,1)S(1)} %bitcast.6, f32[10,3,32,128]{3,2,1,0:T(8,128)S(1)} %bitcast.8, f32[10,3,32,128]{3,2,1,0:T(8,128)S(1)} %get-tuple-element.13.refs_0_, ...), custom_call_target="tpu_custom_call" | custom-call | flops 2457600 | bytes 1966080 | tf_op jit(solution)/shard_map/pallas_call | solution.py:152
  50.3 3.4 %collective-permute-start.9 = (bf16[10,3,32,128]{3,2,1,0:T(8,128)(2,1)}, bf16[10,3,32,128]{3,2,1,0:T(8,128)(2,1)S(1)}, u32[]{:S(2)}, u32[]{:S(2)}) collective-permute-start(bf16[10,3,32,128]{3,2,1,0:T(8,128)(2,1)} %get-tuple-element.17.refs_0_), channel_id=1, source_target_pairs={{0,8},{4,12},{8,0},{12,4},{1,9},{5,13},{9,1},{13,5},{2,10},{6,14},... | collective-permute-start | bytes 737288 | tf_op jit(solution)/shard_map/ppermute | solution.py:530
  53.7 4.9 %later.2.refs_0_ = bf16[512,1280]{1,0:T(8,128)(2,1)S(1)} custom-call(bf16[1024,1280]{1,0:T(8,128)(2,1)} %q_ref.15, bf16[1024,1280]{1,0:T(8,128)(2,1)} %k_ref.17, bf16[1024,1280]{1,0:T(8,128)(2,1)} %v_ref.17), custom_call_target="tpu_custom_call" | custom-call | flops 1006632960 | bytes 5242880 | tf_op jit(solution)/shard_map/later/pallas_call | solution.py:255
  58.6 5.0 %later.3.later_ref = bf16[512,1280]{1,0:T(8,128)(2,1)S(1)} custom-call(bf16[1024,1280]{1,0:T(8,128)(2,1)} %q_ref.15, bf16[1024,1280]{1,0:T(8,128)(2,1)} %k_ref.17, bf16[1024,1280]{1,0:T(8,128)(2,1)} %v_ref.17, bf16[512,1280]{1,0:T(8,128)(2,1)S(1)} %later.2.refs_0_), custom_call_target="tpu_custom_call", output_to_operand_aliasing={{}: (3, {})} | custom-call | flops 1006632960 | bytes 5242880 | tf_op jit(solution)/shard_map/later/pallas_call | solution.py:255
  63.7 0.9 %shard_map.85 = bf16[2,136,512]{2,1,0:T(8,128)(2,1)S(1)} custom-call(bf16[512,256]{1,0:T(8,128)(2,1)S(1)} %collective-permute-done.q_ref, bf16[1024,1280]{1,0:T(8,128)(2,1)S(1)} %copy-done.2, bf16[1024,1280]{1,0:T(8,128)(2,1)S(1)} %copy-done.4), custom_call_target="tpu_custom_call" | custom-call | flops 268435456 | bytes 1048576 | tf_op jit(solution)/shard_map/pallas_call | solution.py:358
  64.6 4.2 %collective-permute-start.1 = (bf16[2,136,512]{2,1,0:T(8,128)(2,1)S(1)}, bf16[2,136,512]{2,1,0:T(8,128)(2,1)S(1)}, u32[]{:S(2)}, u32[]{:S(2)}) collective-permute-start(bf16[2,136,512]{2,1,0:T(8,128)(2,1)S(1)} %shard_map.85), channel_id=1, source_target_pairs={{0,4},{4,8},{8,12},{1,5},{5,9},{9,13},{2,6},{6,10},{10,14},{3,7},{... | collective-permute-start | bytes 835592 | tf_op jit(solution)/shard_map/ppermute | solution.py:526
  68.9 0.1 collective-permute-start.8
  69.0 0.5 collective-permute-done.9.refs_2_
  69.5 5.5 %collective-permute-start.11 = (bf16[5,3,32,128]{3,2,1,0:T(8,128)(2,1)S(1)}, bf16[5,3,32,128]{3,2,1,0:T(8,128)(2,1)S(1)}, u32[]{:S(2)}, u32[]{:S(2)}) collective-permute-start(bf16[5,3,32,128]{3,2,1,0:T(8,128)(2,1)S(1)} %get-tuple-element.19), channel_id=1, source_target_pairs={{0,4},{4,0},{8,12},{12,8},{1,5},{5,1},{9,13},{13,9},{2,6},{6,2},{1... | collective-permute-start | bytes 368648 | tf_op jit(solution)/shard_map/ppermute | solution.py:530
  75.1 0.1 collective-permute-start.10
  75.1 1.9 %shard_map.88._ = bf16[512,1280]{1,0:T(8,128)(2,1)S(1)} custom-call(s32[1]{0:T(128)} %bitcast.z_ref, bf16[1024,1280]{1,0:T(8,128)(2,1)S(1)} %copy-done, bf16[1024,1280]{1,0:T(8,128)(2,1)S(1)} %copy-done.2, bf16[1024,1280]{1,0:T(8,128)(2,1)S(1)} %copy-done.4, bf16[2,512,384]{2,1,0:T(8,128)(2,1)S(1)} %collective-permute-done.4.p_ref), custom_call_target="tpu_custom_call" | custom-call | flops 603979776 | bytes 1966080 | tf_op jit(solution)/shard_map/pallas_call | solution.py:303
  77.1 3.7 %joined.2._ = bf16[512,1280]{1,0:T(8,128)(2,1)S(1)} custom-call(s32[1]{0:T(128)} %bitcast.z_ref, bf16[1024,1280]{1,0:T(8,128)(2,1)S(1)} %copy-done, bf16[1024,1280]{1,0:T(8,128)(2,1)S(1)} %copy-done.2, bf16[1024,1280]{1,0:T(8,128)(2,1)S(1)} %copy-done.4, bf16[5,136,512]{2,1,0:T(8,128)(2,1)S(1)} %collective-permute-done.3.p_ref, ...), custom_call_target="tpu_custom_call", output_to_operand_aliasing={{}: (5, {})} | custom-call | flops 671088640 | bytes 3276800 | tf_op jit(solution)/shard_map/joined/pallas_call | solution.py:405
  80.8 1.0 %joined.3.first_ref = bf16[512,1280]{1,0:T(8,128)(2,1)S(1)} custom-call(s32[1]{0:T(128)} %bitcast.z_ref, bf16[1024,1280]{1,0:T(8,128)(2,1)S(1)} %copy-done, bf16[1024,1280]{1,0:T(8,128)(2,1)S(1)} %copy-done.2, bf16[1024,1280]{1,0:T(8,128)(2,1)S(1)} %copy-done.4, ...), custom_call_target="tpu_custom_call", output_to_operand_aliasing={{}: (5, {})} | custom-call | flops 268435456 | bytes 1310720 | tf_op jit(solution)/shard_map/joined/pallas_call | solution.py:405
  81.9 1.6 %collective-permute-done.11.refs_3_ = bf16[5,3,32,128]{3,2,1,0:T(8,128)(2,1)S(1)} collective-permute-done((bf16[5,3,32,128]{3,2,1,0:T(8,128)(2,1)S(1)}, bf16[5,3,32,128]{3,2,1,0:T(8,128)(2,1)S(1)}, u32[]{:S(2)}, u32[]{:S(2)}) %collective-permute-start.11) | collective-permute-done | bytes 122912 | tf_op jit(solution)/shard_map/ppermute | solution.py:530
  83.4 2.7 %final.2.refs_4_ = bf16[1024,1280]{1,0:T(8,128)(2,1)} custom-call(s32[1]{0:T(128)} %bitcast.z_ref, bf16[1024,1280]{1,0:T(8,128)(2,1)S(1)} %copy-done, bf16[512,1280]{1,0:T(8,128)(2,1)S(1)} %joined.3.first_ref, bf16[512,1280]{1,0:T(8,128)(2,1)S(1)} %later.3.later_ref, bf16[10,3,32,128]{3,2,1,0:T(8,128)(2,1)S(1)} %copy-done.6, ...), custom_call_target="tpu_custom_call" | custom-call | flops 503316480 | bytes 3932160 | tf_op jit(solution)/shard_map/final/pallas_call | solution.py:465
  86.2 2.7 %final.3 = bf16[1024,1280]{1,0:T(8,128)(2,1)} custom-call(s32[1]{0:T(128)} %bitcast.z_ref, bf16[1024,1280]{1,0:T(8,128)(2,1)S(1)} %copy-done, bf16[512,1280]{1,0:T(8,128)(2,1)S(1)} %joined.3.first_ref, bf16[512,1280]{1,0:T(8,128)(2,1)S(1)} %later.3.later_ref, bf16[10,3,32,128]{3,2,1,0:T(8,128)(2,1)S(1)} %copy-done.6, ...), custom_call_target="tpu_custom_call", output_to_operand_aliasing={{}: (8, {})} | custom-call | flops 503316480 | bytes 3932160 | tf_op jit(solution)/shard_map/final/pallas_call | solution.py:465
  (23 shorter events, 0.1 us)
Async XLA Ops:
  2.0 29.0 %collective-permute-start.2 = (bf16[512,640]{1,0:T(8,128)(2,1)S(1)}, bf16[512,640]{1,0:T(8,128)(2,1)S(1)}, u32[]{:S(2)}, u32[]{:S(2)}) collective-permute-start(bf16[512,640]{1,0:T(8,128)(2,1)S(1)} %get-tuple-element.11), channel_id=1, source_target_pairs={{4,0},{8,4},{12,8},{5,1},{9,5},{13,9},{6,2},{10,6},{14,10},{7,3},{... | collective-permute-start | bytes 1966088 | tf_op jit(solution)/shard_map/ppermute | solution.py:526
  3.3 27.7 %copy-start.1 = (bf16[1024,1280]{1,0:T(8,128)(2,1)S(1)}, bf16[1024,1280]{1,0:T(8,128)(2,1)}, u32[]{:S(2)}) copy-start(bf16[1024,1280]{1,0:T(8,128)(2,1)} %k_ref.17) | copy-start | bytes 7864324
  3.3 27.7 %copy-start.3 = (bf16[1024,1280]{1,0:T(8,128)(2,1)S(1)}, bf16[1024,1280]{1,0:T(8,128)(2,1)}, u32[]{:S(2)}) copy-start(bf16[1024,1280]{1,0:T(8,128)(2,1)} %v_ref.17) | copy-start | bytes 7864324
  11.6 16.2 %collective-permute-start.6 = (bf16[10,3,32,128]{3,2,1,0:T(8,128)(2,1)S(1)}, bf16[10,3,32,128]{3,2,1,0:T(8,128)(2,1)S(1)}, u32[]{:S(2)}, u32[]{:S(2)}) collective-permute-start(bf16[10,3,32,128]{3,2,1,0:T(8,128)(2,1)S(1)} %get-tuple-element.16), channel_id=1, source_target_pairs={{0,4},{4,0},{8,12},{12,8},{1,5},{5,1},{9,13},{13,9},{2,6},{6,2},{1... | collective-permute-start | bytes 737288 | tf_op jit(solution)/shard_map/ppermute | solution.py:530
  15.4 59.7 %collective-permute-start.4 = (bf16[2,512,384]{2,1,0:T(8,128)(2,1)S(1)}, bf16[2,512,384]{2,1,0:T(8,128)(2,1)S(1)}, u32[]{:S(2)}, u32[]{:S(2)}) collective-permute-start(bf16[2,512,384]{2,1,0:T(8,128)(2,1)S(1)} %get-tuple-element.12), channel_id=1, source_target_pairs={{0,4},{4,8},{8,12},{1,5},{5,9},{9,13},{2,6},{6,10},{10,14},{3,7},{... | collective-permute-start | bytes 2359304 | tf_op jit(solution)/shard_map/ppermute | solution.py:526
  17.4 26.5 %collective-permute-start.5 = (bf16[10,3,32,128]{3,2,1,0:T(8,128)(2,1)S(1)}, bf16[10,3,32,128]{3,2,1,0:T(8,128)(2,1)S(1)}, u32[]{:S(2)}, u32[]{:S(2)}) collective-permute-start(bf16[10,3,32,128]{3,2,1,0:T(8,128)(2,1)S(1)} %get-tuple-element.14), channel_id=1, source_target_pairs={{0,4},{4,0},{8,12},{12,8},{1,5},{5,1},{9,13},{13,9},{2,6},{6,2},{1... | collective-permute-start | bytes 737288 | tf_op jit(solution)/shard_map/ppermute | solution.py:530
  27.9 21.3 %copy-start.5 = (bf16[128,10,3,128]{3,0,2,1:T(8,128)(2,1)S(1)}, bf16[128,10,3,128]{3,0,2,1:T(8,128)(2,1)}, u32[]{:S(2)}) copy-start(bf16[128,10,3,128]{3,0,2,1:T(8,128)(2,1)} %param.10) | copy-start | bytes 2949124
  27.9 21.3 %copy-start.7 = (f32[32,10,3,128]{3,0,2,1:T(8,128)S(1)}, f32[32,10,3,128]{3,0,2,1:T(8,128)}, u32[]{:S(2)}) copy-start(f32[32,10,3,128]{3,0,2,1:T(8,128)} %param.11) | copy-start | bytes 1474564
  27.9 21.3 %collective-permute-start.7 = (bf16[10,3,32,128]{3,2,1,0:T(8,128)(2,1)S(1)}, bf16[10,3,32,128]{3,2,1,0:T(8,128)(2,1)S(1)}, u32[]{:S(2)}, u32[]{:S(2)}) collective-permute-start(bf16[10,3,32,128]{3,2,1,0:T(8,128)(2,1)S(1)} %add_convert_fusion), channel_id=1, source_target_pairs={{0,8},{4,12},{8,0},{12,4},{1,9},{5,13},{9,1},{13,5},{2,10},{6,14},... | collective-permute-start | bytes 737288 | tf_op jit(solution)/shard_map/ppermute | solution.py:530
  34.2 42.9 %collective-permute-start.3 = (bf16[5,136,512]{2,1,0:T(8,128)(2,1)S(1)}, bf16[5,136,512]{2,1,0:T(8,128)(2,1)S(1)}, u32[]{:S(2)}, u32[]{:S(2)}) collective-permute-start(bf16[5,136,512]{2,1,0:T(8,128)(2,1)S(1)} %shard_map.87), channel_id=1, source_target_pairs={{0,4},{4,8},{8,12},{1,5},{5,9},{9,13},{2,6},{6,10},{10,14},{3,7},{... | collective-permute-start | bytes 2088968 | tf_op jit(solution)/shard_map/ppermute | solution.py:526
  36.6 27.0 %collective-permute-start = (bf16[512,256]{1,0:T(8,128)(2,1)S(1)}, bf16[512,256]{1,0:T(8,128)(2,1)S(1)}, u32[]{:S(2)}, u32[]{:S(2)}) collective-permute-start(bf16[512,256]{1,0:T(8,128)(2,1)S(1)} %slice.9), channel_id=1, source_target_pairs={{4,0},{8,4},{12,8},{5,1},{9,5},{13,9},{6,2},{10,6},{14,10},{7,3},{... | collective-permute-start | bytes 786440 | tf_op jit(solution)/shard_map/ppermute | solution.py:526
  50.3 19.2 %collective-permute-start.9 = (bf16[10,3,32,128]{3,2,1,0:T(8,128)(2,1)}, bf16[10,3,32,128]{3,2,1,0:T(8,128)(2,1)S(1)}, u32[]{:S(2)}, u32[]{:S(2)}) collective-permute-start(bf16[10,3,32,128]{3,2,1,0:T(8,128)(2,1)} %get-tuple-element.17.refs_0_), channel_id=1, source_target_pairs={{0,8},{4,12},{8,0},{12,4},{1,9},{5,13},{9,1},{13,5},{2,10},{6,14},... | collective-permute-start | bytes 737288 | tf_op jit(solution)/shard_map/ppermute | solution.py:530
  58.6 5.1 %copy-start.2 = (bf16[1024,1280]{1,0:T(8,128)(2,1)S(1)}, bf16[1024,1280]{1,0:T(8,128)(2,1)}, u32[]{:S(2)}) copy-start(bf16[1024,1280]{1,0:T(8,128)(2,1)} %k_ref.17) | copy-start | bytes 7864324
  58.6 5.1 %copy-start.4 = (bf16[1024,1280]{1,0:T(8,128)(2,1)S(1)}, bf16[1024,1280]{1,0:T(8,128)(2,1)}, u32[]{:S(2)}) copy-start(bf16[1024,1280]{1,0:T(8,128)(2,1)} %v_ref.17) | copy-start | bytes 7864324
  63.6 5.2 %copy-start.6 = (bf16[10,3,32,128]{3,2,1,0:T(8,128)(2,1)S(1)}, bf16[10,3,32,128]{3,2,1,0:T(8,128)(2,1)}, u32[]{:S(2)}) copy-start(bf16[10,3,32,128]{3,2,1,0:T(8,128)(2,1)} %get-tuple-element.17.refs_0_) | copy-start | bytes 737284
  63.7 11.5 %copy-start = (bf16[1024,1280]{1,0:T(8,128)(2,1)S(1)}, bf16[1024,1280]{1,0:T(8,128)(2,1)}, u32[]{:S(2)}) copy-start(bf16[1024,1280]{1,0:T(8,128)(2,1)} %q_ref.15) | copy-start | bytes 7864324
  64.6 16.2 %collective-permute-start.1 = (bf16[2,136,512]{2,1,0:T(8,128)(2,1)S(1)}, bf16[2,136,512]{2,1,0:T(8,128)(2,1)S(1)}, u32[]{:S(2)}, u32[]{:S(2)}) collective-permute-start(bf16[2,136,512]{2,1,0:T(8,128)(2,1)S(1)} %shard_map.85), channel_id=1, source_target_pairs={{0,4},{4,8},{8,12},{1,5},{5,9},{9,13},{2,6},{6,10},{10,14},{3,7},{... | collective-permute-start | bytes 835592 | tf_op jit(solution)/shard_map/ppermute | solution.py:526
  68.9 13.0 %collective-permute-start.8 = (bf16[10,3,32,128]{3,2,1,0:T(8,128)(2,1)S(1)}, bf16[10,3,32,128]{3,2,1,0:T(8,128)(2,1)S(1)}, u32[]{:S(2)}, u32[]{:S(2)}) collective-permute-start(bf16[10,3,32,128]{3,2,1,0:T(8,128)(2,1)S(1)} %copy-done.6), channel_id=1, source_target_pairs={{0,4},{4,0},{8,12},{12,8},{1,5},{5,1},{9,13},{13,9},{2,6},{6,2},{1... | collective-permute-start | bytes 737288 | tf_op jit(solution)/shard_map/ppermute | solution.py:530
  69.5 13.9 %collective-permute-start.11 = (bf16[5,3,32,128]{3,2,1,0:T(8,128)(2,1)S(1)}, bf16[5,3,32,128]{3,2,1,0:T(8,128)(2,1)S(1)}, u32[]{:S(2)}, u32[]{:S(2)}) collective-permute-start(bf16[5,3,32,128]{3,2,1,0:T(8,128)(2,1)S(1)} %get-tuple-element.19), channel_id=1, source_target_pairs={{0,4},{4,0},{8,12},{12,8},{1,5},{5,1},{9,13},{13,9},{2,6},{6,2},{1... | collective-permute-start | bytes 368648 | tf_op jit(solution)/shard_map/ppermute | solution.py:530
  75.1 11.1 %collective-permute-start.10 = (bf16[5,3,32,128]{3,2,1,0:T(8,128)(2,1)S(1)}, bf16[5,3,32,128]{3,2,1,0:T(8,128)(2,1)S(1)}, u32[]{:S(2)}, u32[]{:S(2)}) collective-permute-start(bf16[5,3,32,128]{3,2,1,0:T(8,128)(2,1)S(1)} %get-tuple-element.20), channel_id=1, source_target_pairs={{0,4},{4,0},{8,12},{12,8},{1,5},{5,1},{9,13},{13,9},{2,6},{6,2},{1... | collective-permute-start | bytes 368648 | tf_op jit(solution)/shard_map/ppermute | solution.py:530

commit v7 on v6

--- a/solution.py
+++ b/solution.py
@@ -270,7 +270,7 @@
             bytes_accessed=8 * rows * size * group,
             transcendentals=0,
         ),
-    )(far(queries), far(keys), far(values), *more)
+    )(*[x if more else far(x) for x in (queries, keys, values)], *more)
 
 
 def carried_body(group, z_ref, q_ref, k_ref, v_ref, p_ref, o_ref, s_ref):
@@ -333,8 +333,9 @@
     return emit
 
 
-def next_part_body(group, q_ref, k_ref, v_ref, o_ref, s_ref):
-    size = q_ref.shape[1] // group
+def next_part_body(group, skip, q_ref, k_ref, v_ref, o_ref, s_ref):
+    size = k_ref.shape[1] // group
+    start = skip + pl.program_id(0) * group if q_ref.shape[1] > group * size else 0
     _, late = masks()
     depth = WIN // TILE
     tasks = []
@@ -346,19 +347,19 @@
                 (spans(k_ref, j, cols), turned(memo, v_ref, j, cols, 0), late if j == t else None)
                 for j in range(t, depth)
             ]
-            tasks.append((spans(q_ref, t, cols), found, put_partial(o_ref, g, t, size)))
+            lanes = pl.ds(pl.multiple_of((start + g) * size, size), size)
+            tasks.append((spans(q_ref, t, lanes), found, put_partial(o_ref, g, t, size)))
     attend(tasks, s_ref)
 
 
-def next_part(asked, keys, values, first, size):
-    heads = asked.shape[1] // size
+def next_part(asked, keys, values, skip, first, heads, size):
     block = keys.shape[0] // WIN - 1
     group = math.gcd(heads, first)
     column = pl.BlockSpec((WIN, group * size), lambda h: (block, h + first // group))
     return call(
-        functools.partial(next_part_body, group),
+        functools.partial(next_part_body, group, skip),
         (heads // group,),
-        [pl.BlockSpec((WIN, group * size), lambda h: (0, h)), column, column],
+        [VMEM, column, column],
         pl.BlockSpec((group, size + EXTRA, WIN), lambda h: (h, 0, 0)),
         jax.ShapeDtypeStruct((heads, size + EXTRA, WIN), jnp.bfloat16),
         [pltpu.VMEM((2, WIN, TILE), jnp.float32)],
@@ -368,7 +369,7 @@
     )(asked, keys, values)
 
 
-def joined_body(group, z_ref, q_ref, k_ref, v_ref, p_ref, _, o_ref, s_ref):
+def joined_body(group, add, z_ref, q_ref, k_ref, v_ref, p_ref, base_ref, o_ref, s_ref):
     size = q_ref.shape[1] // group
     causal, _ = masks()
     depth = WIN // TILE
@@ -381,7 +382,10 @@
             other = terms[0:1] + (terms[1:2] + terms[2:3])
             share = jnp.where(z_ref[0] > 0, jax.nn.sigmoid(other - level), 0.0)
             out = out + share * (p_ref[step + g, :size, span].astype(jnp.float32) - out)
-            o_ref[span, cols] = jnp.transpose(out).astype(o_ref.dtype)
+            out = jnp.transpose(out)
+            if add:
+                out = out + base_ref[span, cols].astype(jnp.float32)
+            o_ref[span, cols] = out.astype(o_ref.dtype)
 
         return emit
 
@@ -398,12 +402,12 @@
     attend(tasks, s_ref)
 
 
-def joined_block(z, queries, keys, values, given, partly, first, size):
+def joined_block(z, queries, keys, values, given, partly, first, size, add):
     heads = given.shape[0]
     group = math.gcd(heads, first)
     column = pl.BlockSpec((WIN, group * size), lambda h, z: (0, h + first // group))
     return pl.pallas_call(
-        functools.partial(joined_body, group),
+        functools.partial(joined_body, group, add),
         name="joined",
         out_shape=jax.ShapeDtypeStruct(partly.shape, partly.dtype),
         grid_spec=pltpu.PrefetchScalarGridSpec(
@@ -414,7 +418,7 @@
                 column,
                 column,
                 VMEM,
-                pl.BlockSpec(memory_space=pl.ANY),
+                column if add else pl.BlockSpec(memory_space=pl.ANY),
             ],
             out_specs=column,
             scratch_shapes=[pltpu.VMEM((2, WIN, TILE), jnp.float32)],
@@ -427,7 +431,7 @@
     )(z, queries, keys, values, given, partly)
 
 
-def final_body(peers, group, start, z_ref, q_ref, first_ref, later_ref, *refs):
+def final_body(peers, group, start, limit, z_ref, q_ref, first_ref, later_ref, *refs):
     blocks, o_ref, whole = refs[:peers], refs[-2], refs[-1]
     size = q_ref.shape[1] // group
     own = blocks[0].shape[2]
@@ -447,8 +451,10 @@
         gate, up = inner[:, :size], inner[:, size:]
         hidden = (gate * sigmoid(gate) * up).astype(jnp.bfloat16)
         fast = dot(hidden, whole[g, 2].astype(jnp.bfloat16), NT)
-        kept = first_ref[:, cols] if c == 0 else later_ref[c - WIN : c, cols]
-        o_ref[c : c + WIN, cols] = (fast + kept.astype(jnp.float32)).astype(o_ref.dtype)
+        if c or start + g < limit:
+            kept = later_ref[c - WIN : c, cols] if c else first_ref[:, cols]
+            fast = fast + kept.astype(jnp.float32)
+        o_ref[c : c + WIN, cols] = fast.astype(o_ref.dtype)
 
     ready = products(*tasks[0])
     for i, task in enumerate(tasks):
@@ -457,13 +463,13 @@
         ready = following
 
 
-def final(z, queries, first, later, blocks, size, step, group, partly):
+def final(z, queries, first, later, blocks, size, step, group, limit, partly):
     rows, width = queries.shape
     peers, own = len(blocks), blocks[0].shape[2]
     kind = jnp.bfloat16 if own % 16 == 0 else jnp.float32
     more = [] if partly is None else [partly]
     return pl.pallas_call(
-        functools.partial(final_body, peers, group, step * group),
+        functools.partial(final_body, peers, group, step * group, limit),
         name="final",
         out_shape=jax.ShapeDtypeStruct((rows, width), jnp.bfloat16),
         grid_spec=pltpu.PrefetchScalarGridSpec(
@@ -541,11 +547,13 @@
     kept = kept_of(heads)
     z = lax.axis_index("seq").astype(jnp.int32).reshape(1)
     early = max(1, heads * EARLY // 10)
-    groups = [(kept, early), (kept + early, heads - kept - early)]
+    late = kept + early
+    lead = (early + 1) // 2
+    groups = [(kept, lead, 0, 0), (kept + lead, early - lead, 0, lead), (late, heads - late, 1, 0)]
 
     asked, carried = packed(queries, keys, values, kept * size, (kept * size, early * size))
     asked = [moved_by(asked, -1)]
-    asked.append(moved_by(queries[:WIN, (kept + early) * size :], -1))
+    asked.append(moved_by(queries[:WIN, late * size :], -1))
     carried = moved_by(carried, 1)
 
     weights = jnp.transpose(fast_weights, (1, 2, 0, 3))
@@ -567,12 +575,12 @@
     for part in range(heads // group):
         later = later_blocks(queries, keys, values, size, part, group, later)
     given = []
-    for i, (place, _) in enumerate(groups):
-        part = next_part(asked[i], keys, values, place, size)
+    for place, count, source, skip in groups:
+        part = next_part(asked[source], keys, values, skip, place, count, size)
         given.append(moved_by(part, 1))
     first = carried_block(z, queries, keys, values, carried, size)
-    for i, (place, _) in enumerate(groups):
-        first = joined_block(z, queries, keys, values, given[i], first, place, size)
+    for i, (place, _, _, _) in enumerate(groups[:-1]):
+        first = joined_block(z, queries, keys, values, given[i], first, place, size, False)
 
     new_rows, new_momentum = updated(z, weights, own_momentum, sums[0])
     blocks = {0: new_rows}
@@ -587,7 +595,9 @@
     for part in range(heads // group):
         last = swapped(blocks[peers - 2][part * group : (part + 1) * group], 1)
         parts = [blocks[m] for m in range(peers - 1)] + [last]
-        mixed = final(z, queries, first, later, parts, size, part, group, mixed)
+        mixed = final(z, queries, first, later, parts, size, part, group, groups[-1][0], mixed)
+    place = groups[-1][0]
+    mixed = joined_block(z, queries, keys, values, given[-1], mixed, place, size, True)
     return (mixed, jnp.transpose(new_rows, (2, 0, 1, 3)), jnp.transpose(new_momentum, (2, 0, 1, 3)))
 
 

time: 89.2 us -> 95.1 us (1.066); the launches traced: 88.9 us -> 93.5 us
  waiting for transfers between devices: 20.1 us -> 25.1 us
  Pallas kernels: 36.9 us -> 34.6 us
  starting transfers between devices: 29.8 us -> 31.8 us
    ppermute x5 -> x6, starting transfers between devices: 10.3 us -> 17.2 us  [moved_by(): return lax.ppermute(value, 'seq', pairs)]
    ppermute x7, starting transfers between devices: 19.5 us -> 14.7 us  [swapped(): lax.ppermute(value, 'seq', [(i, i ^ mask) for i in range(lax.axis_size('s...]
    ppermute x5 -> x6, waiting for transfers between devices: 0.01 us -> 4.4 us  [moved_by(): return lax.ppermute(value, 'seq', pairs)]
    pallas_call x2, Pallas kernels: 9.88 us -> 7.88 us  [later_blocks(): pl.pallas_call(functools.partial(later_body, group), name='later', out_sh...]
    pallas_call x6 -> x8, Pallas kernels: 14.3 us -> 13.9 us  [the longest x2 5.41 us: final(): pl.pallas_call(functools.partial(final_body, peers, group, step * group,...]
  transfers between devices with their start and end apart: 12 -> 13, of which waited for: 5 -> 4; matrix products, arithmetic and copies ran while one was open for 1% -> 1% of each run, Pallas kernels for 37% -> 25%
where the time goes in v7:
time: 95.1 us; the launch traced here: 93.5 us
  Pallas kernels  34.6 us (36%)
  starting transfers between devices  31.8 us (33%)
  waiting for transfers between devices  25.1 us (26%)
  local copies, waits for them, and re-layouts  1.03 us (1%)
    ppermute x7, waiting for transfers between devices, swapped(): lax.ppermute(value, 'seq', [(i, i ^ mask) for i in range(lax.axis_size('s...  20.7 us
    ppermute x6, starting transfers between devices, moved_by(): return lax.ppermute(value, 'seq', pairs)  17.2 us
    ppermute x7, starting transfers between devices, swapped(): lax.ppermute(value, 'seq', [(i, i ^ mask) for i in range(lax.axis_size('s...  14.7 us
    pallas_call x1, Pallas kernels, partial_grads(): call(functools.partial(grad_body, peers, group, min(rows, 256)), (heads /...  8.15 us
    pallas_call x2, Pallas kernels, later_blocks(): pl.pallas_call(functools.partial(later_body, group), name='later', out_sh...  7.88 us
    pallas_call x2, Pallas kernels, final(): pl.pallas_call(functools.partial(final_body, peers, group, step * group,...  5.41 us
    pallas_call x3, Pallas kernels, joined_block(): pl.pallas_call(functools.partial(joined_body, group, add), name='joined',...  5.25 us
    ppermute x6, waiting for transfers between devices, moved_by(): return lax.ppermute(value, 'seq', pairs)  4.4 us
  transfers between devices with their start and end apart: 13, of which 4 were waited for; matrix products, arithmetic and copies ran while one was open for 1% of the time, Pallas kernels for 25%

profile of v7, /device:TPU:0, one launch (start us, length us, event | category | flops | bytes accessed | tf_op | source)
XLA Modules:
  0.0 93.5 jit_solution(11861535981202138188)
XLA Ops:
  0.6 8.2 %shard_map.90 = (f32[10,3,32,128]{3,2,1,0:T(8,128)S(1)}, bf16[10,3,32,128]{3,2,1,0:T(8,128)(2,1)S(1)}, f32[10,3,32,128]{3,2,1,0:T(8,128)S(1)}, bf16[10,3,32,128]{3,2,1,0:T(8,128)(2,1)S(1)}) custom-call(s32[1]{0:T(128)} %bitcast.z_ref, bf16[1024,1280]{1,0:T(8,128)(2,1)} %k_ref.21, bf16[1024,1280]{1,0:T(8,128)(2,1)} %v_ref.21, f32[10,1024]{1,0:T(8,128)} %r_ref.1, ...), custom_call_target="tpu_custom_call" | custom-call | flops 2013265920 | bytes 5242880 | tf_op jit(solution)/shard_map/pallas_call | solution.py:114
  8.8 3.1 %collective-permute-start.7 = (bf16[10,3,32,128]{3,2,1,0:T(8,128)(2,1)S(1)}, bf16[10,3,32,128]{3,2,1,0:T(8,128)(2,1)S(1)}, u32[]{:S(2)}, u32[]{:S(2)}) collective-permute-start(bf16[10,3,32,128]{3,2,1,0:T(8,128)(2,1)S(1)} %get-tuple-element.16), channel_id=1, source_target_pairs={{0,4},{4,0},{8,12},{12,8},{1,5},{5,1},{9,13},{13,9},{2,6},{6,2},{1... | collective-permute-start | bytes 737288 | tf_op jit(solution)/shard_map/ppermute | solution.py:536
  11.9 1.5 %shard_map.86 = (bf16[512,640]{1,0:T(8,128)(2,1)S(1)}, bf16[2,512,384]{2,1,0:T(8,128)(2,1)S(1)}) custom-call(bf16[1024,1280]{1,0:T(8,128)(2,1)} %q_ref.17, bf16[1024,1280]{1,0:T(8,128)(2,1)} %k_ref.21, bf16[1024,1280]{1,0:T(8,128)(2,1)} %v_ref.21), custom_call_target="tpu_custom_call" | custom-call | bytes 2883584 | tf_op jit(solution)/shard_map/pallas_call | solution.py:516
  13.5 1.4 %collective-permute-start.2 = (bf16[512,640]{1,0:T(8,128)(2,1)S(1)}, bf16[512,640]{1,0:T(8,128)(2,1)S(1)}, u32[]{:S(2)}, u32[]{:S(2)}) collective-permute-start(bf16[512,640]{1,0:T(8,128)(2,1)S(1)} %get-tuple-element.11), channel_id=1, source_target_pairs={{4,0},{8,4},{12,8},{5,1},{9,5},{13,9},{6,2},{10,6},{14,10},{7,3},{... | collective-permute-start | bytes 1966088 | tf_op jit(solution)/shard_map/ppermute | solution.py:532
  14.9 2.7 %collective-permute-start.6 = (bf16[10,3,32,128]{3,2,1,0:T(8,128)(2,1)S(1)}, bf16[10,3,32,128]{3,2,1,0:T(8,128)(2,1)S(1)}, u32[]{:S(2)}, u32[]{:S(2)}) collective-permute-start(bf16[10,3,32,128]{3,2,1,0:T(8,128)(2,1)S(1)} %get-tuple-element.14), channel_id=1, source_target_pairs={{0,4},{4,0},{8,12},{12,8},{1,5},{5,1},{9,13},{13,9},{2,6},{6,2},{1... | collective-permute-start | bytes 737288 | tf_op jit(solution)/shard_map/ppermute | solution.py:536
  17.6 2.0 %collective-permute-start.5 = (bf16[2,512,384]{2,1,0:T(8,128)(2,1)S(1)}, bf16[2,512,384]{2,1,0:T(8,128)(2,1)S(1)}, u32[]{:S(2)}, u32[]{:S(2)}) collective-permute-start(bf16[2,512,384]{2,1,0:T(8,128)(2,1)S(1)} %get-tuple-element.12), channel_id=1, source_target_pairs={{0,4},{4,8},{8,12},{1,5},{5,9},{9,13},{2,6},{6,10},{10,14},{3,7},{... | collective-permute-start | bytes 2359304 | tf_op jit(solution)/shard_map/ppermute | solution.py:532
  19.7 2.7 %collective-permute-start.8 = (bf16[10,3,32,128]{3,2,1,0:T(8,128)(2,1)S(1)}, bf16[10,3,32,128]{3,2,1,0:T(8,128)(2,1)S(1)}, u32[]{:S(2)}, u32[]{:S(2)}) collective-permute-start(bf16[10,3,32,128]{3,2,1,0:T(8,128)(2,1)S(1)} %add_convert_fusion), channel_id=1, source_target_pairs={{0,8},{4,12},{8,0},{12,4},{1,9},{5,13},{9,1},{13,5},{2,10},{6,14},... | collective-permute-start | bytes 737288 | tf_op jit(solution)/shard_map/ppermute | solution.py:536
  22.3 1.0 %slice.9 = bf16[512,256]{1,0:T(8,128)(2,1)S(1)} slice(bf16[1024,1280]{1,0:T(8,128)(2,1)} %q_ref.17), slice={[0:512], [1024:1280]} | slice | bytes 524288 | tf_op jit(solution)/shard_map/slice | solution.py:556
  23.3 1.3 %collective-permute-start = (bf16[512,256]{1,0:T(8,128)(2,1)S(1)}, bf16[512,256]{1,0:T(8,128)(2,1)S(1)}, u32[]{:S(2)}, u32[]{:S(2)}) collective-permute-start(bf16[512,256]{1,0:T(8,128)(2,1)S(1)} %slice.9), channel_id=1, source_target_pairs={{4,0},{8,4},{12,8},{5,1},{9,5},{13,9},{6,2},{10,6},{14,10},{7,3},{... | collective-permute-start | bytes 786440 | tf_op jit(solution)/shard_map/ppermute | solution.py:532
  24.6 19.0 %collective-permute-done.6.refs_1_ = bf16[10,3,32,128]{3,2,1,0:T(8,128)(2,1)S(1)} collective-permute-done((bf16[10,3,32,128]{3,2,1,0:T(8,128)(2,1)S(1)}, bf16[10,3,32,128]{3,2,1,0:T(8,128)(2,1)S(1)}, u32[]{:S(2)}, u32[]{:S(2)}) %collective-permute-start.6) | collective-permute-done | bytes 245792 | tf_op jit(solution)/shard_map/ppermute | solution.py:536
  43.6 1.0 %collective-permute-done.8.refs_2_ = bf16[10,3,32,128]{3,2,1,0:T(8,128)(2,1)S(1)} collective-permute-done((bf16[10,3,32,128]{3,2,1,0:T(8,128)(2,1)S(1)}, bf16[10,3,32,128]{3,2,1,0:T(8,128)(2,1)S(1)}, u32[]{:S(2)}, u32[]{:S(2)}) %collective-permute-start.8) | collective-permute-done | bytes 245792 | tf_op jit(solution)/shard_map/ppermute | solution.py:536
  44.6 1.2 %shard_map.91 = (bf16[10,3,32,128]{3,2,1,0:T(8,128)(2,1)}, f32[10,3,32,128]{3,2,1,0:T(8,128)}) custom-call(s32[1]{0:T(128)} %bitcast.z_ref, bf16[10,3,128,128]{3,2,1,0:T(8,128)(2,1)S(1)} %bitcast.6, f32[10,3,32,128]{3,2,1,0:T(8,128)S(1)} %bitcast.8, f32[10,3,32,128]{3,2,1,0:T(8,128)S(1)} %get-tuple-element.13.refs_0_, ...), custom_call_target="tpu_custom_call" | custom-call | flops 2457600 | bytes 1966080 | tf_op jit(solution)/shard_map/pallas_call | solution.py:152
  45.8 3.4 %collective-permute-start.10 = (bf16[10,3,32,128]{3,2,1,0:T(8,128)(2,1)}, bf16[10,3,32,128]{3,2,1,0:T(8,128)(2,1)S(1)}, u32[]{:S(2)}, u32[]{:S(2)}) collective-permute-start(bf16[10,3,32,128]{3,2,1,0:T(8,128)(2,1)} %get-tuple-element.17.refs_0_), channel_id=1, source_target_pairs={{0,8},{4,12},{8,0},{12,4},{1,9},{5,13},{9,1},{13,5},{2,10},{6,14},... | collective-permute-start | bytes 737288 | tf_op jit(solution)/shard_map/ppermute | solution.py:536
  49.2 1.4 %shard_map.88 = bf16[3,136,512]{2,1,0:T(8,128)(2,1)S(1)} custom-call(bf16[512,640]{1,0:T(8,128)(2,1)S(1)} %collective-permute-done.2.q_ref, bf16[1024,1280]{1,0:T(8,128)(2,1)S(1)} %copy-done, bf16[1024,1280]{1,0:T(8,128)(2,1)S(1)} %copy-done.2), custom_call_target="tpu_custom_call" | custom-call | flops 402653184 | bytes 1572864 | tf_op jit(solution)/shard_map/pallas_call | solution.py:359
  50.6 6.7 %collective-permute-start.4 = (bf16[3,136,512]{2,1,0:T(8,128)(2,1)S(1)}, bf16[3,136,512]{2,1,0:T(8,128)(2,1)S(1)}, u32[]{:S(2)}, u32[]{:S(2)}) collective-permute-start(bf16[3,136,512]{2,1,0:T(8,128)(2,1)S(1)} %shard_map.88), channel_id=1, source_target_pairs={{0,4},{4,8},{8,12},{1,5},{5,9},{9,13},{2,6},{6,10},{10,14},{3,7},{... | collective-permute-start | bytes 1253384 | tf_op jit(solution)/shard_map/ppermute | solution.py:532
  57.4 4.9 %later.2.refs_0_ = bf16[512,1280]{1,0:T(8,128)(2,1)S(1)} custom-call(bf16[1024,1280]{1,0:T(8,128)(2,1)} %q_ref.17, bf16[1024,1280]{1,0:T(8,128)(2,1)} %k_ref.21, bf16[1024,1280]{1,0:T(8,128)(2,1)} %v_ref.21), custom_call_target="tpu_custom_call" | custom-call | flops 1006632960 | bytes 5242880 | tf_op jit(solution)/shard_map/later/pallas_call | solution.py:255
  62.3 0.9 %shard_map.85 = bf16[2,136,512]{2,1,0:T(8,128)(2,1)S(1)} custom-call(bf16[512,256]{1,0:T(8,128)(2,1)S(1)} %collective-permute-done.q_ref, bf16[1024,1280]{1,0:T(8,128)(2,1)S(1)} %copy-done.1, bf16[1024,1280]{1,0:T(8,128)(2,1)S(1)} %copy-done.3), custom_call_target="tpu_custom_call" | custom-call | flops 268435456 | bytes 1048576 | tf_op jit(solution)/shard_map/pallas_call | solution.py:359
  63.2 2.2 %collective-permute-start.1 = (bf16[2,136,512]{2,1,0:T(8,128)(2,1)S(1)}, bf16[2,136,512]{2,1,0:T(8,128)(2,1)S(1)}, u32[]{:S(2)}, u32[]{:S(2)}) collective-permute-start(bf16[2,136,512]{2,1,0:T(8,128)(2,1)S(1)} %shard_map.85), channel_id=1, source_target_pairs={{0,4},{4,8},{8,12},{1,5},{5,9},{9,13},{2,6},{6,10},{10,14},{3,7},{... | collective-permute-start | bytes 835592 | tf_op jit(solution)/shard_map/ppermute | solution.py:532
  65.4 0.6 collective-permute-start.9
  66.0 0.9 %shard_map.87 = bf16[2,136,512]{2,1,0:T(8,128)(2,1)S(1)} custom-call(bf16[512,640]{1,0:T(8,128)(2,1)S(1)} %collective-permute-done.2.q_ref, bf16[1024,1280]{1,0:T(8,128)(2,1)S(1)} %copy-done.1, bf16[1024,1280]{1,0:T(8,128)(2,1)S(1)} %copy-done.3), custom_call_target="tpu_custom_call" | custom-call | flops 268435456 | bytes 1048576 | tf_op jit(solution)/shard_map/pallas_call | solution.py:359
  67.0 3.6 %collective-permute-start.3 = (bf16[2,136,512]{2,1,0:T(8,128)(2,1)S(1)}, bf16[2,136,512]{2,1,0:T(8,128)(2,1)S(1)}, u32[]{:S(2)}, u32[]{:S(2)}) collective-permute-start(bf16[2,136,512]{2,1,0:T(8,128)(2,1)S(1)} %shard_map.87), channel_id=1, source_target_pairs={{0,4},{4,8},{8,12},{1,5},{5,9},{9,13},{2,6},{6,10},{10,14},{3,7},{... | collective-permute-start | bytes 835592 | tf_op jit(solution)/shard_map/ppermute | solution.py:532
  70.6 0.1 collective-permute-start.12
  70.7 3.0 %later.3.later_ref = bf16[512,1280]{1,0:T(8,128)(2,1)S(1)} custom-call(bf16[1024,1280]{1,0:T(8,128)(2,1)S(1)} %copy-done.4, bf16[1024,1280]{1,0:T(8,128)(2,1)S(1)} %copy-done.1, bf16[1024,1280]{1,0:T(8,128)(2,1)S(1)} %copy-done.3, bf16[512,1280]{1,0:T(8,128)(2,1)S(1)} %later.2.refs_0_), custom_call_target="tpu_custom_call", output_to_operand_aliasing={{}: (3, {})} | custom-call | flops 1006632960 | bytes 5242880 | tf_op jit(solution)/shard_map/later/pallas_call | solution.py:255
  73.7 2.1 %collective-permute-start.11 = (bf16[5,3,32,128]{3,2,1,0:T(8,128)(2,1)S(1)}, bf16[5,3,32,128]{3,2,1,0:T(8,128)(2,1)S(1)}, u32[]{:S(2)}, u32[]{:S(2)}) collective-permute-start(bf16[5,3,32,128]{3,2,1,0:T(8,128)(2,1)S(1)} %get-tuple-element.20), channel_id=1, source_target_pairs={{0,4},{4,0},{8,12},{12,8},{1,5},{5,1},{9,13},{13,9},{2,6},{6,2},{1... | collective-permute-start | bytes 368648 | tf_op jit(solution)/shard_map/ppermute | solution.py:536
  75.8 1.9 %shard_map.89.base_ref = bf16[512,1280]{1,0:T(8,128)(2,1)S(1)} custom-call(s32[1]{0:T(128)} %bitcast.z_ref, bf16[1024,1280]{1,0:T(8,128)(2,1)S(1)} %copy-done.4, bf16[1024,1280]{1,0:T(8,128)(2,1)S(1)} %copy-done.1, bf16[1024,1280]{1,0:T(8,128)(2,1)S(1)} %copy-done.3, bf16[2,512,384]{2,1,0:T(8,128)(2,1)S(1)} %collective-permute-done.5.p_ref), custom_call_target="tpu_custom_call" | custom-call | flops 603979776 | bytes 1966080 | tf_op jit(solution)/shard_map/pallas_call | solution.py:303
  77.8 1.5 %joined.3.base_ref = bf16[512,1280]{1,0:T(8,128)(2,1)S(1)} custom-call(s32[1]{0:T(128)} %bitcast.z_ref, bf16[1024,1280]{1,0:T(8,128)(2,1)S(1)} %copy-done.4, bf16[1024,1280]{1,0:T(8,128)(2,1)S(1)} %copy-done.1, bf16[1024,1280]{1,0:T(8,128)(2,1)S(1)} %copy-done.3, ...), custom_call_target="tpu_custom_call", output_to_operand_aliasing={{}: (5, {})} | custom-call | flops 402653184 | bytes 1966080 | tf_op jit(solution)/shard_map/joined/pallas_call | solution.py:409
  79.3 4.4 %collective-permute-done.3.p_ref = bf16[2,136,512]{2,1,0:T(8,128)(2,1)S(1)} collective-permute-done((bf16[2,136,512]{2,1,0:T(8,128)(2,1)S(1)}, bf16[2,136,512]{2,1,0:T(8,128)(2,1)S(1)}, u32[]{:S(2)}, u32[]{:S(2)}) %collective-permute-start.3) | collective-permute-done | bytes 278560 | tf_op jit(solution)/shard_map/ppermute | solution.py:532
  83.7 1.0 %joined.4.first_ref = bf16[512,1280]{1,0:T(8,128)(2,1)S(1)} custom-call(s32[1]{0:T(128)} %bitcast.z_ref, bf16[1024,1280]{1,0:T(8,128)(2,1)S(1)} %copy-done.4, bf16[1024,1280]{1,0:T(8,128)(2,1)S(1)} %copy-done.1, bf16[1024,1280]{1,0:T(8,128)(2,1)S(1)} %copy-done.3, ...), custom_call_target="tpu_custom_call", output_to_operand_aliasing={{}: (5, {})} | custom-call | flops 268435456 | bytes 1310720 | tf_op jit(solution)/shard_map/joined/pallas_call | solution.py:409
  84.7 0.7 collective-permute-done.12.refs_3_
  85.4 2.7 %final.2.refs_4_ = bf16[1024,1280]{1,0:T(8,128)(2,1)} custom-call(s32[1]{0:T(128)} %bitcast.z_ref, bf16[1024,1280]{1,0:T(8,128)(2,1)S(1)} %copy-done.4, bf16[512,1280]{1,0:T(8,128)(2,1)S(1)} %joined.4.first_ref, bf16[512,1280]{1,0:T(8,128)(2,1)S(1)} %later.3.later_ref, bf16[10,3,32,128]{3,2,1,0:T(8,128)(2,1)S(1)} %copy-done.6, ...), custom_call_target="tpu_custom_call" | custom-call | flops 503316480 | bytes 3932160 | tf_op jit(solution)/shard_map/final/pallas_call | solution.py:471
  88.1 2.7 %final.3.base_ref = bf16[1024,1280]{1,0:T(8,128)(2,1)} custom-call(s32[1]{0:T(128)} %bitcast.z_ref, bf16[1024,1280]{1,0:T(8,128)(2,1)S(1)} %copy-done.4, bf16[512,1280]{1,0:T(8,128)(2,1)S(1)} %joined.4.first_ref, bf16[512,1280]{1,0:T(8,128)(2,1)S(1)} %later.3.later_ref, bf16[10,3,32,128]{3,2,1,0:T(8,128)(2,1)S(1)} %copy-done.6, ...), custom_call_target="tpu_custom_call", output_to_operand_aliasing={{}: (8, {})} | custom-call | flops 503316480 | bytes 3932160 | tf_op jit(solution)/shard_map/final/pallas_call | solution.py:471
  90.8 2.7 %joined.5 = bf16[1024,1280]{1,0:T(8,128)(2,1)} custom-call(s32[1]{0:T(128)} %bitcast.z_ref, bf16[1024,1280]{1,0:T(8,128)(2,1)S(1)} %copy-done.4, bf16[1024,1280]{1,0:T(8,128)(2,1)S(1)} %copy-done.1, bf16[1024,1280]{1,0:T(8,128)(2,1)S(1)} %copy-done.3, bf16[2,136,512]{2,1,0:T(8,128)(2,1)S(1)} %collective-permute-done.1.p_ref, ...), custom_call_target="tpu_custom_call", output_to_operand_aliasing={{}: (5, {})} | custom-call | flops 268435456 | bytes 1310720 | tf_op jit(solution)/shard_map/joined/pallas_call | solution.py:409
  (27 shorter events, 0.2 us)
Async XLA Ops:
  8.8 35.8 %copy-start.5 = (bf16[128,10,3,128]{3,0,2,1:T(8,128)(2,1)S(1)}, bf16[128,10,3,128]{3,0,2,1:T(8,128)(2,1)}, u32[]{:S(2)}) copy-start(bf16[128,10,3,128]{3,0,2,1:T(8,128)(2,1)} %param.10) | copy-start | bytes 2949124
  8.8 35.8 %copy-start.7 = (f32[32,10,3,128]{3,0,2,1:T(8,128)S(1)}, f32[32,10,3,128]{3,0,2,1:T(8,128)}, u32[]{:S(2)}) copy-start(f32[32,10,3,128]{3,0,2,1:T(8,128)} %param.11) | copy-start | bytes 1474564
  8.8 10.8 %collective-permute-start.7 = (bf16[10,3,32,128]{3,2,1,0:T(8,128)(2,1)S(1)}, bf16[10,3,32,128]{3,2,1,0:T(8,128)(2,1)S(1)}, u32[]{:S(2)}, u32[]{:S(2)}) collective-permute-start(bf16[10,3,32,128]{3,2,1,0:T(8,128)(2,1)S(1)} %get-tuple-element.16), channel_id=1, source_target_pairs={{0,4},{4,0},{8,12},{12,8},{1,5},{5,1},{9,13},{13,9},{2,6},{6,2},{1... | collective-permute-start | bytes 737288 | tf_op jit(solution)/shard_map/ppermute | solution.py:536
  11.9 37.3 %copy-start.2 = (bf16[1024,1280]{1,0:T(8,128)(2,1)S(1)}, bf16[1024,1280]{1,0:T(8,128)(2,1)}, u32[]{:S(2)}) copy-start(bf16[1024,1280]{1,0:T(8,128)(2,1)} %v_ref.21) | copy-start | bytes 7864324
  13.5 35.7 %copy-start = (bf16[1024,1280]{1,0:T(8,128)(2,1)S(1)}, bf16[1024,1280]{1,0:T(8,128)(2,1)}, u32[]{:S(2)}) copy-start(bf16[1024,1280]{1,0:T(8,128)(2,1)} %k_ref.21) | copy-start | bytes 7864324
  13.5 35.7 %collective-permute-start.2 = (bf16[512,640]{1,0:T(8,128)(2,1)S(1)}, bf16[512,640]{1,0:T(8,128)(2,1)S(1)}, u32[]{:S(2)}, u32[]{:S(2)}) collective-permute-start(bf16[512,640]{1,0:T(8,128)(2,1)S(1)} %get-tuple-element.11), channel_id=1, source_target_pairs={{4,0},{8,4},{12,8},{5,1},{9,5},{13,9},{6,2},{10,6},{14,10},{7,3},{... | collective-permute-start | bytes 1966088 | tf_op jit(solution)/shard_map/ppermute | solution.py:532
  14.9 28.7 %collective-permute-start.6 = (bf16[10,3,32,128]{3,2,1,0:T(8,128)(2,1)S(1)}, bf16[10,3,32,128]{3,2,1,0:T(8,128)(2,1)S(1)}, u32[]{:S(2)}, u32[]{:S(2)}) collective-permute-start(bf16[10,3,32,128]{3,2,1,0:T(8,128)(2,1)S(1)} %get-tuple-element.14), channel_id=1, source_target_pairs={{0,4},{4,0},{8,12},{12,8},{1,5},{5,1},{9,13},{13,9},{2,6},{6,2},{1... | collective-permute-start | bytes 737288 | tf_op jit(solution)/shard_map/ppermute | solution.py:536
  17.6 53.0 %collective-permute-start.5 = (bf16[2,512,384]{2,1,0:T(8,128)(2,1)S(1)}, bf16[2,512,384]{2,1,0:T(8,128)(2,1)S(1)}, u32[]{:S(2)}, u32[]{:S(2)}) collective-permute-start(bf16[2,512,384]{2,1,0:T(8,128)(2,1)S(1)} %get-tuple-element.12), channel_id=1, source_target_pairs={{0,4},{4,8},{8,12},{1,5},{5,9},{9,13},{2,6},{6,10},{10,14},{3,7},{... | collective-permute-start | bytes 2359304 | tf_op jit(solution)/shard_map/ppermute | solution.py:532
  19.7 24.9 %collective-permute-start.8 = (bf16[10,3,32,128]{3,2,1,0:T(8,128)(2,1)S(1)}, bf16[10,3,32,128]{3,2,1,0:T(8,128)(2,1)S(1)}, u32[]{:S(2)}, u32[]{:S(2)}) collective-permute-start(bf16[10,3,32,128]{3,2,1,0:T(8,128)(2,1)S(1)} %add_convert_fusion), channel_id=1, source_target_pairs={{0,8},{4,12},{8,0},{12,4},{1,9},{5,13},{9,1},{13,5},{2,10},{6,14},... | collective-permute-start | bytes 737288 | tf_op jit(solution)/shard_map/ppermute | solution.py:536
  23.3 39.0 %collective-permute-start = (bf16[512,256]{1,0:T(8,128)(2,1)S(1)}, bf16[512,256]{1,0:T(8,128)(2,1)S(1)}, u32[]{:S(2)}, u32[]{:S(2)}) collective-permute-start(bf16[512,256]{1,0:T(8,128)(2,1)S(1)} %slice.9), channel_id=1, source_target_pairs={{4,0},{8,4},{12,8},{5,1},{9,5},{13,9},{6,2},{10,6},{14,10},{7,3},{... | collective-permute-start | bytes 786440 | tf_op jit(solution)/shard_map/ppermute | solution.py:532
  45.8 21.2 %collective-permute-start.10 = (bf16[10,3,32,128]{3,2,1,0:T(8,128)(2,1)}, bf16[10,3,32,128]{3,2,1,0:T(8,128)(2,1)S(1)}, u32[]{:S(2)}, u32[]{:S(2)}) collective-permute-start(bf16[10,3,32,128]{3,2,1,0:T(8,128)(2,1)} %get-tuple-element.17.refs_0_), channel_id=1, source_target_pairs={{0,8},{4,12},{8,0},{12,4},{1,9},{5,13},{9,1},{13,5},{2,10},{6,14},... | collective-permute-start | bytes 737288 | tf_op jit(solution)/shard_map/ppermute | solution.py:536
  50.6 11.7 %copy-start.1 = (bf16[1024,1280]{1,0:T(8,128)(2,1)S(1)}, bf16[1024,1280]{1,0:T(8,128)(2,1)}, u32[]{:S(2)}) copy-start(bf16[1024,1280]{1,0:T(8,128)(2,1)} %k_ref.21) | copy-start | bytes 7864324
  50.6 11.7 %copy-start.3 = (bf16[1024,1280]{1,0:T(8,128)(2,1)S(1)}, bf16[1024,1280]{1,0:T(8,128)(2,1)}, u32[]{:S(2)}) copy-start(bf16[1024,1280]{1,0:T(8,128)(2,1)} %v_ref.21) | copy-start | bytes 7864324
  50.6 23.1 %collective-permute-start.4 = (bf16[3,136,512]{2,1,0:T(8,128)(2,1)S(1)}, bf16[3,136,512]{2,1,0:T(8,128)(2,1)S(1)}, u32[]{:S(2)}, u32[]{:S(2)}) collective-permute-start(bf16[3,136,512]{2,1,0:T(8,128)(2,1)S(1)} %shard_map.88), channel_id=1, source_target_pairs={{0,4},{4,8},{8,12},{1,5},{5,9},{9,13},{2,6},{6,10},{10,14},{3,7},{... | collective-permute-start | bytes 1253384 | tf_op jit(solution)/shard_map/ppermute | solution.py:532
  62.2 3.2 %copy-start.6 = (bf16[10,3,32,128]{3,2,1,0:T(8,128)(2,1)S(1)}, bf16[10,3,32,128]{3,2,1,0:T(8,128)(2,1)}, u32[]{:S(2)}) copy-start(bf16[10,3,32,128]{3,2,1,0:T(8,128)(2,1)} %get-tuple-element.17.refs_0_) | copy-start | bytes 737284
  63.2 7.5 %copy-start.4 = (bf16[1024,1280]{1,0:T(8,128)(2,1)S(1)}, bf16[1024,1280]{1,0:T(8,128)(2,1)}, u32[]{:S(2)}) copy-start(bf16[1024,1280]{1,0:T(8,128)(2,1)} %q_ref.17) | copy-start | bytes 7864324
  63.2 27.6 %collective-permute-start.1 = (bf16[2,136,512]{2,1,0:T(8,128)(2,1)S(1)}, bf16[2,136,512]{2,1,0:T(8,128)(2,1)S(1)}, u32[]{:S(2)}, u32[]{:S(2)}) collective-permute-start(bf16[2,136,512]{2,1,0:T(8,128)(2,1)S(1)} %shard_map.85), channel_id=1, source_target_pairs={{0,4},{4,8},{8,12},{1,5},{5,9},{9,13},{2,6},{6,10},{10,14},{3,7},{... | collective-permute-start | bytes 835592 | tf_op jit(solution)/shard_map/ppermute | solution.py:532
  65.4 19.3 %collective-permute-start.9 = (bf16[10,3,32,128]{3,2,1,0:T(8,128)(2,1)S(1)}, bf16[10,3,32,128]{3,2,1,0:T(8,128)(2,1)S(1)}, u32[]{:S(2)}, u32[]{:S(2)}) collective-permute-start(bf16[10,3,32,128]{3,2,1,0:T(8,128)(2,1)S(1)} %copy-done.6), channel_id=1, source_target_pairs={{0,4},{4,0},{8,12},{12,8},{1,5},{5,1},{9,13},{13,9},{2,6},{6,2},{1... | collective-permute-start | bytes 737288 | tf_op jit(solution)/shard_map/ppermute | solution.py:536
  67.0 16.7 %collective-permute-start.3 = (bf16[2,136,512]{2,1,0:T(8,128)(2,1)S(1)}, bf16[2,136,512]{2,1,0:T(8,128)(2,1)S(1)}, u32[]{:S(2)}, u32[]{:S(2)}) collective-permute-start(bf16[2,136,512]{2,1,0:T(8,128)(2,1)S(1)} %shard_map.87), channel_id=1, source_target_pairs={{0,4},{4,8},{8,12},{1,5},{5,9},{9,13},{2,6},{6,10},{10,14},{3,7},{... | collective-permute-start | bytes 835592 | tf_op jit(solution)/shard_map/ppermute | solution.py:532
  70.6 14.8 %collective-permute-start.12 = (bf16[5,3,32,128]{3,2,1,0:T(8,128)(2,1)S(1)}, bf16[5,3,32,128]{3,2,1,0:T(8,128)(2,1)S(1)}, u32[]{:S(2)}, u32[]{:S(2)}) collective-permute-start(bf16[5,3,32,128]{3,2,1,0:T(8,128)(2,1)S(1)} %get-tuple-element.19), channel_id=1, source_target_pairs={{0,4},{4,0},{8,12},{12,8},{1,5},{5,1},{9,13},{13,9},{2,6},{6,2},{1... | collective-permute-start | bytes 368648 | tf_op jit(solution)/shard_map/ppermute | solution.py:536
  73.7 14.4 %collective-permute-start.11 = (bf16[5,3,32,128]{3,2,1,0:T(8,128)(2,1)S(1)}, bf16[5,3,32,128]{3,2,1,0:T(8,128)(2,1)S(1)}, u32[]{:S(2)}, u32[]{:S(2)}) collective-permute-start(bf16[5,3,32,128]{3,2,1,0:T(8,128)(2,1)S(1)} %get-tuple-element.20), channel_id=1, source_target_pairs={{0,4},{4,0},{8,12},{12,8},{1,5},{5,1},{9,13},{13,9},{2,6},{6,2},{1... | collective-permute-start | bytes 368648 | tf_op jit(solution)/shard_map/ppermute | solution.py:536
